TPU v7x, 32 devices: a whole 2x2x4 slice. The times are simulated.
32 devices in a mesh: rows: 8 (over z, x), feat: 4 (over y, core).
Axes of the slice: x: 2, y: 2, z: 4, core: 2. Of those that a mesh axis runs over, the one named last changes fastest.
Arguments:
- pixels: bfloat16 [12288, 1024], P(('rows', 'feat')), may hold values from -6 to 6
- qkv_weight: bfloat16 [3, 1024, 1024], P(None, None, 'feat'), may hold values from -0.1875 to 0.1875
- out_weight: bfloat16 [1024, 1024], P('feat'), may hold values from -1.5 to 1.5
- up_weight: bfloat16 [1024, 4096], P(None, 'feat'), as said below
- down_weight: bfloat16 [4096, 1024], P('feat'), may hold values from -0.09375 to 0.09375
- norm1_gain: float32 [1024], replicated, may hold values from 0.5 to 1.5
- norm1_bias: float32 [1024], replicated, may hold values from -3 to 3
- norm2_gain: float32 [1024], replicated, may hold values from 0.5 to 1.5
- norm2_bias: float32 [1024], replicated, may hold values from -3 to 3
- crop_lengths: int32 [32], replicated, may hold values from 0 to 3072, as said below
- crop_offsets: int32 [32], replicated, may hold values from 0 to 12288, as said below
- pixel_mask: int32 [12288], P('rows'), may hold values 0 or 1
- out_grad: bfloat16 [12288, 1024], P(('rows', 'feat')), may hold values from -6 to 6
Outputs:
- output: bfloat16 [12288, 1024], P(('rows', 'feat'))
- pixels_grad: bfloat16 [12288, 1024], P(('rows', 'feat'))
- qkv_weight_grad: float32 [3, 1024, 1024], P(None, None, 'feat')
- out_weight_grad: float32 [1024, 1024], P('feat')
- up_weight_grad: float32 [1024, 4096], P(None, 'feat')
- down_weight_grad: float32 [4096, 1024], P('feat')
- norm1_gain_grad: float32 [1024], replicated
- norm1_bias_grad: float32 [1024], replicated
- norm2_gain_grad: float32 [1024], replicated
- norm2_bias_grad: float32 [1024], replicated
- crop_rms: float32 [3, 32], replicated
Inputs may be any that keep to these rules, and one draw needn't show every extreme that they name: Crops lie in order and do not intersection: crop c covers pixels crop_offsets[c] to crop_offsets[c] + crop_lengths[c] - 1. Crop 0 starts at pixel 0 and has exactly 3072 pixels. Crops that would pass the end are cut short; those starting at or past the end have length 0. `crop_offsets`: Non-decreasing; a crop of length 0 at the end has offset 12288. `up_weight`: entries of order 1024 ** -0.5.
All inputs are finite; a program needn't handle non-finite values. No bound on the sum of `pixel_mask` on one device may be relied on, other than what follows from the above.
Results may differ from a plain program's by a relative error of at most 0.02.
Values may be sent and summed in bfloat16 or wider, within the bound.
No kernel may reach another device: no remote copies, remote signals or barrier semaphores. Data moves between devices by JAX's collectives and lax.ppermute only.
A program may use at most 192 MiB of HBM per device.

v0:
```python
import functools

import jax
import jax.numpy as jnp
from jax import lax
from jax.experimental import pallas as pl
from jax.experimental.pallas import tpu as pltpu
from jax.sharding import PartitionSpec as P

D = 1024
HEAD = 64
CHUNK = 384
CROP_MAX = 3072
PACK = HEAD + 16

BF = jnp.bfloat16
F32 = jnp.float32
precise = lax.Precision.HIGHEST


def nn(a, b):
    return lax.dot_general(a, b, (((1,), (0,)), ((), ())), preferred_element_type=F32)


def nt(a, b):
    return lax.dot_general(a, b, (((1,), (1,)), ((), ())), preferred_element_type=F32)


def tn(a, b):
    return lax.dot_general(a, b, (((0,), (0,)), ((), ())), preferred_element_type=F32)


def same_head(width):
    row = lax.broadcasted_iota(jnp.int32, (width, width), 0) // HEAD
    col = lax.broadcasted_iota(jnp.int32, (width, width), 1) // HEAD
    return row == col


def lane_head(rows, width):
    return lax.broadcasted_iota(jnp.int32, (rows, width), 1) // HEAD


def causal(rows):
    row = lax.broadcasted_iota(jnp.int32, (rows, rows), 0)
    col = lax.broadcasted_iota(jnp.int32, (rows, rows), 1)
    return row >= col


def fold_heads(full, width):
    out = full[0:HEAD]
    for h in range(1, width // HEAD):
        out = out + full[h * HEAD : (h + 1) * HEAD]
    return out


def spread_heads(part, width, block):
    tall = jnp.concatenate([part] * (width // HEAD), axis=0)
    return jnp.where(block, tall, jnp.zeros_like(tall))


def pick(mask, value):
    return jnp.where(mask, value, jnp.zeros_like(value))


def vmem():
    return pl.BlockSpec(memory_space=pltpu.VMEM)


def smem():
    return pl.BlockSpec(memory_space=pltpu.SMEM)


def shape(rows, cols, kind):
    return jax.ShapeDtypeStruct((rows, cols), kind)


ROW_TILE = 192


def tiles(rows):
    return [slice(i, i + ROW_TILE) for i in range(0, rows, ROW_TILE)]


def kernel(body, name, out_shape, in_specs, megabytes, scratch=(), aliases=None, tokens=()):
    outs = vmem() if not isinstance(out_shape, tuple) else (vmem(),) * len(out_shape)
    count = len(in_specs)

    def run(*refs):
        body(*refs[:count], *refs[count + len(tokens) :])

    call = pl.pallas_call(
        run,
        out_shape=out_shape,
        in_specs=in_specs + [pl.BlockSpec(memory_space=pl.ANY)] * len(tokens),
        out_specs=outs,
        scratch_shapes=list(scratch),
        input_output_aliases=aliases or {},
        compiler_params=pltpu.CompilerParams(vmem_limit_bytes=megabytes << 20),
        name=name,
    )
    return lambda *args: call(*args, *tokens)


def normal(values):
    centre = jnp.mean(values, axis=-1, keepdims=True)
    moved = values - centre
    scale = lax.rsqrt(jnp.mean(moved * moved, axis=-1, keepdims=True) + 1e-05)
    return moved * scale, scale


def normal_back(grad, gain, xhat, scale):
    g = grad * gain
    return scale * (
        g - jnp.mean(g, axis=-1, keepdims=True) - xhat * jnp.mean(g * xhat, axis=-1, keepdims=True)
    )


def total(refs):
    value = refs[0][...].astype(F32)
    for ref in refs[1:]:
        value = value + ref[...].astype(F32)
    return value


def norm_body(x_ref, gain_ref, bias_ref, out_ref):
    for at in tiles(x_ref.shape[0]):
        xhat, _ = normal(x_ref[at, :].astype(F32))
        out_ref[at, :] = (xhat * gain_ref[...] + bias_ref[...]).astype(BF)


def norm_one(x, gain, bias):
    call = kernel(norm_body, "norm_one", shape(x.shape[0], D, BF), [vmem()] * 3, 8)
    return call(x, gain, bias)


def total(refs, at):
    value = refs[0][at, :].astype(F32)
    for ref in refs[1:]:
        value = value + ref[at, :].astype(F32)
    return value


def middle_body(*refs):
    x_ref, gain_ref, bias_ref = refs[:3]
    parts = refs[3:-3]
    middle_ref, out_ref, square_ref = refs[-3:]
    for at in tiles(x_ref.shape[0]):
        attended = total(parts, at)
        middle = x_ref[at, :].astype(F32) + attended
        middle_ref[at, :] = middle
        xhat, _ = normal(middle)
        out_ref[at, :] = (xhat * gain_ref[...] + bias_ref[...]).astype(BF)
        square_ref[at, :] = jnp.sum(attended * attended, axis=-1, keepdims=True)


def norm_two(x, gain, bias, parts):
    rows = x.shape[0]
    call = kernel(
        middle_body, "norm_two", (shape(rows, D, F32), shape(rows, D, BF), shape(rows, 1, F32)),
        [vmem()] * (3 + len(parts)), 12,
    )
    return call(x, gain, bias, *parts)


def middle_back_body(*refs):
    grad_ref, middle_ref, gain_ref = refs[:3]
    parts = refs[3:-4]
    wide_ref, low_ref, gain_grad_ref, bias_grad_ref = refs[-4:]
    gain_grad = bias_grad = jnp.zeros(gain_ref.shape, F32)
    for at in tiles(grad_ref.shape[0]):
        grad = total(parts, at)
        xhat, scale = normal(middle_ref[at, :])
        gain_grad = gain_grad + jnp.sum(grad * xhat, axis=0, keepdims=True)
        bias_grad = bias_grad + jnp.sum(grad, axis=0, keepdims=True)
        out = grad_ref[at, :].astype(F32) + normal_back(grad, gain_ref[...], xhat, scale)
        wide_ref[at, :] = out
        low_ref[at, :] = out.astype(BF)
    gain_grad_ref[...] = gain_grad
    bias_grad_ref[...] = bias_grad


def norm_two_back(grad, middle, gain, parts, tokens):
    rows = grad.shape[0]
    call = kernel(
        middle_back_body, "norm_two_back",
        (shape(rows, D, F32), shape(rows, D, BF), shape(1, D, F32), shape(1, D, F32)),
        [vmem()] * (3 + len(parts)), 16, tokens=tokens,
    )
    return call(grad, middle, gain, *parts)


def pixels_back_body(*refs):
    x_ref, wide_ref, gain_ref = refs[:3]
    parts = refs[3:-3]
    out_ref, gain_grad_ref, bias_grad_ref = refs[-3:]
    gain_grad = bias_grad = jnp.zeros(gain_ref.shape, F32)
    for at in tiles(x_ref.shape[0]):
        grad = total(parts, at)
        xhat, scale = normal(x_ref[at, :].astype(F32))
        gain_grad = gain_grad + jnp.sum(grad * xhat, axis=0, keepdims=True)
        bias_grad = bias_grad + jnp.sum(grad, axis=0, keepdims=True)
        out_ref[at, :] = (wide_ref[at, :] + normal_back(grad, gain_ref[...], xhat, scale)).astype(BF)
    gain_grad_ref[...] = gain_grad
    bias_grad_ref[...] = bias_grad


def norm_one_back(x, wide, gain, parts):
    rows = x.shape[0]
    call = kernel(
        pixels_back_body, "norm_one_back", (shape(rows, D, BF), shape(1, D, F32), shape(1, D, F32)),
        [vmem()] * (3 + len(parts)), 16,
    )
    return call(x, wide, gain, *parts)


def result_body(*refs):
    middle_ref = refs[0]
    parts = refs[1:-3]
    out_ref, result_square_ref, branch_square_ref = refs[-3:]
    for at in tiles(middle_ref.shape[0]):
        branch = total(parts, at)
        result = middle_ref[at, :] + branch
        out_ref[at, :] = result.astype(BF)
        result_square_ref[at, :] = jnp.sum(result * result, axis=-1, keepdims=True)
        branch_square_ref[at, :] = jnp.sum(branch * branch, axis=-1, keepdims=True)


def finish(middle, parts, tokens):
    rows = middle.shape[0]
    call = kernel(
        result_body, "finish", (shape(rows, D, BF), shape(rows, 1, F32), shape(rows, 1, F32)),
        [vmem()] * (1 + len(parts)), 12, tokens=tokens,
    )
    return call(middle, *parts)


def pair_slices(pair, rows):
    for i in range(2):
        yield i, slice(i * rows, (i + 1) * rows), slice((2 * pair + i) * rows, (2 * pair + i + 1) * rows)


def qkv_body(pair, tail_ref, xa_ref, xb_ref, w_ref, valid_ref, seg_ref, was_ref, *rest):
    q_ref, k_ref, v_ref, pack_ref = rest[-4:]
    width = q_ref.shape[1]
    block = same_head(width)
    state, sums = was_ref[0:HEAD, :], was_ref[HEAD:PACK, :]
    for i, _, at in pair_slices(pair, xa_ref.shape[0]):
        x = (xa_ref, xb_ref)[i][...]
        q_ref[at, :] = feature(nn(x, w_ref[0])).astype(BF)
        k = (feature(nn(x, w_ref[1])) * valid_ref[at, :]).astype(BF)
        v = nn(x, w_ref[2]).astype(BF)
        k_ref[at, :] = k
        v_ref[at, :] = v
        kept = pick(seg_ref[at, :] == tail_ref[0], k)
        state = state + fold_heads(pick(block, tn(kept, v)), width)
        sums = sums + jnp.sum(kept.astype(F32), axis=0, keepdims=True)
    pack_ref[0:HEAD, :] = state
    pack_ref[HEAD:PACK, :] = sums


def project_qkv(pair, tail, xa, xb, w, valid, seg, was, made):
    width, whole = w.shape[2], valid.shape[0]
    call = kernel(
        functools.partial(qkv_body, pair), "project_qkv",
        (shape(whole, width, BF),) * 3 + (shape(PACK, width, F32),),
        [smem()] + [vmem()] * (6 + len(made)), 16,
        aliases={7 + i: i for i in range(len(made))},
    )
    return call(tail, xa, xb, w, valid, seg, was, *made)


def swap_heads(x):
    return jnp.concatenate(
        [pltpu.roll(x[:, i : i + 2 * HEAD], HEAD, 1) for i in range(0, x.shape[1], 2 * HEAD)], axis=1
    )


def forward_body(
    last_ref, spot_ref, q_ref, k_ref, v_ref, segc_ref, segr_ref, num_ref, den_ref, st_ref, ks_ref
):
    rows, width = q_ref.shape
    size = CHUNK
    block = same_head(width)
    ones_block = block.astype(BF)
    lanes = lane_head(size, width)
    even = (lanes % 2) == 0
    lower = causal(size)
    st_ref[...] = jnp.zeros_like(st_ref)
    ks_ref[...] = jnp.zeros_like(ks_ref)

    def step(c, carry):
        spot = spot_ref[c]
        at = pl.ds(pl.multiple_of(spot * size, size), size)
        q, k, v = q_ref[at, :], k_ref[at, :], v_ref[at, :]
        seg = segc_ref[at, :]
        keep = (lower & (seg == segr_ref[spot])).astype(BF)
        before, after = last_ref[c], last_ref[c + 1]
        carried = (seg == before).astype(F32)
        sums = [jnp.zeros((size, width), F32)] * 2
        for h in range(width // HEAD):
            mine = lanes == h
            score = nt(pick(mine, q), k).astype(BF) * keep
            both = jnp.where(mine, v, (lanes == (h ^ 1)).astype(BF))
            sums[h % 2] = sums[h % 2] + nn(score, both)
        num = jnp.where(even, sums[0], sums[1])
        den = swap_heads(jnp.where(even, sums[1], sums[0]))
        num_ref[at, :] = num + carried * nn(q, st_ref[...].astype(BF))
        den_ref[at, :] = den + carried * nn((q.astype(F32) * ks_ref[0:1, :]).astype(BF), ones_block)
        kept = pick(seg == after, k)
        cont = (before == after).astype(F32)
        st_ref[...] = cont * st_ref[...] + pick(block, tn(kept, v))
        ks_ref[...] = cont * ks_ref[...] + jnp.sum(kept.astype(F32), axis=0, keepdims=True)
        return carry

    lax.fori_loop(0, rows // size, step, 0)


def attend(last, spot, q, k, v, segc, segr):
    rows, width = q.shape
    call = kernel(
        forward_body, "attend", (shape(rows, width, F32),) * 2, [smem()] * 2 + [vmem()] * 5, 24,
        scratch=[pltpu.VMEM((width, width), F32), pltpu.VMEM((8, width), F32)],
    )
    return call(last, spot, q, k, v, segc, segr)


def project_body(
    pair, first_ref, num_ref, den_ref, q_ref, pack_ref, segc_ref, valid_ref, w_ref,
    heads_ref, wide_ref, rinv_ref, a_ref, b_ref
):
    width = q_ref.shape[1]
    block = same_head(width)
    state = spread_heads(pack_ref[0:HEAD, :], width, block).astype(BF)
    sums = pack_ref[HEAD : HEAD + 1, :]
    for i, own, at in pair_slices(pair, a_ref.shape[0]):
        q = q_ref[at, :]
        opening = (segc_ref[at, :] == first_ref[0]).astype(F32)
        valid = valid_ref[at, :]
        num = num_ref[at, :] + opening * nn(q, state)
        den = den_ref[at, :] + opening * nn((q.astype(F32) * sums).astype(BF), block.astype(BF))
        rinv = valid / (den + 1e-06 + 1.0 - valid)
        wide = num * rinv
        heads = wide.astype(BF)
        heads_ref[own, :] = heads
        wide_ref[own, :] = wide
        rinv_ref[own, :] = rinv
        (a_ref, b_ref)[i][...] = nn(heads, w_ref[...]).astype(BF)


def project(pair, rows, last, num, den, q, pack, segc, valid, w, tokens):
    width = q.shape[1]
    call = kernel(
        functools.partial(project_body, pair), "project",
        (shape(2 * rows, width, BF), shape(2 * rows, width, F32), shape(2 * rows, width, F32))
        + (shape(rows, D, BF),) * 2,
        [smem()] + [vmem()] * 7, 12, tokens=tokens,
    )
    return call(last, num, den, q, pack, segc, valid, w)


def mlp_body(
    xa_ref, xb_ref, ga_ref, gb_ref, up_ref, down_ref, act_ref, hid_ref, na_ref, nb_ref, ba_ref, bb_ref
):
    root = 0.7978845608028654
    tile = min(512, up_ref.shape[1])
    for i, own, _ in pair_slices(0, xa_ref.shape[0]):
        x, g = (xa_ref, xb_ref)[i][...], (ga_ref, gb_ref)[i][...]
        for j in range(0, up_ref.shape[1], tile):
            cols = slice(j, j + tile)
            h = nn(x, up_ref[:, cols])
            grad = nt(g, down_ref[cols, :])
            square = h * h
            t = jnp.tanh(root * h * (1.0 + 0.044715 * square))
            plus = 0.5 * (1.0 + t)
            slope = plus + 0.5 * h * (1.0 - t * t) * (root + (3.0 * 0.044715 * root) * square)
            act_ref[own, cols] = (h * plus).astype(BF)
            hid_ref[own, cols] = (grad * slope).astype(BF)
        (na_ref, nb_ref)[i][...] = nt(hid_ref[own, :], up_ref[...]).astype(BF)
        (ba_ref, bb_ref)[i][...] = nn(act_ref[own, :], down_ref[...]).astype(BF)


def mlp(xa, xb, ga, gb, up, down):
    rows, hidden = xa.shape[0], up.shape[1]
    call = kernel(
        mlp_body, "mlp", (shape(2 * rows, hidden, BF),) * 2 + (shape(rows, D, BF),) * 4,
        [vmem()] * 6, 32,
    )
    return call(xa, xb, ga, gb, up, down)


def heads_back_body(
    pair, first_ref, ga_ref, gb_ref, w_ref, wide_ref, rinv_ref, q_ref, segc_ref, was_ref, *rest
):
    ng_ref, dg_ref, pack_ref = rest[-3:]
    width = q_ref.shape[1]
    block = same_head(width)
    ones_block = block.astype(BF)
    state, sums = was_ref[0:HEAD, :], was_ref[HEAD:PACK, :]
    for i, own, at in pair_slices(pair, ga_ref.shape[0]):
        hg = nt((ga_ref, gb_ref)[i][...], w_ref[...])
        rinv = rinv_ref[own, :]
        ng = (hg * rinv).astype(BF)
        prod = hg * wide_ref[own, :]
        high = prod.astype(BF)
        low = (prod - high.astype(F32)).astype(BF)
        dg = -(nn(high, ones_block) + nn(low, ones_block)) * rinv
        ng_ref[at, :] = ng
        dg_ref[at, :] = dg
        opened = pick(segc_ref[at, :] == first_ref[0], q_ref[at, :])
        state = state + fold_heads(pick(block, tn(opened, ng)), width)
        sums = sums + jnp.sum(opened.astype(F32) * dg, axis=0, keepdims=True)
    pack_ref[0:HEAD, :] = state
    pack_ref[HEAD:PACK, :] = sums


def heads_back(pair, last, ga, gb, w, wide, rinv, q, segc, was, made, tokens=()):
    whole, width = q.shape
    call = kernel(
        functools.partial(heads_back_body, pair), "heads_back",
        (shape(whole, width, BF), shape(whole, width, F32), shape(PACK, width, F32)),
        [smem()] + [vmem()] * (8 + len(made)), 16,
        aliases={9 + i: i for i in range(len(made))}, tokens=tokens,
    )
    return call(last, ga, gb, w, wide, rinv, q, segc, was, *made)


def backward_body(
    last_ref, spot_ref, q_ref, k_ref, v_ref, ng_ref, dg_ref, segc_ref, segr_ref, pack_ref,
    dq_ref, dk_ref, dv_ref, all_ref, sums_ref, st_ref, ks_ref
):
    rows, width = q_ref.shape
    size = CHUNK
    count = rows // size
    block = same_head(width)
    lanes = lane_head(size, width)
    half = (lax.broadcasted_iota(jnp.int32, (size, width), 1) % HEAD) < HEAD // 2
    lower = causal(size)
    st_ref[...] = spread_heads(pack_ref[0:HEAD, :], width, block)
    ks_ref[...] = jnp.broadcast_to(pack_ref[HEAD : HEAD + 1, :], ks_ref.shape)

    def collect(c, carry):
        at = pl.ds(pl.multiple_of(spot_ref[c] * size, size), size)
        all_ref[c] = st_ref[...].astype(BF)
        sums_ref[c] = ks_ref[...]
        before, after = last_ref[c], last_ref[c + 1]
        kept = pick(segc_ref[at, :] == after, k_ref[at, :])
        cont = (before == after).astype(F32)
        st_ref[...] = cont * st_ref[...] + pick(block, tn(kept, v_ref[at, :]))
        ks_ref[...] = cont * ks_ref[...] + jnp.sum(kept.astype(F32), axis=0, keepdims=True)
        return carry

    lax.fori_loop(0, count, collect, 0)
    st_ref[...] = jnp.zeros_like(st_ref)
    ks_ref[...] = jnp.zeros_like(ks_ref)

    def step(i, carry):
        c = count - 1 - i
        spot = spot_ref[c]
        at = pl.ds(pl.multiple_of(spot * size, size), size)
        q, k, v, ng, dg = q_ref[at, :], k_ref[at, :], v_ref[at, :], ng_ref[at, :], dg_ref[at, :]
        seg = segc_ref[at, :]
        keep = (lower & (seg == segr_ref[spot])).astype(BF)
        before, after = last_ref[c], last_ref[c + 1]
        opened = seg == before
        carried = opened.astype(F32)
        tail = (seg == after).astype(F32)
        grad_state = st_ref[...].astype(BF)
        moved = swap_heads(dg)
        high = moved.astype(BF)
        low = (moved - high.astype(F32)).astype(BF)
        terms = jnp.where(half, high, low) * jnp.asarray(2.0 / HEAD, BF)
        one = jnp.ones((), BF)
        dq = carried * (nt(ng, all_ref[c]) + dg * sums_ref[c][0:1, :])
        dk = tail * (nt(v, grad_state) + ks_ref[0:1, :])
        dv = tail * nn(k, grad_state)
        for h in range(width // HEAD):
            mine = lanes == h
            qh, kh, nh = pick(mine, q), pick(mine, k), pick(mine, ng)
            score = nt(qh, k).astype(BF) * keep
            left = jnp.where(mine, ng, pick(lanes == (h ^ 1), terms))
            back = nt(left, jnp.where(mine, v, one)).astype(BF) * keep
            dq = dq + nn(back, kh)
            dk = dk + tn(back, qh)
            dv = dv + tn(score, nh)
        dq_ref[at, :] = (dq * jnp.minimum(q.astype(F32), 1.0)).astype(BF)
        dk_ref[at, :] = dk
        dv_ref[at, :] = dv
        cont = (before == after).astype(F32)
        st_ref[...] = cont * st_ref[...] + pick(block, tn(pick(opened, q), ng))
        ks_ref[...] = cont * ks_ref[...] + jnp.sum(carried * q.astype(F32) * dg, axis=0, keepdims=True)
        return carry

    lax.fori_loop(0, count, step, 0)


def attend_back(last, spot, q, k, v, ng, dg, segc, segr, pack, tokens):
    rows, width = q.shape
    count = rows // CHUNK
    call = kernel(
        backward_body, "attend_back",
        (shape(rows, width, BF), shape(rows, width, F32), shape(rows, width, F32)),
        [smem()] * 2 + [vmem()] * 8, 32,
        scratch=[
            pltpu.VMEM((count, width, width), BF),
            pltpu.VMEM((count, 8, width), F32),
            pltpu.VMEM((width, width), F32),
            pltpu.VMEM((8, width), F32),
        ],
        tokens=tokens,
    )
    return call(last, spot, q, k, v, ng, dg, segc, segr, pack)


def mix_body(
    pair, tail_ref, dq_ref, dk_ref, dv_ref, k_ref, v_ref, segc_ref, valid_ref, pack_ref, w_ref,
    mixed_ref, a_ref, b_ref
):
    width = k_ref.shape[1]
    block = same_head(width)
    state = spread_heads(pack_ref[0:HEAD, :], width, block).astype(BF)
    sums = pack_ref[HEAD : HEAD + 1, :]
    for i, own, at in pair_slices(pair, a_ref.shape[0]):
        tail = (segc_ref[at, :] == tail_ref[0]).astype(F32)
        k = k_ref[at, :]
        dk = dk_ref[at, :] + tail * (nt(v_ref[at, :], state) + sums)
        dv = dv_ref[at, :] + tail * nn(k, state)
        dq = dq_ref[at, :]
        dk = (valid_ref[at, :] * dk * jnp.minimum(k.astype(F32), 1.0)).astype(BF)
        dv = dv.astype(BF)
        mixed_ref[own, 0:width] = dq
        mixed_ref[own, width : 2 * width] = dk
        mixed_ref[own, 2 * width : 3 * width] = dv
        out = nt(dq, w_ref[0]) + nt(dk, w_ref[1]) + nt(dv, w_ref[2])
        (a_ref, b_ref)[i][...] = out.astype(BF)


def mix(pair, rows, tail, dq, dk, dv, k, v, segc, valid, pack, w, tokens):
    width = k.shape[1]
    call = kernel(
        functools.partial(mix_body, pair), "mix",
        (shape(2 * rows, 3 * width, BF),) + (shape(rows, D, BF),) * 2,
        [smem()] + [vmem()] * 9, 16, tokens=tokens,
    )
    return call(tail, dq, dk, dv, k, v, segc, valid, pack, w)


def feature(values):
    return jnp.where(values > 0, values + 1.0, jnp.exp(jnp.minimum(values, 0.0)))


def bits_of(count):
    return [1 << b for b in range(count.bit_length() - 1)]


def swap(value, axis, bit):
    return lax.ppermute(value, axis, [(i, i ^ bit) for i in range(lax.axis_size(axis))])


def after(value, *tokens):
    return lax.optimization_barrier((value, *tokens))[0] if tokens else value


def gather_begin(value):
    slots = {0: value}
    for bit in reversed(bits_of(lax.axis_size("feat"))[1:]):
        for s in sorted(slots):
            slots[s | bit] = swap(slots[s], "feat", bit)
    slots[1] = swap(value, "feat", 1)
    return slots


def gather_end(slots, *tokens):
    for s in range(2, lax.axis_size("feat"), 2):
        slots[s + 1] = swap(after(slots[s], *tokens), "feat", 1)
    return [slots[s] for s in range(len(slots))]


def scatter_begin(parts):
    sums = {}
    for s in range(len(parts) - 2, -1, -2):
        got = swap(parts[s + 1], "feat", 1)
        sums[s] = (parts[s].astype(F32) + got.astype(F32)).astype(BF) if s else [parts[0], got]
    return sums


def scatter_end(sums, *tokens):
    sums = {s: part if s == 0 else [after(part, *tokens)] for s, part in sums.items()}
    for bit in bits_of(lax.axis_size("feat"))[1:]:
        for s in sorted(sums, reverse=True):
            if s & bit:
                pieces = sums.pop(s)
                value = pieces[0]
                if len(pieces) > 1:
                    value = functools.reduce(jnp.add, [p.astype(F32) for p in pieces]).astype(BF)
                sums[s ^ bit].append(swap(value, "feat", bit))
    return sums[0]


def sum_everywhere(value):
    for axis in ("feat", "rows"):
        for bit in bits_of(lax.axis_size(axis)):
            value = value + swap(value, axis, bit)
    return value


class RowSum:
    def __init__(self, value, order, *tokens):
        self.order, self.step = order, 0
        self.value = after(value, *tokens)
        self.launch()

    def launch(self):
        count = len(self.order)
        halving = self.step < count
        bit = self.order[self.step] if halving else self.order[2 * count - 1 - self.step]
        self.upper = (lax.axis_index("rows") & bit) != 0
        self.sent = self.kept = self.value
        if halving:
            half = self.value.shape[0] // 2
            low, high = self.value[:half], self.value[half:]
            self.sent = jnp.where(self.upper, low, high)
            self.kept = jnp.where(self.upper, high, low)
        self.got = swap(self.sent, "rows", bit)

    def next(self, *tokens):
        got = after(self.got, *tokens)
        if self.step < len(self.order):
            self.value = (self.kept.astype(F32) + got.astype(F32)).astype(BF)
        else:
            first = jnp.where(self.upper, got, self.kept)
            self.value = jnp.concatenate([first, jnp.where(self.upper, self.kept, got)], axis=0)
        self.step += 1
        if self.step < 2 * len(self.order):
            self.launch()
            return self.sent
        return self.value

    def finish(self, *tokens):
        while self.step < 2 * len(self.order):
            self.next(*tokens)
        return self.value


def shifted(pack, hop, groups, reverse):
    if reverse:
        pairs = [(i, i - hop) for i in range(hop, groups)]
    else:
        pairs = [(i, i + hop) for i in range(groups - hop)]
    return lax.ppermute(pack, "rows", pairs)


def gather_carry(pack, crops_at, here, groups, reach, reverse):
    total = jnp.zeros(pack.shape, F32)
    mine = crops_at[here + 1] if reverse else crops_at[here]
    for hop in range(1, reach + 1):
        got = shifted(pack, hop, groups, reverse).astype(F32)
        other = here + hop if reverse else here - hop
        inside = (other < groups) if reverse else (other >= 0)
        at = jnp.clip(other, 0, groups - 1)
        theirs = crops_at[at] if reverse else crops_at[at + 1]
        total = total + jnp.where(inside & (theirs == mine), got, 0.0)
    return total


def on_device(
    pixels,
    qkv_weight,
    out_weight,
    up_weight,
    down_weight,
    norm1_gain,
    norm1_bias,
    norm2_gain,
    norm2_bias,
    crop_lengths,
    crop_offsets,
    pixel_mask,
    out_grad,
):
    local_rows = pixels.shape[0]
    group_rows = pixel_mask.shape[0]
    width = qkv_weight.shape[2]
    crop_count = crop_offsets.shape[0]
    groups = lax.axis_size("rows")
    members = lax.axis_size("feat")
    pairs = members // 2
    here = lax.axis_index("rows")
    member = lax.axis_index("feat")
    reach = min(groups - 1, -(-(CROP_MAX - 1) // group_rows))
    group_start = here * group_rows
    slot_ids = jnp.arange(members, dtype=jnp.int32) ^ member
    in_group = (slot_ids[:, None] * local_rows + jnp.arange(local_rows, dtype=jnp.int32)[None, :]).reshape(-1)
    places = group_start + in_group
    started = crop_offsets[None, :] <= places[:, None]
    crop_ends = crop_offsets + crop_lengths
    segment = jnp.sum(started.astype(jnp.int32), axis=1) - 1
    inside = jnp.sum((started & (places[:, None] < crop_ends[None, :])).astype(jnp.int32), axis=1)
    mask = jnp.concatenate(
        [
            lax.dynamic_slice_in_dim(pixel_mask, (member ^ s) * local_rows, local_rows)
            for s in range(members)
        ]
    )
    pixel_valid = (mask * inside).astype(F32)
    edges = jnp.arange(groups + 1, dtype=jnp.int32) * group_rows - 1
    crops_at = jnp.sum((crop_offsets[None, :] <= edges[:, None]).astype(jnp.int32), axis=1) - 1
    chunks = group_rows // CHUNK
    per = local_rows // CHUNK
    chunk_edges = group_start - 1 + jnp.arange(chunks + 1, dtype=jnp.int32) * CHUNK
    last = jnp.sum((crop_offsets[None, :] <= chunk_edges[:, None]).astype(jnp.int32), axis=1) - 1
    tail = last[-1:]
    order = jnp.arange(chunks, dtype=jnp.int32)
    spot = ((order // per) ^ member) * per + order % per
    segc = segment[:, None]
    segr = segment.reshape(chunks, 1, CHUNK)
    validc = pixel_valid[:, None]
    gain1, bias1, gain2, bias2 = (
        a[None, :] for a in (norm1_gain, norm1_bias, norm2_gain, norm2_bias)
    )
    no_pack = jnp.zeros((PACK, width), F32)

    normed_slots = gather_begin(norm_one(pixels, gain1, bias1))
    grad_slots = gather_begin(after(out_grad, normed_slots[members // 2]))
    *made, pack = project_qkv(0, tail, normed_slots[0], normed_slots[1], qkv_weight, validc, segc, no_pack, ())
    normed_slots = gather_end(normed_slots, pack)
    for p in range(1, pairs):
        *made, pack = project_qkv(
            p, tail, normed_slots[2 * p], normed_slots[2 * p + 1], qkv_weight, validc, segc, pack, made
        )
    q, k, v = made
    carry = gather_carry(pack.astype(BF), crops_at, here, groups, reach, False)
    num, den = attend(last, spot, q, k, v, segc, segr)
    grad_slots = gather_end(grad_slots, num)
    sent = {
        p: project(
            p, local_rows, last, num, den, q, carry, segc, validc, out_weight, [grad_slots[members // 2]]
        )
        for p in reversed(range(pairs))
    }
    parts = scatter_end(scatter_begin([sent[s // 2][3 + s % 2] for s in range(members)]))
    middle, normed_two, attended_square = norm_two(pixels, gain2, bias2, parts)
    two_slots = gather_begin(normed_two)
    hidden = [mlp(two_slots[0], two_slots[1], grad_slots[0], grad_slots[1], up_weight, down_weight)]
    two_slots = gather_end(two_slots, hidden[0][0])
    for p in range(1, pairs):
        hidden.append(mlp(*two_slots[2 * p : 2 * p + 2], *grad_slots[2 * p : 2 * p + 2], up_weight, down_weight))
    two_parts = scatter_end(scatter_begin([hidden[s // 2][2 + s % 2] for s in range(members)]))
    branch_sums = scatter_begin([hidden[s // 2][4 + s % 2] for s in range(members)])
    down_grad = tn(
        jnp.concatenate([h[0] for h in hidden], axis=0), jnp.concatenate(grad_slots, axis=0)
    ).astype(BF)
    up_grad = tn(
        jnp.concatenate(two_slots, axis=0), jnp.concatenate([h[1] for h in hidden], axis=0)
    ).astype(BF)
    bits = bits_of(groups)
    turned = bits[1:] + bits[:1]
    down_sum = RowSum(down_grad, bits, two_parts[-1])
    up_sum = RowSum(up_grad, turned, two_parts[-1])
    middle_grad, middle_low, gain2_grad, bias2_grad = norm_two_back(
        out_grad, middle, gain2, two_parts,
        [down_sum.sent, up_sum.sent, branch_sums[0][1], branch_sums[members - 2]],
    )
    middle_slots = gather_begin(middle_low)
    *made, grad_pack = heads_back(
        0, last, middle_slots[0], middle_slots[1], out_weight, sent[0][1], sent[0][2], q, segc, no_pack, ()
    )
    branch_parts = scatter_end(branch_sums, middle_slots[members // 2])
    tokens = [x.next(middle_slots[members // 2]) for x in (down_sum, up_sum)]
    middle_slots = gather_end(middle_slots, grad_pack)
    for p in range(1, pairs):
        *made, grad_pack = heads_back(
            p, last, middle_slots[2 * p], middle_slots[2 * p + 1], out_weight,
            sent[p][1], sent[p][2], q, segc, grad_pack, made, tokens
        )
    ng, dg = made
    grad_carry = gather_carry(grad_pack.astype(BF), crops_at, here, groups, reach, True)
    out_weight_grad = tn(
        jnp.concatenate([sent[p][0] for p in range(pairs)], axis=0), jnp.concatenate(middle_slots, axis=0)
    ).astype(BF)
    tokens = [out_weight_grad]
    dq, dk, dv = attend_back(last, spot, q, k, v, ng, dg, segc, segr, carry, tokens)
    out_sum = RowSum(out_weight_grad, turned, dq)
    tokens = [down_sum.next(dq), up_sum.next(dq), out_sum.sent]
    mixes = {
        p: mix(p, local_rows, tail, dq, dk, dv, k, v, segc, validc, grad_carry, qkv_weight, tokens)
        for p in reversed(range(pairs))
    }
    normed_sums = scatter_begin([mixes[s // 2][1 + s % 2] for s in range(members)])
    normed_parts = scatter_end(normed_sums)
    mixed_grad = jnp.concatenate([mixes[p][0] for p in range(pairs)], axis=0)
    qkv_grad = tn(mixed_grad, jnp.concatenate(normed_slots, axis=0)).astype(BF)
    output, result_square, branch_square = finish(middle, branch_parts, [dq])
    pixels_grad, gain1_grad, bias1_grad = norm_one_back(pixels, middle_grad, gain1, normed_parts)

    tokens = [down_sum.next(mixed_grad), up_sum.next(mixed_grad), out_sum.next(mixed_grad)]
    cut = 3 * width // 2
    low_sum = RowSum(qkv_grad[:cut], bits, *tokens)
    high_sum = RowSum(qkv_grad[cut:], turned, *tokens)
    normed_sent = normed_sums[members - 2]
    tokens = [low_sum.next(normed_sent), high_sum.next(normed_sent)]
    tokens = [down_sum.next(*tokens), up_sum.next(*tokens), out_sum.next(*tokens)]
    tokens = [low_sum.next(*tokens), high_sum.next(*tokens)]
    out_weight_grad = out_sum.finish(*tokens).astype(F32)
    tokens = [low_sum.next(), high_sum.next()]
    down_grad = down_sum.finish(*tokens).astype(F32)
    up_grad = up_sum.finish(*tokens).astype(F32)
    qkv_grad = jnp.concatenate([low_sum.finish(), high_sum.finish()], axis=0)
    qkv_grad = jnp.swapaxes(qkv_grad.reshape(3, width, D), 1, 2).astype(F32)

    crop_onehot = (
        segment[:local_rows, None] == jnp.arange(crop_count, dtype=jnp.int32)[None, :]
    ).astype(F32)
    squares = (
        jnp.concatenate(
            [result_square, attended_square, branch_square, jnp.ones((local_rows, 1), F32)], axis=1
        )
        * validc[:local_rows]
    )
    crop_sums = lax.dot_general(
        squares, crop_onehot, (((0,), (0,)), ((), ())), precision=precise, preferred_element_type=F32
    )
    sums = jnp.concatenate(
        [gain1_grad[0], bias1_grad[0], gain2_grad[0], bias2_grad[0], crop_sums.reshape(-1)]
    )
    sums = sum_everywhere(sums)
    gain1_grad, bias1_grad, gain2_grad, bias2_grad = sums[: 4 * D].reshape(4, D)
    crop_sums = sums[4 * D :].reshape(4, crop_count)
    crop_rms = jnp.sqrt(crop_sums[:3] / (D * jnp.maximum(crop_sums[3], 1.0))[None, :])
    return (
        output,
        pixels_grad,
        qkv_grad,
        out_weight_grad,
        up_grad,
        down_grad,
        gain1_grad,
        bias1_grad,
        gain2_grad,
        bias2_grad,
        crop_rms,
    )


def solution(mesh):
    split = P(("rows", "feat"), None)
    qkv, rows_feat, cols_feat = P(None, None, "feat"), P("feat", None), P(None, "feat")
    in_specs = (
        (split, qkv, rows_feat, cols_feat, rows_feat) + (P(),) * 6 + (P("rows"), split)
    )
    out_specs = (split, split, qkv, rows_feat, cols_feat, rows_feat) + (P(),) * 5
    return jax.shard_map(
        on_device, mesh=mesh, in_specs=in_specs, out_specs=out_specs, check_vma=False
    )
```

profile of v0, /device:TPU:0, one launch (start us, length us, event | category | flops | bytes accessed | tf_op | source)
XLA Modules:
  0.0 398.1 jit_solution(13249694806072120447)
XLA Ops:
  4.6 3.0 collective-permute-start
  15.2 4.1 %project_qkv.2 = (bf16[1536,256]{1,0:T(8,128)(2,1)S(1)}, bf16[1536,256]{1,0:T(8,128)(2,1)S(1)}, bf16[1536,256]{1,0:T(8,128)(2,1)S(1)}, f32[80,256]{1,0:T(8,128)S(1)}) custom-call(s32[1]{0:T(128)} %slice.138.refs_0_, bf16[384,1024]{1,0:T(8,128)(2,1)} %norm_one.1.refs_1_, bf16[384,1024]{1,0:T(8,128)(2,1)S(1)} %copy-done.35, bf16[3,1024,256]{2,1,0:T(8,128)(2,1)S(1)} %copy-done, ...), custom_call_target="tpu_custom_call" | custom-call | tf_op jit(solution)/shard_map/project_qkv/pallas_call | solution.py:101
  19.2 6.2 %collective-permute-done.refs_1_ = bf16[384,1024]{1,0:T(8,128)(2,1)} collective-permute-done((bf16[384,1024]{1,0:T(8,128)(2,1)}, bf16[384,1024]{1,0:T(8,128)(2,1)}, u32[]{:S(2)}, u32[]{:S(2)}) %collective-permute-start) | collective-permute-done | bytes 786464 | tf_op jit(solution)/shard_map/ppermute | solution.py:556
  25.5 1.7 collective-permute-start.5
  27.9 4.0 %project_qkv.3 = (bf16[1536,256]{1,0:T(8,128)(2,1)S(1)}, bf16[1536,256]{1,0:T(8,128)(2,1)S(1)}, bf16[1536,256]{1,0:T(8,128)(2,1)S(1)}, f32[80,256]{1,0:T(8,128)S(1)}) custom-call(s32[1]{0:T(128)} %slice.138.refs_0_, bf16[384,1024]{1,0:T(8,128)(2,1)} %collective-permute-done.refs_1_, ...), custom_call_target="tpu_custom_call", output_to_operand_aliasing={{0}: (7, {}), {1}: (8, {}), {2}: (9, {})} | custom-call | tf_op jit(solution)/shard_map/project_qkv/pallas_call | solution.py:101
  32.9 3.7 collective-permute-start.4
  36.6 3.4 collective-permute-start.3
  44.5 5.9 %attend.1 = (f32[1536,256]{1,0:T(8,128)S(1)}, f32[1536,256]{1,0:T(8,128)S(1)}) custom-call(s32[5]{0:T(128)S(1)} %broadcast_add_fusion.2.refs_0_, s32[4]{0:T(128)S(1)} %iota_xor_fusion.refs_1_, bf16[1536,256]{1,0:T(8,128)(2,1)S(1)} %get-tuple-element.109.refs_2_.refs_3_.refs_6_, bf16[1536,256]{1,0:T(8,128)(2,1)S(1)} %get-tuple-element.110.refs_3_.refs_4_, ...), custom_call_target="tpu_custom_call" | custom-call | tf_op jit(solution)/shard_map/attend/pallas_call | solution.py:101
  50.5 1.5 project.3
  54.6 1.5 project.2
  59.6 1.6 collective-permute-start.8
  61.1 18.0 %collective-permute-done.8.refs_5_ = bf16[384,1024]{1,0:T(8,128)(2,1)S(1)} collective-permute-done((bf16[384,1024]{1,0:T(8,128)(2,1)S(1)}, bf16[384,1024]{1,0:T(8,128)(2,1)S(1)}, u32[]{:S(2)}, u32[]{:S(2)}) %collective-permute-start.8) | collective-permute-done | bytes 786464 | tf_op jit(solution)/shard_map/ppermute | solution.py:556
  83.5 9.1 %mlp.2 = (bf16[768,1024]{1,0:T(8,128)(2,1)S(1)}, bf16[768,1024]{1,0:T(8,128)(2,1)S(1)}, bf16[384,1024]{1,0:T(8,128)(2,1)S(1)}, bf16[384,1024]{1,0:T(8,128)(2,1)S...) custom-call(bf16[384,1024]{1,0:T(8,128)(2,1)S(1)} %get-tuple-element.121.refs_0_, ...), custom_call_target="tpu_custom_call" | custom-call | tf_op jit(solution)/shard_map/mlp/pallas_call | solution.py:101
  98.5 2.8 collective-permute-done.12.refs_0_
  101.8 3.2 collective-permute-done.13.refs_1_
  105.0 1.6 copy-done.9
  106.6 1.6 copy-done.11
  108.2 10.0 %mlp.3 = (bf16[768,1024]{1,0:T(8,128)(2,1)S(1)}, bf16[768,1024]{1,0:T(8,128)(2,1)S(1)}, bf16[384,1024]{1,0:T(8,128)(2,1)S(1)}, bf16[384,1024]{1,0:T(8,128)(2,1)S...) custom-call(bf16[384,1024]{1,0:T(8,128)(2,1)} %collective-permute-done.12.refs_0_, ...), custom_call_target="tpu_custom_call" | custom-call | tf_op jit(solution)/shard_map/mlp/pallas_call | solution.py:101
  118.8 5.3 %fusion.43 = bf16[1024,1024]{1,0:T(8,128)(2,1)S(1)} fusion(bf16[384,1024]{1,0:T(8,128)(2,1)} %collective-permute-done.14.refs_3_, bf16[384,1024]{1,0:T(8,128)(2,1)} %collective-permute-done.5.refs_8_.refs_2_, bf16[384,1024]{1,0:T(8,128)(2,1)S(1)} %copy-done.48, bf16[384,1024]{1,0:T(8,128)(2,1)} %refs_0_.6, bf16[768,1024]{1,0:T(8,128)(2,1)S(1)} %get-tuple-element.133, ...), kind=kOutput, calls=%fused_computation.43 | convolution fusion | flops 3241148416 | bytes 8388608 | tf_op jit(solution)/shard_map/dot_general | solution.py:30
  124.5 1.6 collective-permute-start.18
  126.2 5.3 %fusion.38 = bf16[1024,1024]{1,0:T(8,128)(2,1)S(1)} fusion(bf16[768,1024]{1,0:T(8,128)(2,1)S(1)} %get-tuple-element.136, bf16[768,1024]{1,0:T(8,128)(2,1)S(1)} %copy-done.67, bf16[384,1024]{1,0:T(8,128)(2,1)} %collective-permute-done.13.refs_1_, bf16[384,1024]{1,0:T(8,128)(2,1)} %collective-permute-done.12.refs_0_, bf16[384,1024]{1,0:T(8,128)(2,1)S(1)} %copy-done.50, ...), kind=kOutput, calls=%fused_computation.42 | convolution fusion | flops 3241148416 | bytes 8388608 | tf_op jit(solution)/shard_map/dot_general | solution.py:30
  131.9 12.2 %collective-permute-done.18.refs_5_ = bf16[384,1024]{1,0:T(8,128)(2,1)S(1)} collective-permute-done((bf16[384,1024]{1,0:T(8,128)(2,1)S(1)}, bf16[384,1024]{1,0:T(8,128)(2,1)S(1)}, u32[]{:S(2)}, u32[]{:S(2)}) %collective-permute-start.18) | collective-permute-done | bytes 786464 | tf_op jit(solution)/shard_map/ppermute | solution.py:556
  145.2 1.5 collective-permute-start.23
  147.9 3.7 norm_two_back.1
  152.8 1.5 collective-permute-start.19
  154.3 1.6 collective-permute-start.24
  160.3 11.2 %collective-permute-done.19.refs_1_ = bf16[384,1024]{1,0:T(8,128)(2,1)} collective-permute-done((bf16[384,1024]{1,0:T(8,128)(2,1)}, bf16[384,1024]{1,0:T(8,128)(2,1)}, u32[]{:S(2)}, u32[]{:S(2)}) %collective-permute-start.19) | collective-permute-done | bytes 786464 | tf_op jit(solution)/shard_map/ppermute | solution.py:556
  171.5 1.5 collective-permute-start.20
  176.4 3.2 heads_back.2
  179.7 2.0 add_convert_fusion.1
  181.8 1.6 collective-permute-start.27
  183.5 1.9 add_convert_fusion
  186.0 2.9 heads_back.3
  191.6 2.7 fusion.51.refs_10_
  194.3 13.8 %attend_back.1 = (bf16[1536,256]{1,0:T(8,128)(2,1)S(1)}, f32[1536,256]{1,0:T(8,128)S(1)}, f32[1536,256]{1,0:T(8,128)S(1)}) custom-call(s32[5]{0:T(128)S(1)} %broadcast_add_fusion.2.refs_0_, s32[4]{0:T(128)S(1)} %iota_xor_fusion.refs_1_, bf16[1536,256]{1,0:T(8,128)(2,1)S(1)} %get-tuple-element.109.refs_2_.refs_3_.refs_6_, ...), custom_call_target="tpu_custom_call" | custom-call | tf_op jit(solution)/shard_map/attend_back/pallas_call | solution.py:101
  209.2 3.3 collective-permute-done.28
  213.6 2.4 collective-permute-start.32
  229.5 2.5 mix.2
  233.7 2.5 mix.3
  237.7 4.0 %fusion.48 = bf16[768,1024]{1,0:T(8,128)(2,1)S(1)} fusion(bf16[1536,768]{1,0:T(8,128)(2,1)S(1)} %constant_dynamic-update-slice_fusion, bf16[384,1024]{1,0:T(8,128)(2,1)S(1)} %copy-done.38, bf16[384,1024]{1,0:T(8,128)(2,1)} %collective-permute-done.refs_1_, bf16[384,1024]{1,0:T(8,128)(2,1)S(1)} %copy-done.36, bf16[384,1024]{1,0:T(8,128)(2,1)} %norm_one.1.refs_1_), kind=kOutput, calls=%fused_computation.44 | convolution fusion | flops 2429288448 | bytes 7077888 | tf_op jit(solution)/shard_map/dot_general | solution.py:30
  247.7 2.9 collective-permute-start.40
  253.4 16.0 %collective-permute-done.38 = bf16[192,1024]{1,0:T(8,128)(2,1)S(1)} collective-permute-done((bf16[192,1024]{1,0:T(8,128)(2,1)S(1)}, bf16[192,1024]{1,0:T(8,128)(2,1)S(1)}, u32[]{:S(2)}, u32[]{:S(2)}) %collective-permute-start.38) | collective-permute-done | bytes 393248 | tf_op jit(solution)/shard_map/ppermute | solution.py:556
  272.4 7.1 %collective-permute-done.45 = bf16[96,1024]{1,0:T(8,128)(2,1)S(1)} collective-permute-done((bf16[96,1024]{1,0:T(8,128)(2,1)S(1)}, bf16[96,1024]{1,0:T(8,128)(2,1)S(1)}, u32[]{:S(2)}, u32[]{:S(2)}) %collective-permute-start.45) | collective-permute-done | bytes 196640 | tf_op jit(solution)/shard_map/ppermute | solution.py:556
  285.2 3.8 collective-permute-done.46
  289.4 22.4 %collective-permute-done.41 = bf16[48,1024]{1,0:T(8,128)(2,1)S(1)} collective-permute-done((bf16[48,1024]{1,0:T(8,128)(2,1)S(1)}, bf16[48,1024]{1,0:T(8,128)(2,1)S(1)}, u32[]{:S(2)}, u32[]{:S(2)}) %collective-permute-start.41) | collective-permute-done | bytes 98336 | tf_op jit(solution)/shard_map/ppermute | solution.py:556
  313.0 3.5 collective-permute-done.47
  316.6 5.8 %collective-permute-done.42 = bf16[48,1024]{1,0:T(8,128)(2,1)S(1)} collective-permute-done((bf16[48,1024]{1,0:T(8,128)(2,1)S(1)}, bf16[48,1024]{1,0:T(8,128)(2,1)S(1)}, u32[]{:S(2)}, u32[]{:S(2)}) %collective-permute-start.42) | collective-permute-done | bytes 98336 | tf_op jit(solution)/shard_map/ppermute | solution.py:556
  322.4 7.8 %collective-permute-done.52 = bf16[64,1024]{1,0:T(8,128)(2,1)S(1)} collective-permute-done((bf16[64,1024]{1,0:T(8,128)(2,1)S(1)}, bf16[64,1024]{1,0:T(8,128)(2,1)S(1)}, u32[]{:S(2)}, u32[]{:S(2)}) %collective-permute-start.52) | collective-permute-done | bytes 131104 | tf_op jit(solution)/shard_map/ppermute | solution.py:556
  330.3 2.4 collective-permute-start.43
  335.5 5.9 %collective-permute-done.48 = bf16[96,1024]{1,0:T(8,128)(2,1)S(1)} collective-permute-done((bf16[96,1024]{1,0:T(8,128)(2,1)S(1)}, bf16[96,1024]{1,0:T(8,128)(2,1)S(1)}, u32[]{:S(2)}, u32[]{:S(2)}) %collective-permute-start.48) | collective-permute-done | bytes 196640 | tf_op jit(solution)/shard_map/ppermute | solution.py:556
  341.6 2.6 norm_one_back.1
  345.5 2.0 collective-permute-start.49
  347.5 1.6 collective-permute-start.59
  349.2 2.2 collective-permute-done.59
  351.4 2.0 collective-permute-start.60
  354.2 14.1 %collective-permute-done.60 = f32[4224]{0:T(1024)S(1)} collective-permute-done((f32[4224]{0:T(1024)S(1)}, f32[4224]{0:T(1024)S(1)}, u32[]{:S(2)}, u32[]{:S(2)}) %collective-permute-start.60) | collective-permute-done | bytes 16928 | tf_op jit(solution)/shard_map/ppermute | solution.py:556
  368.2 2.1 collective-permute-start.61
  370.4 8.2 %collective-permute-done.61 = f32[4224]{0:T(1024)S(1)} collective-permute-done((f32[4224]{0:T(1024)S(1)}, f32[4224]{0:T(1024)S(1)}, u32[]{:S(2)}, u32[]{:S(2)}) %collective-permute-start.61) | collective-permute-done | bytes 16928 | tf_op jit(solution)/shard_map/ppermute | solution.py:556
  379.9 3.4 collective-permute-done.62
  387.3 2.1 copy.74
  389.4 1.8 broadcast_select_fusion.1
  391.2 1.8 broadcast_select_fusion.4
  393.0 2.4 maximum_convert_fusion
  395.5 2.4 maximum_convert_fusion.1
  (399 shorter events, 93.0 us)
Async XLA Ops:
  4.6 20.8 %collective-permute-start = (bf16[384,1024]{1,0:T(8,128)(2,1)}, bf16[384,1024]{1,0:T(8,128)(2,1)}, u32[]{:S(2)}, u32[]{:S(2)}) collective-permute-start(bf16[384,1024]{1,0:T(8,128)(2,1)} %norm_one.1.refs_1_), channel_id=1, source_target_pairs={{0,2},{1,3},{2,0},{3,1},{4,6},{5,7},{6,4},{7,5},{8,10},{9,11},{10,... | collective-permute-start | bytes 2359304 | tf_op jit(solution)/shard_map/ppermute | solution.py:556
  7.6 4.1 %collective-permute-start.1 = (bf16[384,1024]{1,0:T(8,128)(2,1)}, bf16[384,1024]{1,0:T(8,128)(2,1)S(1)}, u32[]{:S(2)}, u32[]{:S(2)}) collective-permute-start(bf16[384,1024]{1,0:T(8,128)(2,1)} %norm_one.1.refs_1_), channel_id=1, source_target_pairs={{0,1},{1,0},{2,3},{3,2},{4,5},{5,4},{6,7},{7,6},{8,9},{9,8},{10,11... | collective-permute-start | bytes 2359304 | tf_op jit(solution)/shard_map/ppermute | solution.py:556
  25.4 2.5 collective-permute-start.2
  25.5 25.0 %collective-permute-start.5 = (bf16[384,1024]{1,0:T(8,128)(2,1)}, bf16[384,1024]{1,0:T(8,128)(2,1)}, u32[]{:S(2)}, u32[]{:S(2)}) collective-permute-start(bf16[384,1024]{1,0:T(8,128)(2,1)} %refs_0_.6), channel_id=1, source_target_pairs={{0,2},{1,3},{2,0},{3,1},{4,6},{5,7},{6,4},{7,5},{8,10},{9,11},{10,... | collective-permute-start | bytes 2359304 | tf_op jit(solution)/shard_map/ppermute | solution.py:556
  32.9 161.3 %copy-start.2 = (bf16[1536,256]{1,0:T(8,128)(2,1)}, bf16[1536,256]{1,0:T(8,128)(2,1)S(1)}, u32[]{:S(2)}) copy-start(bf16[1536,256]{1,0:T(8,128)(2,1)S(1)} %get-tuple-element.110.refs_3_.refs_4_) | copy-start | bytes 2359300
  32.9 17.5 %collective-permute-start.4 = (bf16[80,256]{1,0:T(8,128)(2,1)S(1)}, bf16[80,256]{1,0:T(8,128)(2,1)S(1)}, u32[]{:S(2)}, u32[]{:S(2)}) collective-permute-start(bf16[80,256]{1,0:T(8,128)(2,1)S(1)} %convert_element_type.249), channel_id=1, source_target_pairs={{0,8},{4,12},{8,16},{12,20},{16,24},{20,28},{1,9},{5,13},{9,17},{1... | collective-permute-start | bytes 122888 | tf_op jit(solution)/shard_map/ppermute | solution.py:649
  36.6 13.8 %collective-permute-start.3 = (bf16[80,256]{1,0:T(8,128)(2,1)S(1)}, bf16[80,256]{1,0:T(8,128)(2,1)S(1)}, u32[]{:S(2)}, u32[]{:S(2)}) collective-permute-start(bf16[80,256]{1,0:T(8,128)(2,1)S(1)} %convert_element_type.249), channel_id=1, source_target_pairs={{0,4},{4,8},{8,12},{12,16},{16,20},{20,24},{24,28},{1,5},{5,9},{9,... | collective-permute-start | bytes 122888 | tf_op jit(solution)/shard_map/ppermute | solution.py:649
  54.6 4.7 %collective-permute-start.7 = (bf16[384,1024]{1,0:T(8,128)(2,1)S(1)}, bf16[384,1024]{1,0:T(8,128)(2,1)S(1)}, u32[]{:S(2)}, u32[]{:S(2)}) collective-permute-start(bf16[384,1024]{1,0:T(8,128)(2,1)S(1)} %get-tuple-element.119), channel_id=1, source_target_pairs={{0,1},{1,0},{2,3},{3,2},{4,5},{5,4},{6,7},{7,6},{8,9},{9,8},{10,11... | collective-permute-start | bytes 2359304 | tf_op jit(solution)/shard_map/ppermute | solution.py:556
  58.7 2.4 collective-permute-start.6
  59.6 19.5 %collective-permute-start.8 = (bf16[384,1024]{1,0:T(8,128)(2,1)S(1)}, bf16[384,1024]{1,0:T(8,128)(2,1)S(1)}, u32[]{:S(2)}, u32[]{:S(2)}) collective-permute-start(bf16[384,1024]{1,0:T(8,128)(2,1)S(1)} %add_convert_fusion.5), channel_id=1, source_target_pairs={{0,2},{1,3},{2,0},{3,1},{4,6},{5,7},{6,4},{7,5},{8,10},{9,11},{10,... | collective-permute-start | bytes 2359304 | tf_op jit(solution)/shard_map/ppermute | solution.py:556
  61.1 21.8 %collective-permute-start.10 = (bf16[384,1024]{1,0:T(8,128)(2,1)}, bf16[384,1024]{1,0:T(8,128)(2,1)S(1)}, u32[]{:S(2)}, u32[]{:S(2)}) collective-permute-start(bf16[384,1024]{1,0:T(8,128)(2,1)} %refs_0_.6), channel_id=1, source_target_pairs={{0,1},{1,0},{2,3},{3,2},{4,5},{5,4},{6,7},{7,6},{8,9},{9,8},{10,11... | collective-permute-start | bytes 2359304 | tf_op jit(solution)/shard_map/ppermute | solution.py:556
  81.2 2.3 collective-permute-start.9
  81.2 20.1 %collective-permute-start.12 = (bf16[384,1024]{1,0:T(8,128)(2,1)S(1)}, bf16[384,1024]{1,0:T(8,128)(2,1)}, u32[]{:S(2)}, u32[]{:S(2)}) collective-permute-start(bf16[384,1024]{1,0:T(8,128)(2,1)S(1)} %get-tuple-element.121.refs_0_), channel_id=1, source_target_pairs={{0,2},{1,3},{2,0},{3,1},{4,6},{5,7},{6,4},{7,5},{8,10},{9,11},{10,... | collective-permute-start | bytes 2359304 | tf_op jit(solution)/shard_map/ppermute | solution.py:556
  82.7 19.1 %collective-permute-start.14 = (bf16[384,1024]{1,0:T(8,128)(2,1)}, bf16[384,1024]{1,0:T(8,128)(2,1)}, u32[]{:S(2)}, u32[]{:S(2)}) collective-permute-start(bf16[384,1024]{1,0:T(8,128)(2,1)} %collective-permute-done.5.refs_8_.refs_2_), channel_id=1, source_target_pairs={{0,1},{1,0},{2,3},{3,2},{4,5},{5,4},{6,7},{7,6},{8,9},{9,8},{10,11... | collective-permute-start | bytes 2359304 | tf_op jit(solution)/shard_map/ppermute | solution.py:556
  101.2 3.7 collective-permute-start.13
  101.3 46.6 %collective-permute-start.11 = (bf16[384,1024]{1,0:T(8,128)(2,1)}, bf16[384,1024]{1,0:T(8,128)(2,1)S(1)}, u32[]{:S(2)}, u32[]{:S(2)}) collective-permute-start(bf16[384,1024]{1,0:T(8,128)(2,1)} %copy-done.73), channel_id=1, source_target_pairs={{0,1},{1,0},{2,3},{3,2},{4,5},{5,4},{6,7},{7,6},{8,9},{9,8},{10,11... | collective-permute-start | bytes 2359304 | tf_op jit(solution)/shard_map/ppermute | solution.py:556
  101.8 46.1 %collective-permute-start.16 = (bf16[384,1024]{1,0:T(8,128)(2,1)}, bf16[384,1024]{1,0:T(8,128)(2,1)S(1)}, u32[]{:S(2)}, u32[]{:S(2)}) collective-permute-start(bf16[384,1024]{1,0:T(8,128)(2,1)} %copy-done.72), channel_id=1, source_target_pairs={{0,1},{1,0},{2,3},{3,2},{4,5},{5,4},{6,7},{7,6},{8,9},{9,8},{10,11... | collective-permute-start | bytes 2359304 | tf_op jit(solution)/shard_map/ppermute | solution.py:556
  118.2 13.4 %collective-permute-start.15 = (bf16[384,1024]{1,0:T(8,128)(2,1)S(1)}, bf16[384,1024]{1,0:T(8,128)(2,1)S(1)}, u32[]{:S(2)}, u32[]{:S(2)}) collective-permute-start(bf16[384,1024]{1,0:T(8,128)(2,1)S(1)} %get-tuple-element.128), channel_id=1, source_target_pairs={{0,1},{1,0},{2,3},{3,2},{4,5},{5,4},{6,7},{7,6},{8,9},{9,8},{10,11... | collective-permute-start | bytes 2359304 | tf_op jit(solution)/shard_map/ppermute | solution.py:556
  118.4 5.7 %collective-permute-start.17 = (bf16[384,1024]{1,0:T(8,128)(2,1)S(1)}, bf16[384,1024]{1,0:T(8,128)(2,1)S(1)}, u32[]{:S(2)}, u32[]{:S(2)}) collective-permute-start(bf16[384,1024]{1,0:T(8,128)(2,1)S(1)} %get-tuple-element.132), channel_id=1, source_target_pairs={{0,1},{1,0},{2,3},{3,2},{4,5},{5,4},{6,7},{7,6},{8,9},{9,8},{10,11... | collective-permute-start | bytes 2359304 | tf_op jit(solution)/shard_map/ppermute | solution.py:556
  124.5 19.6 %collective-permute-start.18 = (bf16[384,1024]{1,0:T(8,128)(2,1)S(1)}, bf16[384,1024]{1,0:T(8,128)(2,1)S(1)}, u32[]{:S(2)}, u32[]{:S(2)}) collective-permute-start(bf16[384,1024]{1,0:T(8,128)(2,1)S(1)} %add_convert_fusion.3), channel_id=1, source_target_pairs={{0,2},{1,3},{2,0},{3,1},{4,6},{5,7},{6,4},{7,5},{8,10},{9,11},{10,... | collective-permute-start | bytes 2359304 | tf_op jit(solution)/shard_map/ppermute | solution.py:556
  145.2 34.5 %collective-permute-start.23 = (bf16[512,1024]{1,0:T(8,128)(2,1)}, bf16[512,1024]{1,0:T(8,128)(2,1)}, u32[]{:S(2)}, u32[]{:S(2)}) collective-permute-start(bf16[512,1024]{1,0:T(8,128)(2,1)} %broadcast_select_fusion.5.refs_6_), channel_id=1, source_target_pairs={{0,4},{4,0},{8,12},{12,8},{16,20},{20,16},{24,28},{28,24},{1,5},{5... | collective-permute-start | bytes 3145736 | tf_op jit(solution)/shard_map/ppermute | solution.py:556
  152.8 18.8 %collective-permute-start.19 = (bf16[384,1024]{1,0:T(8,128)(2,1)}, bf16[384,1024]{1,0:T(8,128)(2,1)}, u32[]{:S(2)}, u32[]{:S(2)}) collective-permute-start(bf16[384,1024]{1,0:T(8,128)(2,1)} %get-tuple-element.138.refs_1_), channel_id=1, source_target_pairs={{0,2},{1,3},{2,0},{3,1},{4,6},{5,7},{6,4},{7,5},{8,10},{9,11},{10,... | collective-permute-start | bytes 2359304 | tf_op jit(solution)/shard_map/ppermute | solution.py:556
  154.3 18.8 %collective-permute-start.21 = (bf16[384,1024]{1,0:T(8,128)(2,1)}, bf16[384,1024]{1,0:T(8,128)(2,1)}, u32[]{:S(2)}, u32[]{:S(2)}) collective-permute-start(bf16[384,1024]{1,0:T(8,128)(2,1)} %get-tuple-element.138.refs_1_), channel_id=1, source_target_pairs={{0,1},{1,0},{2,3},{3,2},{4,5},{5,4},{6,7},{7,6},{8,9},{9,8},{10,11... | collective-permute-start | bytes 2359304 | tf_op jit(solution)/shard_map/ppermute | solution.py:556
  154.3 27.4 %collective-permute-start.24 = (bf16[512,1024]{1,0:T(8,128)(2,1)}, bf16[512,1024]{1,0:T(8,128)(2,1)}, u32[]{:S(2)}, u32[]{:S(2)}) collective-permute-start(bf16[512,1024]{1,0:T(8,128)(2,1)} %broadcast_select_fusion.2.refs_7_), channel_id=1, source_target_pairs={{0,8},{4,12},{8,0},{12,4},{16,24},{20,28},{24,16},{28,20},{1,9},{5... | collective-permute-start | bytes 3145736 | tf_op jit(solution)/shard_map/ppermute | solution.py:556
  171.5 45.7 %collective-permute-start.20 = (bf16[384,1024]{1,0:T(8,128)(2,1)}, bf16[384,1024]{1,0:T(8,128)(2,1)S(1)}, u32[]{:S(2)}, u32[]{:S(2)}) collective-permute-start(bf16[384,1024]{1,0:T(8,128)(2,1)} %copy-done.31), channel_id=1, source_target_pairs={{0,2},{1,3},{2,0},{3,1},{4,6},{5,7},{6,4},{7,5},{8,10},{9,11},{10,... | collective-permute-start | bytes 2359304 | tf_op jit(solution)/shard_map/ppermute | solution.py:556
  179.6 6.3 %collective-permute-start.22 = (bf16[384,1024]{1,0:T(8,128)(2,1)}, bf16[384,1024]{1,0:T(8,128)(2,1)S(1)}, u32[]{:S(2)}, u32[]{:S(2)}) collective-permute-start(bf16[384,1024]{1,0:T(8,128)(2,1)} %collective-permute-done.19.refs_1_), channel_id=1, source_target_pairs={{0,1},{1,0},{2,3},{3,2},{4,5},{5,4},{6,7},{7,6},{8,9},{9,8},{10,11... | collective-permute-start | bytes 2359304 | tf_op jit(solution)/shard_map/ppermute | solution.py:556
  181.8 26.3 %collective-permute-start.27 = (bf16[256,1024]{1,0:T(8,128)(2,1)S(1)}, bf16[256,1024]{1,0:T(8,128)(2,1)S(1)}, u32[]{:S(2)}, u32[]{:S(2)}) collective-permute-start(bf16[256,1024]{1,0:T(8,128)(2,1)S(1)} %broadcast_select_fusion.11.refs_11_), channel_id=1, source_target_pairs={{0,8},{4,12},{8,0},{12,4},{16,24},{20,28},{24,16},{28,20},{1,9},{5... | collective-permute-start | bytes 1572872 | tf_op jit(solution)/shard_map/ppermute | solution.py:556
  185.4 27.0 %collective-permute-start.28 = (bf16[256,1024]{1,0:T(8,128)(2,1)S(1)}, bf16[256,1024]{1,0:T(8,128)(2,1)S(1)}, u32[]{:S(2)}, u32[]{:S(2)}) collective-permute-start(bf16[256,1024]{1,0:T(8,128)(2,1)S(1)} %broadcast_select_fusion.8.refs_12_), channel_id=1, source_target_pairs={{0,16},{4,20},{8,24},{12,28},{16,0},{20,4},{24,8},{28,12},{1,17},{... | collective-permute-start | bytes 1572872 | tf_op jit(solution)/shard_map/ppermute | solution.py:556
  188.9 34.3 %collective-permute-start.26 = (bf16[80,256]{1,0:T(8,128)(2,1)S(1)}, bf16[80,256]{1,0:T(8,128)(2,1)S(1)}, u32[]{:S(2)}, u32[]{:S(2)}) collective-permute-start(bf16[80,256]{1,0:T(8,128)(2,1)S(1)} %convert_element_type.270), channel_id=1, source_target_pairs={{8,0},{12,4},{16,8},{20,12},{24,16},{28,20},{9,1},{13,5},{17,9},{2... | collective-permute-start | bytes 122888 | tf_op jit(solution)/shard_map/ppermute | solution.py:649
  190.2 33.0 %collective-permute-start.25 = (bf16[80,256]{1,0:T(8,128)(2,1)S(1)}, bf16[80,256]{1,0:T(8,128)(2,1)S(1)}, u32[]{:S(2)}, u32[]{:S(2)}) collective-permute-start(bf16[80,256]{1,0:T(8,128)(2,1)S(1)} %convert_element_type.270), channel_id=1, source_target_pairs={{4,0},{8,4},{12,8},{16,12},{20,16},{24,20},{28,24},{5,1},{9,5},{13... | collective-permute-start | bytes 122888 | tf_op jit(solution)/shard_map/ppermute | solution.py:649
  213.6 28.3 %collective-permute-start.32 = (bf16[128,1024]{1,0:T(8,128)(2,1)}, bf16[128,1024]{1,0:T(8,128)(2,1)}, u32[]{:S(2)}, u32[]{:S(2)}) collective-permute-start(bf16[128,1024]{1,0:T(8,128)(2,1)} %broadcast_select_fusion.26.refs_10_), channel_id=1, source_target_pairs={{0,16},{4,20},{8,24},{12,28},{16,0},{20,4},{24,8},{28,12},{1,17},{... | collective-permute-start | bytes 786440 | tf_op jit(solution)/shard_map/ppermute | solution.py:556
  216.0 27.8 %collective-permute-start.33 = (bf16[128,1024]{1,0:T(8,128)(2,1)}, bf16[128,1024]{1,0:T(8,128)(2,1)}, u32[]{:S(2)}, u32[]{:S(2)}) collective-permute-start(bf16[128,1024]{1,0:T(8,128)(2,1)} %broadcast_select_fusion.23.refs_11_), channel_id=1, source_target_pairs={{0,4},{4,0},{8,12},{12,8},{16,20},{20,16},{24,28},{28,24},{1,5},{5... | collective-permute-start | bytes 786440 | tf_op jit(solution)/shard_map/ppermute | solution.py:556
  217.2 27.7 %collective-permute-start.34 = (bf16[128,1024]{1,0:T(8,128)(2,1)S(1)}, bf16[128,1024]{1,0:T(8,128)(2,1)}, u32[]{:S(2)}, u32[]{:S(2)}) collective-permute-start(bf16[128,1024]{1,0:T(8,128)(2,1)S(1)} %broadcast_select_fusion.20.refs_12_), channel_id=1, source_target_pairs={{0,8},{4,12},{8,0},{12,4},{16,24},{20,28},{24,16},{28,20},{1,9},{5... | collective-permute-start | bytes 786440 | tf_op jit(solution)/shard_map/ppermute | solution.py:556
  236.2 14.7 %collective-permute-start.30 = (bf16[384,1024]{1,0:T(8,128)(2,1)S(1)}, bf16[384,1024]{1,0:T(8,128)(2,1)S(1)}, u32[]{:S(2)}, u32[]{:S(2)}) collective-permute-start(bf16[384,1024]{1,0:T(8,128)(2,1)S(1)} %get-tuple-element.166), channel_id=1, source_target_pairs={{0,1},{1,0},{2,3},{3,2},{4,5},{5,4},{6,7},{7,6},{8,9},{9,8},{10,11... | collective-permute-start | bytes 2359304 | tf_op jit(solution)/shard_map/ppermute | solution.py:556
  246.0 24.2 %collective-permute-start.37 = (bf16[128,1024]{1,0:T(8,128)(2,1)S(1)}, bf16[128,1024]{1,0:T(8,128)(2,1)S(1)}, u32[]{:S(2)}, u32[]{:S(2)}) collective-permute-start(bf16[128,1024]{1,0:T(8,128)(2,1)S(1)} %add_convert_fusion.12), channel_id=1, source_target_pairs={{0,16},{4,20},{8,24},{12,28},{16,0},{20,4},{24,8},{28,12},{1,17},{... | collective-permute-start | bytes 786440 | tf_op jit(solution)/shard_map/ppermute | solution.py:556
  246.5 23.8 %collective-permute-start.39 = (bf16[128,1024]{1,0:T(8,128)(2,1)S(1)}, bf16[128,1024]{1,0:T(8,128)(2,1)S(1)}, u32[]{:S(2)}, u32[]{:S(2)}) collective-permute-start(bf16[128,1024]{1,0:T(8,128)(2,1)S(1)} %add_convert_fusion.11), channel_id=1, source_target_pairs={{0,4},{4,0},{8,12},{12,8},{16,20},{20,16},{24,28},{28,24},{1,5},{5... | collective-permute-start | bytes 786440 | tf_op jit(solution)/shard_map/ppermute | solution.py:556
  247.7 22.7 %collective-permute-start.40 = (bf16[64,1024]{1,0:T(8,128)(2,1)S(1)}, bf16[64,1024]{1,0:T(8,128)(2,1)S(1)}, u32[]{:S(2)}, u32[]{:S(2)}) collective-permute-start(bf16[64,1024]{1,0:T(8,128)(2,1)S(1)} %broadcast_select_fusion.35), channel_id=1, source_target_pairs={{0,16},{4,20},{8,24},{12,28},{16,0},{20,4},{24,8},{28,12},{1,17},{... | collective-permute-start | bytes 393224 | tf_op jit(solution)/shard_map/ppermute | solution.py:556
  250.6 18.8 %collective-permute-start.38 = (bf16[192,1024]{1,0:T(8,128)(2,1)S(1)}, bf16[192,1024]{1,0:T(8,128)(2,1)S(1)}, u32[]{:S(2)}, u32[]{:S(2)}) collective-permute-start(bf16[192,1024]{1,0:T(8,128)(2,1)S(1)} %broadcast_select_fusion.14), channel_id=1, source_target_pairs={{0,8},{4,12},{8,0},{12,4},{16,24},{20,28},{24,16},{28,20},{1,9},{5... | collective-permute-start | bytes 1179656 | tf_op jit(solution)/shard_map/ppermute | solution.py:556
  250.9 18.8 %collective-permute-start.35 = (bf16[192,1024]{1,0:T(8,128)(2,1)S(1)}, bf16[192,1024]{1,0:T(8,128)(2,1)S(1)}, u32[]{:S(2)}, u32[]{:S(2)}) collective-permute-start(bf16[192,1024]{1,0:T(8,128)(2,1)S(1)} %broadcast_select_fusion.17), channel_id=1, source_target_pairs={{0,4},{4,0},{8,12},{12,8},{16,20},{20,16},{24,28},{28,24},{1,5},{5... | collective-permute-start | bytes 1179656 | tf_op jit(solution)/shard_map/ppermute | solution.py:556
  269.6 9.8 %collective-permute-start.45 = (bf16[96,1024]{1,0:T(8,128)(2,1)S(1)}, bf16[96,1024]{1,0:T(8,128)(2,1)S(1)}, u32[]{:S(2)}, u32[]{:S(2)}) collective-permute-start(bf16[96,1024]{1,0:T(8,128)(2,1)S(1)} %broadcast_select_fusion.29), channel_id=1, source_target_pairs={{0,16},{4,20},{8,24},{12,28},{16,0},{20,4},{24,8},{28,12},{1,17},{... | collective-permute-start | bytes 589832 | tf_op jit(solution)/shard_map/ppermute | solution.py:556
  270.0 9.8 %collective-permute-start.36 = (bf16[96,1024]{1,0:T(8,128)(2,1)S(1)}, bf16[96,1024]{1,0:T(8,128)(2,1)S(1)}, u32[]{:S(2)}, u32[]{:S(2)}) collective-permute-start(bf16[96,1024]{1,0:T(8,128)(2,1)S(1)} %broadcast_select_fusion.32), channel_id=1, source_target_pairs={{0,8},{4,12},{8,0},{12,4},{16,24},{20,28},{24,16},{28,20},{1,9},{5... | collective-permute-start | bytes 589832 | tf_op jit(solution)/shard_map/ppermute | solution.py:556
  270.5 9.4 %collective-permute-start.50 = (bf16[32,1024]{1,0:T(8,128)(2,1)S(1)}, bf16[32,1024]{1,0:T(8,128)(2,1)S(1)}, u32[]{:S(2)}, u32[]{:S(2)}) collective-permute-start(bf16[32,1024]{1,0:T(8,128)(2,1)S(1)} %broadcast_select_fusion.44), channel_id=1, source_target_pairs={{0,4},{4,0},{8,12},{12,8},{16,20},{20,16},{24,28},{28,24},{1,5},{5... | collective-permute-start | bytes 196616 | tf_op jit(solution)/shard_map/ppermute | solution.py:556
  280.0 4.3 %collective-permute-start.51 = (bf16[32,1024]{1,0:T(8,128)(2,1)S(1)}, bf16[32,1024]{1,0:T(8,128)(2,1)S(1)}, u32[]{:S(2)}, u32[]{:S(2)}) collective-permute-start(bf16[32,1024]{1,0:T(8,128)(2,1)S(1)} %add_convert_fusion.18), channel_id=1, source_target_pairs={{0,4},{4,0},{8,12},{12,8},{16,20},{20,16},{24,28},{28,24},{1,5},{5... | collective-permute-start | bytes 196616 | tf_op jit(solution)/shard_map/ppermute | solution.py:556
  281.2 60.3 %collective-permute-start.29 = (bf16[384,1024]{1,0:T(8,128)(2,1)S(1)}, bf16[384,1024]{1,0:T(8,128)(2,1)S(1)}, u32[]{:S(2)}, u32[]{:S(2)}) collective-permute-start(bf16[384,1024]{1,0:T(8,128)(2,1)S(1)} %copy-done.71), channel_id=1, source_target_pairs={{0,1},{1,0},{2,3},{3,2},{4,5},{5,4},{6,7},{7,6},{8,9},{9,8},{10,11... | collective-permute-start | bytes 2359304 | tf_op jit(solution)/shard_map/ppermute | solution.py:556
  281.2 60.4 %collective-permute-start.31 = (bf16[384,1024]{1,0:T(8,128)(2,1)}, bf16[384,1024]{1,0:T(8,128)(2,1)S(1)}, u32[]{:S(2)}, u32[]{:S(2)}) collective-permute-start(bf16[384,1024]{1,0:T(8,128)(2,1)} %add_convert_fusion.2), channel_id=1, source_target_pairs={{0,2},{1,3},{2,0},{3,1},{4,6},{5,7},{6,4},{7,5},{8,10},{9,11},{10,... | collective-permute-start | bytes 2359304 | tf_op jit(solution)/shard_map/ppermute | solution.py:556
  281.8 48.5 %collective-permute-start.54 = (bf16[256,1024]{1,0:T(8,128)(2,1)}, bf16[256,1024]{1,0:T(8,128)(2,1)S(1)}, u32[]{:S(2)}, u32[]{:S(2)}) collective-permute-start(bf16[256,1024]{1,0:T(8,128)(2,1)} %get-tuple-element.246), channel_id=1, source_target_pairs={{0,16},{4,20},{8,24},{12,28},{16,0},{20,4},{24,8},{28,12},{1,17},{... | collective-permute-start | bytes 1572872 | tf_op jit(solution)/shard_map/ppermute | solution.py:556
  282.0 50.9 %collective-permute-start.56 = (bf16[256,1024]{1,0:T(8,128)(2,1)}, bf16[256,1024]{1,0:T(8,128)(2,1)S(1)}, u32[]{:S(2)}, u32[]{:S(2)}) collective-permute-start(bf16[256,1024]{1,0:T(8,128)(2,1)} %get-tuple-element.245), channel_id=1, source_target_pairs={{0,8},{4,12},{8,0},{12,4},{16,24},{20,28},{24,16},{28,20},{1,9},{5... | collective-permute-start | bytes 1572872 | tf_op jit(solution)/shard_map/ppermute | solution.py:556
  284.3 4.6 %collective-permute-start.46 = (bf16[48,1024]{1,0:T(8,128)(2,1)S(1)}, bf16[48,1024]{1,0:T(8,128)(2,1)S(1)}, u32[]{:S(2)}, u32[]{:S(2)}) collective-permute-start(bf16[48,1024]{1,0:T(8,128)(2,1)S(1)} %broadcast_select_fusion.38), channel_id=1, source_target_pairs={{0,4},{4,0},{8,12},{12,8},{16,20},{20,16},{24,28},{28,24},{1,5},{5... | collective-permute-start | bytes 294920 | tf_op jit(solution)/shard_map/ppermute | solution.py:556
  288.9 22.9 %collective-permute-start.41 = (bf16[48,1024]{1,0:T(8,128)(2,1)S(1)}, bf16[48,1024]{1,0:T(8,128)(2,1)S(1)}, u32[]{:S(2)}, u32[]{:S(2)}) collective-permute-start(bf16[48,1024]{1,0:T(8,128)(2,1)S(1)} %broadcast_select_fusion.41), channel_id=1, source_target_pairs={{0,16},{4,20},{8,24},{12,28},{16,0},{20,4},{24,8},{28,12},{1,17},{... | collective-permute-start | bytes 294920 | tf_op jit(solution)/shard_map/ppermute | solution.py:556
  311.8 4.7 %collective-permute-start.47 = (bf16[48,1024]{1,0:T(8,128)(2,1)S(1)}, bf16[48,1024]{1,0:T(8,128)(2,1)S(1)}, u32[]{:S(2)}, u32[]{:S(2)}) collective-permute-start(bf16[48,1024]{1,0:T(8,128)(2,1)S(1)} %add_convert_fusion.16), channel_id=1, source_target_pairs={{0,4},{4,0},{8,12},{12,8},{16,20},{20,16},{24,28},{28,24},{1,5},{5... | collective-permute-start | bytes 294920 | tf_op jit(solution)/shard_map/ppermute | solution.py:556
  316.5 5.8 %collective-permute-start.42 = (bf16[48,1024]{1,0:T(8,128)(2,1)S(1)}, bf16[48,1024]{1,0:T(8,128)(2,1)S(1)}, u32[]{:S(2)}, u32[]{:S(2)}) collective-permute-start(bf16[48,1024]{1,0:T(8,128)(2,1)S(1)} %add_convert_fusion.17), channel_id=1, source_target_pairs={{0,16},{4,20},{8,24},{12,28},{16,0},{20,4},{24,8},{28,12},{1,17},{... | collective-permute-start | bytes 294920 | tf_op jit(solution)/shard_map/ppermute | solution.py:556
  322.4 7.8 %collective-permute-start.52 = (bf16[64,1024]{1,0:T(8,128)(2,1)S(1)}, bf16[64,1024]{1,0:T(8,128)(2,1)S(1)}, u32[]{:S(2)}, u32[]{:S(2)}) collective-permute-start(bf16[64,1024]{1,0:T(8,128)(2,1)S(1)} %pad_maximum_fusion.10), channel_id=1, source_target_pairs={{0,16},{4,20},{8,24},{12,28},{16,0},{20,4},{24,8},{28,12},{1,17},{... | collective-permute-start | bytes 393224 | tf_op jit(solution)/shard_map/ppermute | solution.py:556
  330.2 11.2 %collective-permute-start.48 = (bf16[96,1024]{1,0:T(8,128)(2,1)S(1)}, bf16[96,1024]{1,0:T(8,128)(2,1)S(1)}, u32[]{:S(2)}, u32[]{:S(2)}) collective-permute-start(bf16[96,1024]{1,0:T(8,128)(2,1)S(1)} %pad_maximum_fusion.9), channel_id=1, source_target_pairs={{0,16},{4,20},{8,24},{12,28},{16,0},{20,4},{24,8},{28,12},{1,17},{... | collective-permute-start | bytes 589832 | tf_op jit(solution)/shard_map/ppermute | solution.py:556
  330.3 17.2 %collective-permute-start.43 = (bf16[96,1024]{1,0:T(8,128)(2,1)S(1)}, bf16[96,1024]{1,0:T(8,128)(2,1)S(1)}, u32[]{:S(2)}, u32[]{:S(2)}) collective-permute-start(bf16[96,1024]{1,0:T(8,128)(2,1)S(1)} %pad_maximum_fusion.8), channel_id=1, source_target_pairs={{0,8},{4,12},{8,0},{12,4},{16,24},{20,28},{24,16},{28,20},{1,9},{5... | collective-permute-start | bytes 589832 | tf_op jit(solution)/shard_map/ppermute | solution.py:556
  333.0 21.2 %collective-permute-start.53 = (bf16[128,1024]{1,0:T(8,128)(2,1)S(1)}, bf16[128,1024]{1,0:T(8,128)(2,1)S(1)}, u32[]{:S(2)}, u32[]{:S(2)}) collective-permute-start(bf16[128,1024]{1,0:T(8,128)(2,1)S(1)} %pad_maximum_fusion.7), channel_id=1, source_target_pairs={{0,8},{4,12},{8,0},{12,4},{16,24},{20,28},{24,16},{28,20},{1,9},{5... | collective-permute-start | bytes 786440 | tf_op jit(solution)/shard_map/ppermute | solution.py:556
  341.4 48.0 %collective-permute-start.55 = (bf16[512,1024]{1,0:T(8,128)(2,1)}, bf16[512,1024]{1,0:T(8,128)(2,1)}, u32[]{:S(2)}, u32[]{:S(2)}) collective-permute-start(bf16[512,1024]{1,0:T(8,128)(2,1)} %pad_maximum_fusion.1), channel_id=1, source_target_pairs={{0,8},{4,12},{8,0},{12,4},{16,24},{20,28},{24,16},{28,20},{1,9},{5... | collective-permute-start | bytes 3145736 | tf_op jit(solution)/shard_map/ppermute | solution.py:556
  341.5 49.7 %collective-permute-start.57 = (bf16[512,1024]{1,0:T(8,128)(2,1)}, bf16[512,1024]{1,0:T(8,128)(2,1)}, u32[]{:S(2)}, u32[]{:S(2)}) collective-permute-start(bf16[512,1024]{1,0:T(8,128)(2,1)} %pad_maximum_fusion.2), channel_id=1, source_target_pairs={{0,4},{4,0},{8,12},{12,8},{16,20},{20,16},{24,28},{28,24},{1,5},{5... | collective-permute-start | bytes 3145736 | tf_op jit(solution)/shard_map/ppermute | solution.py:556
  344.2 1.3 collective-permute-start.58
  345.5 39.2 %collective-permute-start.49 = (bf16[192,1024]{1,0:T(8,128)(2,1)S(1)}, bf16[192,1024]{1,0:T(8,128)(2,1)}, u32[]{:S(2)}, u32[]{:S(2)}) collective-permute-start(bf16[192,1024]{1,0:T(8,128)(2,1)S(1)} %pad_maximum_fusion.6), channel_id=1, source_target_pairs={{0,8},{4,12},{8,0},{12,4},{16,24},{20,28},{24,16},{28,20},{1,9},{5... | collective-permute-start | bytes 1179656 | tf_op jit(solution)/shard_map/ppermute | solution.py:556
  347.5 3.8 collective-permute-start.59
  351.4 16.9 %collective-permute-start.60 = (f32[4224]{0:T(1024)S(1)}, f32[4224]{0:T(1024)S(1)}, u32[]{:S(2)}, u32[]{:S(2)}) collective-permute-start(f32[4224]{0:T(1024)S(1)} %add.244), channel_id=1, source_target_pairs={{0,4},{4,0},{8,12},{12,8},{16,20},{20,16},{24,28},{28,24},{1,5},{5... | collective-permute-start | bytes 50696 | tf_op jit(solution)/shard_map/ppermute | solution.py:556
  354.1 31.8 %collective-permute-start.44 = (bf16[192,1024]{1,0:T(8,128)(2,1)}, bf16[192,1024]{1,0:T(8,128)(2,1)}, u32[]{:S(2)}, u32[]{:S(2)}) collective-permute-start(bf16[192,1024]{1,0:T(8,128)(2,1)} %pad_maximum_fusion.5), channel_id=1, source_target_pairs={{0,4},{4,0},{8,12},{12,8},{16,20},{20,16},{24,28},{28,24},{1,5},{5... | collective-permute-start | bytes 1179656 | tf_op jit(solution)/shard_map/ppermute | solution.py:556
  368.2 10.4 %collective-permute-start.61 = (f32[4224]{0:T(1024)S(1)}, f32[4224]{0:T(1024)S(1)}, u32[]{:S(2)}, u32[]{:S(2)}) collective-permute-start(f32[4224]{0:T(1024)S(1)} %add.245), channel_id=1, source_target_pairs={{0,8},{4,12},{8,0},{12,4},{16,24},{20,28},{24,16},{28,20},{1,9},{5... | collective-permute-start | bytes 50696 | tf_op jit(solution)/shard_map/ppermute | solution.py:556
  378.7 4.7 %collective-permute-start.62 = (f32[4224]{0:T(1024)S(1)}, f32[4224]{0:T(1024)S(1)}, u32[]{:S(2)}, u32[]{:S(2)}) collective-permute-start(f32[4224]{0:T(1024)S(1)} %add.246), channel_id=1, source_target_pairs={{0,16},{4,20},{8,24},{12,28},{16,0},{20,4},{24,8},{28,12},{1,17},{... | collective-permute-start | bytes 50696 | tf_op jit(solution)/shard_map/ppermute | solution.py:556
  (98 other events, 694.5 us)
where the time goes:
time: 405 us; the launch traced here: 398 us
  waiting for transfers between devices  161 us (40%)
  Pallas kernels  71.2 us (18%)
  starting transfers between devices  57.4 us (14%)
  local copies, waits for them, and re-layouts  48.7 us (12%)
  other arithmetic  35.1 us (9%)
  matrix products  17.6 us (4%)
  between operations  7.58 us (2%)
    ppermute x59, waiting for transfers between devices, swap(): lax.ppermute(value, axis, [(i, i ^ bit) for i in range(lax.axis_size(axis...  161 us
    pallas_call x17, Pallas kernels, kernel(): return lambda *args: call(*args, *tokens)  71.2 us
    ppermute x59, starting transfers between devices, swap(): lax.ppermute(value, axis, [(i, i ^ bit) for i in range(lax.axis_size(axis...  47.8 us
    unnamed x201, local copies, waits for them, and re-layouts  40.2 us
    dot_general x4, matrix products, tn(): lax.dot_general(a, b, (((0,), (0,)), ((), ())), preferred_element_type=F32)  17.3 us
    ppermute x4, starting transfers between devices, shifted(): return lax.ppermute(pack, 'rows', pairs)  9.69 us
    convert_element_type x15, other arithmetic, next(): self.value = (self.kept.astype(F32) + got.astype(F32)).astype(BF)  8.33 us
  transfers between devices with their start and end apart: 63, of which 24 were waited for; matrix products, arithmetic and copies ran while one was open for 14% of the time, Pallas kernels for 17%

commit v1 on v0

--- a/solution.py
+++ b/solution.py
@@ -129,7 +129,7 @@
 
 
 def norm_one(x, gain, bias):
-    call = kernel(norm_body, "norm_one", shape(x.shape[0], D, BF), [vmem()] * 3, 8)
+    call = kernel(norm_body, "norm_one", shape(x.shape[0], D, BF), [vmem()] * 3, 4)
     return call(x, gain, bias)
 
 
@@ -147,7 +147,7 @@
     for at in tiles(x_ref.shape[0]):
         attended = total(parts, at)
         middle = x_ref[at, :].astype(F32) + attended
-        middle_ref[at, :] = middle
+        middle_ref[at, :] = middle.astype(BF)
         xhat, _ = normal(middle)
         out_ref[at, :] = (xhat * gain_ref[...] + bias_ref[...]).astype(BF)
         square_ref[at, :] = jnp.sum(attended * attended, axis=-1, keepdims=True)
@@ -156,24 +156,23 @@
 def norm_two(x, gain, bias, parts):
     rows = x.shape[0]
     call = kernel(
-        middle_body, "norm_two", (shape(rows, D, F32), shape(rows, D, BF), shape(rows, 1, F32)),
-        [vmem()] * (3 + len(parts)), 12,
+        middle_body, "norm_two", (shape(rows, D, BF), shape(rows, D, BF), shape(rows, 1, F32)),
+        [vmem()] * (3 + len(parts)), 4,
     )
     return call(x, gain, bias, *parts)
 
 
 def middle_back_body(*refs):
     grad_ref, middle_ref, gain_ref = refs[:3]
-    parts = refs[3:-4]
-    wide_ref, low_ref, gain_grad_ref, bias_grad_ref = refs[-4:]
+    parts = refs[3:-3]
+    low_ref, gain_grad_ref, bias_grad_ref = refs[-3:]
     gain_grad = bias_grad = jnp.zeros(gain_ref.shape, F32)
     for at in tiles(grad_ref.shape[0]):
         grad = total(parts, at)
-        xhat, scale = normal(middle_ref[at, :])
+        xhat, scale = normal(middle_ref[at, :].astype(F32))
         gain_grad = gain_grad + jnp.sum(grad * xhat, axis=0, keepdims=True)
         bias_grad = bias_grad + jnp.sum(grad, axis=0, keepdims=True)
         out = grad_ref[at, :].astype(F32) + normal_back(grad, gain_ref[...], xhat, scale)
-        wide_ref[at, :] = out
         low_ref[at, :] = out.astype(BF)
     gain_grad_ref[...] = gain_grad
     bias_grad_ref[...] = bias_grad
@@ -183,8 +182,8 @@
     rows = grad.shape[0]
     call = kernel(
         middle_back_body, "norm_two_back",
-        (shape(rows, D, F32), shape(rows, D, BF), shape(1, D, F32), shape(1, D, F32)),
-        [vmem()] * (3 + len(parts)), 16, tokens=tokens,
+        (shape(rows, D, BF), shape(1, D, F32), shape(1, D, F32)),
+        [vmem()] * (3 + len(parts)), 9, tokens=tokens,
     )
     return call(grad, middle, gain, *parts)
 
@@ -199,7 +198,7 @@
         xhat, scale = normal(x_ref[at, :].astype(F32))
         gain_grad = gain_grad + jnp.sum(grad * xhat, axis=0, keepdims=True)
         bias_grad = bias_grad + jnp.sum(grad, axis=0, keepdims=True)
-        out_ref[at, :] = (wide_ref[at, :] + normal_back(grad, gain_ref[...], xhat, scale)).astype(BF)
+        out_ref[at, :] = (wide_ref[at, :].astype(F32) + normal_back(grad, gain_ref[...], xhat, scale)).astype(BF)
     gain_grad_ref[...] = gain_grad
     bias_grad_ref[...] = bias_grad
 
@@ -208,7 +207,7 @@
     rows = x.shape[0]
     call = kernel(
         pixels_back_body, "norm_one_back", (shape(rows, D, BF), shape(1, D, F32), shape(1, D, F32)),
-        [vmem()] * (3 + len(parts)), 16,
+        [vmem()] * (3 + len(parts)), 9,
     )
     return call(x, wide, gain, *parts)
 
@@ -219,7 +218,7 @@
     out_ref, result_square_ref, branch_square_ref = refs[-3:]
     for at in tiles(middle_ref.shape[0]):
         branch = total(parts, at)
-        result = middle_ref[at, :] + branch
+        result = middle_ref[at, :].astype(F32) + branch
         out_ref[at, :] = result.astype(BF)
         result_square_ref[at, :] = jnp.sum(result * result, axis=-1, keepdims=True)
         branch_square_ref[at, :] = jnp.sum(branch * branch, axis=-1, keepdims=True)
@@ -229,9 +228,13 @@
     rows = middle.shape[0]
     call = kernel(
         result_body, "finish", (shape(rows, D, BF), shape(rows, 1, F32), shape(rows, 1, F32)),
-        [vmem()] * (1 + len(parts)), 12, tokens=tokens,
+        [vmem()] * (1 + len(parts)), 4, tokens=tokens,
     )
     return call(middle, *parts)
+
+
+def decode(code):
+    return code >> 1, (code & 1).astype(F32)
 
 
 def pair_slices(pair, rows):
@@ -239,7 +242,7 @@
         yield i, slice(i * rows, (i + 1) * rows), slice((2 * pair + i) * rows, (2 * pair + i + 1) * rows)
 
 
-def qkv_body(pair, tail_ref, xa_ref, xb_ref, w_ref, valid_ref, seg_ref, was_ref, *rest):
+def qkv_body(pair, tail_ref, xa_ref, xb_ref, w_ref, code_ref, was_ref, *rest):
     q_ref, k_ref, v_ref, pack_ref = rest[-4:]
     width = q_ref.shape[1]
     block = same_head(width)
@@ -247,26 +250,27 @@
     for i, _, at in pair_slices(pair, xa_ref.shape[0]):
         x = (xa_ref, xb_ref)[i][...]
         q_ref[at, :] = feature(nn(x, w_ref[0])).astype(BF)
-        k = (feature(nn(x, w_ref[1])) * valid_ref[at, :]).astype(BF)
+        segment, valid = decode(code_ref[at, :])
+        k = (feature(nn(x, w_ref[1])) * valid).astype(BF)
         v = nn(x, w_ref[2]).astype(BF)
         k_ref[at, :] = k
         v_ref[at, :] = v
-        kept = pick(seg_ref[at, :] == tail_ref[0], k)
+        kept = pick(segment == tail_ref[0], k)
         state = state + fold_heads(pick(block, tn(kept, v)), width)
         sums = sums + jnp.sum(kept.astype(F32), axis=0, keepdims=True)
     pack_ref[0:HEAD, :] = state
     pack_ref[HEAD:PACK, :] = sums
 
 
-def project_qkv(pair, tail, xa, xb, w, valid, seg, was, made):
-    width, whole = w.shape[2], valid.shape[0]
+def project_qkv(pair, tail, xa, xb, w, code, was, made):
+    width, whole = w.shape[2], code.shape[0]
     call = kernel(
         functools.partial(qkv_body, pair), "project_qkv",
         (shape(whole, width, BF),) * 3 + (shape(PACK, width, F32),),
-        [smem()] + [vmem()] * (6 + len(made)), 16,
-        aliases={7 + i: i for i in range(len(made))},
-    )
-    return call(tail, xa, xb, w, valid, seg, was, *made)
+        [smem()] + [vmem()] * (5 + len(made)), 8,
+        aliases={6 + i: i for i in range(len(made))},
+    )
+    return call(tail, xa, xb, w, code, was, *made)
 
 
 def swap_heads(x):
@@ -276,7 +280,7 @@
 
 
 def forward_body(
-    last_ref, spot_ref, q_ref, k_ref, v_ref, segc_ref, segr_ref, num_ref, den_ref, st_ref, ks_ref
+    last_ref, spot_ref, q_ref, k_ref, v_ref, code_ref, segr_ref, num_ref, den_ref, st_ref, ks_ref
 ):
     rows, width = q_ref.shape
     size = CHUNK
@@ -292,7 +296,7 @@
         spot = spot_ref[c]
         at = pl.ds(pl.multiple_of(spot * size, size), size)
         q, k, v = q_ref[at, :], k_ref[at, :], v_ref[at, :]
-        seg = segc_ref[at, :]
+        seg = decode(code_ref[at, :])[0]
         keep = (lower & (seg == segr_ref[spot])).astype(BF)
         before, after = last_ref[c], last_ref[c + 1]
         carried = (seg == before).astype(F32)
@@ -315,18 +319,18 @@
     lax.fori_loop(0, rows // size, step, 0)
 
 
-def attend(last, spot, q, k, v, segc, segr):
+def attend(last, spot, q, k, v, code, segr):
     rows, width = q.shape
     call = kernel(
-        forward_body, "attend", (shape(rows, width, F32),) * 2, [smem()] * 2 + [vmem()] * 5, 24,
+        forward_body, "attend", (shape(rows, width, F32),) * 2, [smem()] * 2 + [vmem()] * 5, 8,
         scratch=[pltpu.VMEM((width, width), F32), pltpu.VMEM((8, width), F32)],
     )
-    return call(last, spot, q, k, v, segc, segr)
+    return call(last, spot, q, k, v, code, segr)
 
 
 def project_body(
-    pair, first_ref, num_ref, den_ref, q_ref, pack_ref, segc_ref, valid_ref, w_ref,
-    heads_ref, wide_ref, rinv_ref, a_ref, b_ref
+    pair, first_ref, num_ref, den_ref, q_ref, pack_ref, code_ref, w_ref,
+    heads_ref, rinv_ref, a_ref, b_ref
 ):
     width = q_ref.shape[1]
     block = same_head(width)
@@ -334,28 +338,25 @@
     sums = pack_ref[HEAD : HEAD + 1, :]
     for i, own, at in pair_slices(pair, a_ref.shape[0]):
         q = q_ref[at, :]
-        opening = (segc_ref[at, :] == first_ref[0]).astype(F32)
-        valid = valid_ref[at, :]
+        segment, valid = decode(code_ref[at, :])
+        opening = (segment == first_ref[0]).astype(F32)
         num = num_ref[at, :] + opening * nn(q, state)
         den = den_ref[at, :] + opening * nn((q.astype(F32) * sums).astype(BF), block.astype(BF))
         rinv = valid / (den + 1e-06 + 1.0 - valid)
-        wide = num * rinv
-        heads = wide.astype(BF)
+        heads = (num * rinv).astype(BF)
         heads_ref[own, :] = heads
-        wide_ref[own, :] = wide
-        rinv_ref[own, :] = rinv
+        rinv_ref[own, :] = rinv.astype(BF)
         (a_ref, b_ref)[i][...] = nn(heads, w_ref[...]).astype(BF)
 
 
-def project(pair, rows, last, num, den, q, pack, segc, valid, w, tokens):
+def project(pair, rows, last, num, den, q, pack, code, w, tokens):
     width = q.shape[1]
     call = kernel(
         functools.partial(project_body, pair), "project",
-        (shape(2 * rows, width, BF), shape(2 * rows, width, F32), shape(2 * rows, width, F32))
-        + (shape(rows, D, BF),) * 2,
-        [smem()] + [vmem()] * 7, 12, tokens=tokens,
-    )
-    return call(last, num, den, q, pack, segc, valid, w)
+        (shape(2 * rows, width, BF),) * 2 + (shape(rows, D, BF),) * 2,
+        [smem()] + [vmem()] * 6, 8, tokens=tokens,
+    )
+    return call(last, num, den, q, pack, code, w)
 
 
 def mlp_body(
@@ -383,13 +384,13 @@
     rows, hidden = xa.shape[0], up.shape[1]
     call = kernel(
         mlp_body, "mlp", (shape(2 * rows, hidden, BF),) * 2 + (shape(rows, D, BF),) * 4,
-        [vmem()] * 6, 32,
+        [vmem()] * 6, 9,
     )
     return call(xa, xb, ga, gb, up, down)
 
 
 def heads_back_body(
-    pair, first_ref, ga_ref, gb_ref, w_ref, wide_ref, rinv_ref, q_ref, segc_ref, was_ref, *rest
+    pair, first_ref, ga_ref, gb_ref, w_ref, heads_ref, rinv_ref, q_ref, code_ref, was_ref, *rest
 ):
     ng_ref, dg_ref, pack_ref = rest[-3:]
     width = q_ref.shape[1]
@@ -398,34 +399,34 @@
     state, sums = was_ref[0:HEAD, :], was_ref[HEAD:PACK, :]
     for i, own, at in pair_slices(pair, ga_ref.shape[0]):
         hg = nt((ga_ref, gb_ref)[i][...], w_ref[...])
-        rinv = rinv_ref[own, :]
+        rinv = rinv_ref[own, :].astype(F32)
         ng = (hg * rinv).astype(BF)
-        prod = hg * wide_ref[own, :]
+        prod = hg * heads_ref[own, :].astype(F32)
         high = prod.astype(BF)
         low = (prod - high.astype(F32)).astype(BF)
         dg = -(nn(high, ones_block) + nn(low, ones_block)) * rinv
         ng_ref[at, :] = ng
         dg_ref[at, :] = dg
-        opened = pick(segc_ref[at, :] == first_ref[0], q_ref[at, :])
+        opened = pick(decode(code_ref[at, :])[0] == first_ref[0], q_ref[at, :])
         state = state + fold_heads(pick(block, tn(opened, ng)), width)
         sums = sums + jnp.sum(opened.astype(F32) * dg, axis=0, keepdims=True)
     pack_ref[0:HEAD, :] = state
     pack_ref[HEAD:PACK, :] = sums
 
 
-def heads_back(pair, last, ga, gb, w, wide, rinv, q, segc, was, made, tokens=()):
+def heads_back(pair, last, ga, gb, w, heads, rinv, q, code, was, made, tokens=()):
     whole, width = q.shape
     call = kernel(
         functools.partial(heads_back_body, pair), "heads_back",
         (shape(whole, width, BF), shape(whole, width, F32), shape(PACK, width, F32)),
-        [smem()] + [vmem()] * (8 + len(made)), 16,
+        [smem()] + [vmem()] * (8 + len(made)), 5,
         aliases={9 + i: i for i in range(len(made))}, tokens=tokens,
     )
-    return call(last, ga, gb, w, wide, rinv, q, segc, was, *made)
+    return call(last, ga, gb, w, heads, rinv, q, code, was, *made)
 
 
 def backward_body(
-    last_ref, spot_ref, q_ref, k_ref, v_ref, ng_ref, dg_ref, segc_ref, segr_ref, pack_ref,
+    last_ref, spot_ref, q_ref, k_ref, v_ref, ng_ref, dg_ref, code_ref, segr_ref, pack_ref,
     dq_ref, dk_ref, dv_ref, all_ref, sums_ref, st_ref, ks_ref
 ):
     rows, width = q_ref.shape
@@ -443,7 +444,7 @@
         all_ref[c] = st_ref[...].astype(BF)
         sums_ref[c] = ks_ref[...]
         before, after = last_ref[c], last_ref[c + 1]
-        kept = pick(segc_ref[at, :] == after, k_ref[at, :])
+        kept = pick(decode(code_ref[at, :])[0] == after, k_ref[at, :])
         cont = (before == after).astype(F32)
         st_ref[...] = cont * st_ref[...] + pick(block, tn(kept, v_ref[at, :]))
         ks_ref[...] = cont * ks_ref[...] + jnp.sum(kept.astype(F32), axis=0, keepdims=True)
@@ -458,7 +459,7 @@
         spot = spot_ref[c]
         at = pl.ds(pl.multiple_of(spot * size, size), size)
         q, k, v, ng, dg = q_ref[at, :], k_ref[at, :], v_ref[at, :], ng_ref[at, :], dg_ref[at, :]
-        seg = segc_ref[at, :]
+        seg = decode(code_ref[at, :])[0]
         keep = (lower & (seg == segr_ref[spot])).astype(BF)
         before, after = last_ref[c], last_ref[c + 1]
         opened = seg == before
@@ -483,8 +484,8 @@
             dk = dk + tn(back, qh)
             dv = dv + tn(score, nh)
         dq_ref[at, :] = (dq * jnp.minimum(q.astype(F32), 1.0)).astype(BF)
-        dk_ref[at, :] = dk
-        dv_ref[at, :] = dv
+        dk_ref[at, :] = dk.astype(BF)
+        dv_ref[at, :] = dv.astype(BF)
         cont = (before == after).astype(F32)
         st_ref[...] = cont * st_ref[...] + pick(block, tn(pick(opened, q), ng))
         ks_ref[...] = cont * ks_ref[...] + jnp.sum(carried * q.astype(F32) * dg, axis=0, keepdims=True)
@@ -493,13 +494,13 @@
     lax.fori_loop(0, count, step, 0)
 
 
-def attend_back(last, spot, q, k, v, ng, dg, segc, segr, pack, tokens):
+def attend_back(last, spot, q, k, v, ng, dg, code, segr, pack, tokens):
     rows, width = q.shape
     count = rows // CHUNK
     call = kernel(
         backward_body, "attend_back",
-        (shape(rows, width, BF), shape(rows, width, F32), shape(rows, width, F32)),
-        [smem()] * 2 + [vmem()] * 8, 32,
+        (shape(rows, width, BF),) * 3,
+        [smem()] * 2 + [vmem()] * 8, 12,
         scratch=[
             pltpu.VMEM((count, width, width), BF),
             pltpu.VMEM((count, 8, width), F32),
@@ -508,11 +509,11 @@
         ],
         tokens=tokens,
     )
-    return call(last, spot, q, k, v, ng, dg, segc, segr, pack)
+    return call(last, spot, q, k, v, ng, dg, code, segr, pack)
 
 
 def mix_body(
-    pair, tail_ref, dq_ref, dk_ref, dv_ref, k_ref, v_ref, segc_ref, valid_ref, pack_ref, w_ref,
+    pair, tail_ref, dq_ref, dk_ref, dv_ref, k_ref, v_ref, code_ref, pack_ref, w_ref,
     mixed_ref, a_ref, b_ref
 ):
     width = k_ref.shape[1]
@@ -520,12 +521,12 @@
     state = spread_heads(pack_ref[0:HEAD, :], width, block).astype(BF)
     sums = pack_ref[HEAD : HEAD + 1, :]
     for i, own, at in pair_slices(pair, a_ref.shape[0]):
-        tail = (segc_ref[at, :] == tail_ref[0]).astype(F32)
+        tail = (decode(code_ref[at, :])[0] == tail_ref[0]).astype(F32)
         k = k_ref[at, :]
-        dk = dk_ref[at, :] + tail * (nt(v_ref[at, :], state) + sums)
-        dv = dv_ref[at, :] + tail * nn(k, state)
+        dk = dk_ref[at, :].astype(F32) + tail * (nt(v_ref[at, :], state) + sums)
+        dv = dv_ref[at, :].astype(F32) + tail * nn(k, state)
         dq = dq_ref[at, :]
-        dk = (valid_ref[at, :] * dk * jnp.minimum(k.astype(F32), 1.0)).astype(BF)
+        dk = (dk * jnp.minimum(k.astype(F32), 1.0)).astype(BF)
         dv = dv.astype(BF)
         mixed_ref[own, 0:width] = dq
         mixed_ref[own, width : 2 * width] = dk
@@ -534,14 +535,14 @@
         (a_ref, b_ref)[i][...] = out.astype(BF)
 
 
-def mix(pair, rows, tail, dq, dk, dv, k, v, segc, valid, pack, w, tokens):
+def mix(pair, rows, tail, dq, dk, dv, k, v, code, pack, w, tokens):
     width = k.shape[1]
     call = kernel(
         functools.partial(mix_body, pair), "mix",
         (shape(2 * rows, 3 * width, BF),) + (shape(rows, D, BF),) * 2,
-        [smem()] + [vmem()] * 9, 16, tokens=tokens,
-    )
-    return call(tail, dq, dk, dv, k, v, segc, valid, pack, w)
+        [smem()] + [vmem()] * 8, 8, tokens=tokens,
+    )
+    return call(tail, dq, dk, dv, k, v, code, pack, w)
 
 
 def feature(values):
@@ -711,7 +712,7 @@
     tail = last[-1:]
     order = jnp.arange(chunks, dtype=jnp.int32)
     spot = ((order // per) ^ member) * per + order % per
-    segc = segment[:, None]
+    code = (segment * 2 + mask * inside)[:, None]
     segr = segment.reshape(chunks, 1, CHUNK)
     validc = pixel_valid[:, None]
     gain1, bias1, gain2, bias2 = (
@@ -721,89 +722,83 @@
 
     normed_slots = gather_begin(norm_one(pixels, gain1, bias1))
     grad_slots = gather_begin(after(out_grad, normed_slots[members // 2]))
-    *made, pack = project_qkv(0, tail, normed_slots[0], normed_slots[1], qkv_weight, validc, segc, no_pack, ())
+    *made, pack = project_qkv(0, tail, normed_slots[0], normed_slots[1], qkv_weight, code, no_pack, ())
     normed_slots = gather_end(normed_slots, pack)
     for p in range(1, pairs):
         *made, pack = project_qkv(
-            p, tail, normed_slots[2 * p], normed_slots[2 * p + 1], qkv_weight, validc, segc, pack, made
+            p, tail, normed_slots[2 * p], normed_slots[2 * p + 1], qkv_weight, code, pack, made
         )
     q, k, v = made
     carry = gather_carry(pack.astype(BF), crops_at, here, groups, reach, False)
-    num, den = attend(last, spot, q, k, v, segc, segr)
+    num, den = attend(last, spot, q, k, v, code, segr)
     grad_slots = gather_end(grad_slots, num)
     sent = {
         p: project(
-            p, local_rows, last, num, den, q, carry, segc, validc, out_weight, [grad_slots[members // 2]]
+            p, local_rows, last, num, den, q, carry, code, out_weight, [grad_slots[members // 2]]
         )
         for p in reversed(range(pairs))
     }
-    parts = scatter_end(scatter_begin([sent[s // 2][3 + s % 2] for s in range(members)]))
+    parts = scatter_end(scatter_begin([sent[s // 2][2 + s % 2] for s in range(members)]))
     middle, normed_two, attended_square = norm_two(pixels, gain2, bias2, parts)
     two_slots = gather_begin(normed_two)
     hidden = [mlp(two_slots[0], two_slots[1], grad_slots[0], grad_slots[1], up_weight, down_weight)]
     two_slots = gather_end(two_slots, hidden[0][0])
     for p in range(1, pairs):
         hidden.append(mlp(*two_slots[2 * p : 2 * p + 2], *grad_slots[2 * p : 2 * p + 2], up_weight, down_weight))
-    two_parts = scatter_end(scatter_begin([hidden[s // 2][2 + s % 2] for s in range(members)]))
+    two_sums = scatter_begin([hidden[s // 2][2 + s % 2] for s in range(members)])
+    two_parts = scatter_end(two_sums)
     branch_sums = scatter_begin([hidden[s // 2][4 + s % 2] for s in range(members)])
-    down_grad = tn(
-        jnp.concatenate([h[0] for h in hidden], axis=0), jnp.concatenate(grad_slots, axis=0)
-    ).astype(BF)
-    up_grad = tn(
-        jnp.concatenate(two_slots, axis=0), jnp.concatenate([h[1] for h in hidden], axis=0)
-    ).astype(BF)
+    acts, hids, twos = after(
+        ([h[0] for h in hidden], [h[1] for h in hidden], two_slots), two_sums[members - 2]
+    )
+    down_grad = tn(jnp.concatenate(acts, axis=0), jnp.concatenate(grad_slots, axis=0)).astype(BF)
+    up_grad = tn(jnp.concatenate(twos, axis=0), jnp.concatenate(hids, axis=0)).astype(BF)
     bits = bits_of(groups)
     turned = bits[1:] + bits[:1]
-    down_sum = RowSum(down_grad, bits, two_parts[-1])
-    up_sum = RowSum(up_grad, turned, two_parts[-1])
-    middle_grad, middle_low, gain2_grad, bias2_grad = norm_two_back(
+    both = jnp.concatenate([down_grad, up_grad.reshape(-1, D)], axis=0)
+    both = lax.psum_scatter(after(both, two_parts[-1]), "rows", scatter_dimension=0, tiled=True)
+    middle_low, gain2_grad, bias2_grad = norm_two_back(
         out_grad, middle, gain2, two_parts,
-        [down_sum.sent, up_sum.sent, branch_sums[0][1], branch_sums[members - 2]],
+        [down_grad, up_grad, branch_sums[0][1], branch_sums[members - 2]],
     )
     middle_slots = gather_begin(middle_low)
     *made, grad_pack = heads_back(
-        0, last, middle_slots[0], middle_slots[1], out_weight, sent[0][1], sent[0][2], q, segc, no_pack, ()
-    )
-    branch_parts = scatter_end(branch_sums, middle_slots[members // 2])
-    tokens = [x.next(middle_slots[members // 2]) for x in (down_sum, up_sum)]
+        0, last, middle_slots[0], middle_slots[1], out_weight, sent[0][0], sent[0][1], q, code, no_pack, ()
+    )
+    branch_parts = scatter_end(branch_sums, middle_slots[members // 2], grad_pack)
     middle_slots = gather_end(middle_slots, grad_pack)
     for p in range(1, pairs):
         *made, grad_pack = heads_back(
             p, last, middle_slots[2 * p], middle_slots[2 * p + 1], out_weight,
-            sent[p][1], sent[p][2], q, segc, grad_pack, made, tokens
+            sent[p][0], sent[p][1], q, code, grad_pack, made
         )
     ng, dg = made
     grad_carry = gather_carry(grad_pack.astype(BF), crops_at, here, groups, reach, True)
-    out_weight_grad = tn(
-        jnp.concatenate([sent[p][0] for p in range(pairs)], axis=0), jnp.concatenate(middle_slots, axis=0)
-    ).astype(BF)
-    tokens = [out_weight_grad]
-    dq, dk, dv = attend_back(last, spot, q, k, v, ng, dg, segc, segr, carry, tokens)
-    out_sum = RowSum(out_weight_grad, turned, dq)
-    tokens = [down_sum.next(dq), up_sum.next(dq), out_sum.sent]
+    dq, dk, dv = attend_back(last, spot, q, k, v, ng, dg, code, segr, carry, [])
     mixes = {
-        p: mix(p, local_rows, tail, dq, dk, dv, k, v, segc, validc, grad_carry, qkv_weight, tokens)
+        p: mix(p, local_rows, tail, dq, dk, dv, k, v, code, grad_carry, qkv_weight, [])
         for p in reversed(range(pairs))
     }
     normed_sums = scatter_begin([mixes[s // 2][1 + s % 2] for s in range(members)])
     normed_parts = scatter_end(normed_sums)
     mixed_grad = jnp.concatenate([mixes[p][0] for p in range(pairs)], axis=0)
     qkv_grad = tn(mixed_grad, jnp.concatenate(normed_slots, axis=0)).astype(BF)
-    output, result_square, branch_square = finish(middle, branch_parts, [dq])
-    pixels_grad, gain1_grad, bias1_grad = norm_one_back(pixels, middle_grad, gain1, normed_parts)
-
-    tokens = [down_sum.next(mixed_grad), up_sum.next(mixed_grad), out_sum.next(mixed_grad)]
+    both = lax.all_gather(after(both, dq), "rows", axis=0, tiled=True)
+    down_grad = both[: down_grad.shape[0]].astype(F32)
+    up_grad = both[down_grad.shape[0] :].reshape(up_grad.shape).astype(F32)
     cut = 3 * width // 2
-    low_sum = RowSum(qkv_grad[:cut], bits, *tokens)
-    high_sum = RowSum(qkv_grad[cut:], turned, *tokens)
+    low_sum = RowSum(qkv_grad[:cut], bits)
+    high_sum = RowSum(qkv_grad[cut:], turned)
     normed_sent = normed_sums[members - 2]
+    heads_all = jnp.concatenate([sent[p][0] for p in range(pairs)], axis=0)
+    out_weight_grad = tn(after(heads_all, low_sum.sent, normed_sent), jnp.concatenate(middle_slots, axis=0))
+    out_sum = RowSum(out_weight_grad.astype(BF), turned)
     tokens = [low_sum.next(normed_sent), high_sum.next(normed_sent)]
-    tokens = [down_sum.next(*tokens), up_sum.next(*tokens), out_sum.next(*tokens)]
+    output, result_square, branch_square = finish(middle, branch_parts, tokens)
+    pixels_grad, gain1_grad, bias1_grad = norm_one_back(pixels, middle_low, gain1, normed_parts)
+    tokens = [out_sum.next(*tokens)]
     tokens = [low_sum.next(*tokens), high_sum.next(*tokens)]
     out_weight_grad = out_sum.finish(*tokens).astype(F32)
-    tokens = [low_sum.next(), high_sum.next()]
-    down_grad = down_sum.finish(*tokens).astype(F32)
-    up_grad = up_sum.finish(*tokens).astype(F32)
     qkv_grad = jnp.concatenate([low_sum.finish(), high_sum.finish()], axis=0)
     qkv_grad = jnp.swapaxes(qkv_grad.reshape(3, width, D), 1, 2).astype(F32)
 

time: 405 us -> 383 us (0.946)
  waiting for transfers between devices: 161 us -> 123 us
  between operations: 7.58 us -> 21.1 us
  local copies, waits for them, and re-layouts: 48.7 us -> 53.3 us
  starting transfers between devices: 57.4 us -> 61.7 us
  other arithmetic: 35.1 us -> 31 us
    ppermute x59 -> x47, waiting for transfers between devices: 161 us -> 123 us  [swap(): lax.ppermute(value, axis, [(i, i ^ bit) for i in range(lax.axis_size(axis...]
    select_n x15 -> x9, other arithmetic: 6.93 us -> 0.76 us  [next(): first = jnp.where(self.upper, got, self.kept)]
    ppermute x59 -> x47, starting transfers between devices: 47.8 us -> 52 us  [swap(): lax.ppermute(value, axis, [(i, i ^ bit) for i in range(lax.axis_size(axis...]
    convert_element_type x15 -> x8, other arithmetic: 8.33 us -> 4.8 us  [next(): self.value = (self.kept.astype(F32) + got.astype(F32)).astype(BF)]
    unnamed x201 -> x202, local copies, waits for them, and re-layouts: 40.2 us -> 41.4 us
  transfers between devices with their start and end apart: 63 -> 53, of which waited for: 24 -> 23; matrix products, arithmetic and copies ran while one was open for 14% -> 13% of each run, Pallas kernels for 17% -> 16%
where the time goes in v1:
time: 383 us; the launch traced here: 376 us
  waiting for transfers between devices  123 us (32%)
  Pallas kernels  70.6 us (18%)
  starting transfers between devices  61.7 us (16%)
  local copies, waits for them, and re-layouts  53.3 us (14%)
  other arithmetic  31 us (8%)
  between operations  21.1 us (6%)
  matrix products  15.3 us (4%)
    ppermute x47, waiting for transfers between devices, swap(): lax.ppermute(value, axis, [(i, i ^ bit) for i in range(lax.axis_size(axis...  123 us
    pallas_call x17, Pallas kernels, kernel(): return lambda *args: call(*args, *tokens)  70.6 us
    ppermute x47, starting transfers between devices, swap(): lax.ppermute(value, axis, [(i, i ^ bit) for i in range(lax.axis_size(axis...  52 us
    unnamed x202, local copies, waits for them, and re-layouts  41.4 us
    dot_general x4, matrix products, tn(): lax.dot_general(a, b, (((0,), (0,)), ((), ())), preferred_element_type=F32)  15 us
    ppermute x4, starting transfers between devices, shifted(): return lax.ppermute(pack, 'rows', pairs)  9.66 us
  transfers between devices with their start and end apart: 53, of which 23 were waited for; matrix products, arithmetic and copies ran while one was open for 13% of the time, Pallas kernels for 16%

profile of v1, /device:TPU:0, one launch (start us, length us, event | category | flops | bytes accessed | tf_op | source)
XLA Modules:
  0.0 375.7 jit_solution(15676526571419802430)
XLA Ops:
  11.3 3.0 collective-permute-start
  20.0 1.9 fusion.59.refs_4_.refs_5_.refs_7_.refs_6_
  24.0 4.0 %project_qkv.2 = (bf16[1536,256]{1,0:T(8,128)(2,1)S(1)}, bf16[1536,256]{1,0:T(8,128)(2,1)S(1)}, bf16[1536,256]{1,0:T(8,128)(2,1)S(1)}, f32[80,256]{1,0:T(8,128)S(1)}) custom-call(s32[1]{0:T(128)} %slice.108.refs_0_, bf16[384,1024]{1,0:T(8,128)(2,1)} %norm_one.1.refs_1_, bf16[384,1024]{1,0:T(8,128)(2,1)S(1)} %copy-done.53, bf16[3,1024,256]{2,1,0:T(8,128)(2,1)S(1)} %copy-done, ...), custom_call_target="tpu_custom_call" | custom-call | tf_op jit(solution)/shard_map/project_qkv/pallas_call | solution.py:101
  28.0 4.1 %collective-permute-done.refs_1_ = bf16[384,1024]{1,0:T(8,128)(2,1)} collective-permute-done((bf16[384,1024]{1,0:T(8,128)(2,1)}, bf16[384,1024]{1,0:T(8,128)(2,1)}, u32[]{:S(2)}, u32[]{:S(2)}) %collective-permute-start) | collective-permute-done | bytes 786464 | tf_op jit(solution)/shard_map/ppermute | solution.py:557
  32.1 1.7 collective-permute-start.5
  34.6 4.0 %project_qkv.3 = (bf16[1536,256]{1,0:T(8,128)(2,1)S(1)}, bf16[1536,256]{1,0:T(8,128)(2,1)S(1)}, bf16[1536,256]{1,0:T(8,128)(2,1)S(1)}, f32[80,256]{1,0:T(8,128)S(1)}) custom-call(s32[1]{0:T(128)} %slice.108.refs_0_, bf16[384,1024]{1,0:T(8,128)(2,1)} %collective-permute-done.refs_1_, ...), custom_call_target="tpu_custom_call", output_to_operand_aliasing={{0}: (6, {}), {1}: (7, {}), {2}: (8, {})} | custom-call | tf_op jit(solution)/shard_map/project_qkv/pallas_call | solution.py:101
  40.5 3.7 collective-permute-start.4
  44.2 3.4 collective-permute-start.3
  53.2 6.2 %attend.1 = (f32[1536,256]{1,0:T(8,128)S(1)}, f32[1536,256]{1,0:T(8,128)S(1)}) custom-call(s32[5]{0:T(128)S(1)} %broadcast_add_fusion.2.refs_0_, s32[4]{0:T(128)S(1)} %iota_xor_fusion.refs_1_, bf16[1536,256]{1,0:T(8,128)(2,1)S(1)} %get-tuple-element.100.refs_2_.refs_3_.refs_6_, bf16[1536,256]{1,0:T(8,128)(2,1)S(1)} %copy-done.2, ...), custom_call_target="tpu_custom_call" | custom-call | tf_op jit(solution)/shard_map/attend/pallas_call | solution.py:101
  59.5 1.6 project.3
  62.0 1.6 project.2
  65.1 1.6 collective-permute-start.8
  66.7 17.9 %collective-permute-done.8.refs_5_ = bf16[384,1024]{1,0:T(8,128)(2,1)S(1)} collective-permute-done((bf16[384,1024]{1,0:T(8,128)(2,1)S(1)}, bf16[384,1024]{1,0:T(8,128)(2,1)S(1)}, u32[]{:S(2)}, u32[]{:S(2)}) %collective-permute-start.8) | collective-permute-done | bytes 786464 | tf_op jit(solution)/shard_map/ppermute | solution.py:557
  87.2 1.5 collective-permute-start.12
  89.5 7.7 %mlp.2 = (bf16[768,1024]{1,0:T(8,128)(2,1)S(1)}, bf16[768,1024]{1,0:T(8,128)(2,1)S(1)}, bf16[384,1024]{1,0:T(8,128)(2,1)S(1)}, bf16[384,1024]{1,0:T(8,128)(2,1)S...) custom-call(bf16[384,1024]{1,0:T(8,128)(2,1)S(1)} %get-tuple-element.129.refs_0_, ...), custom_call_target="tpu_custom_call" | custom-call | tf_op jit(solution)/shard_map/mlp/pallas_call | solution.py:101
  100.0 7.2 %collective-permute-done.12.refs_0_ = bf16[384,1024]{1,0:T(8,128)(2,1)S(1)} collective-permute-done((bf16[384,1024]{1,0:T(8,128)(2,1)S(1)}, bf16[384,1024]{1,0:T(8,128)(2,1)S(1)}, u32[]{:S(2)}, u32[]{:S(2)}) %collective-permute-start.12) | collective-permute-done | bytes 786464 | tf_op jit(solution)/shard_map/ppermute | solution.py:557
  107.1 2.3 collective-permute-done.13.refs_1_
  109.4 9.1 %mlp.3 = (bf16[768,1024]{1,0:T(8,128)(2,1)S(1)}, bf16[768,1024]{1,0:T(8,128)(2,1)S(1)}, bf16[384,1024]{1,0:T(8,128)(2,1)S(1)}, bf16[384,1024]{1,0:T(8,128)(2,1)S...) custom-call(bf16[384,1024]{1,0:T(8,128)(2,1)S(1)} %collective-permute-done.12.refs_0_, ...), custom_call_target="tpu_custom_call" | custom-call | tf_op jit(solution)/shard_map/mlp/pallas_call | solution.py:101
  118.7 2.2 collective-permute-done.17
  122.1 1.5 collective-permute-start.18
  123.6 4.7 %fusion.46.refs_6_ = bf16[1024,1024]{1,0:T(8,128)(2,1)S(1)} fusion(bf16[384,1024]{1,0:T(8,128)(2,1)S(1)} %collective-permute-done.14.refs_3_, bf16[384,1024]{1,0:T(8,128)(2,1)} %collective-permute-done.5.refs_7_.refs_2_, bf16[384,1024]{1,0:T(8,128)(2,1)S(1)} %collective-permute-done.10.refs_3_, bf16[384,1024]{1,0:T(8,128)(2,1)S(1)} %copy-done.25, ...), kind=kOutput, calls=%fused_computation.45 | convolution fusion | flops 3241148416 | bytes 8388608 | tf_op jit(solution)/shard_map/dot_general | solution.py:30
  128.3 3.8 %fusion.41.refs_7_ = bf16[1024,1024]{1,0:T(8,128)(2,1)S(1)} fusion(bf16[768,1024]{1,0:T(8,128)(2,1)S(1)} %get-tuple-element.134, bf16[768,1024]{1,0:T(8,128)(2,1)S(1)} %get-tuple-element.133, bf16[384,1024]{1,0:T(8,128)(2,1)S(1)} %collective-permute-done.13.refs_1_, bf16[384,1024]{1,0:T(8,128)(2,1)S(1)} %collective-permute-done.12.refs_0_, ...), kind=kOutput, calls=%fused_computation.44 | convolution fusion | flops 3241148416 | bytes 8388608 | tf_op jit(solution)/shard_map/dot_general | solution.py:30
  132.2 2.5 pad_maximum_fusion
  136.0 6.0 %collective-permute-done.18.refs_5_ = bf16[384,1024]{1,0:T(8,128)(2,1)} collective-permute-done((bf16[384,1024]{1,0:T(8,128)(2,1)}, bf16[384,1024]{1,0:T(8,128)(2,1)}, u32[]{:S(2)}, u32[]{:S(2)}) %collective-permute-start.18) | collective-permute-done | bytes 786464 | tf_op jit(solution)/shard_map/ppermute | solution.py:557
  142.7 1.9 collective-permute-done.15
  146.9 1.6 copy-done.17
  151.9 2.7 norm_two_back.1
  154.9 1.6 collective-permute-start.19
  157.0 2.3 heads_back.2
  162.0 12.8 %collective-permute-done.19.refs_1_ = bf16[384,1024]{1,0:T(8,128)(2,1)} collective-permute-done((bf16[384,1024]{1,0:T(8,128)(2,1)S(1)}, bf16[384,1024]{1,0:T(8,128)(2,1)}, u32[]{:S(2)}, u32[]{:S(2)}) %collective-permute-start.19) | collective-permute-done | bytes 786464 | tf_op jit(solution)/shard_map/ppermute | solution.py:557
  181.6 1.5 copy-done.22
  187.2 3.1 heads_back.3
  196.5 1.6 copy.49
  198.1 1.6 collective-permute-start.21
  205.4 13.8 %attend_back.1 = (bf16[1536,256]{1,0:T(8,128)(2,1)S(1)}, bf16[1536,256]{1,0:T(8,128)(2,1)S(1)}, bf16[1536,256]{1,0:T(8,128)(2,1)S(1)}) custom-call(s32[5]{0:T(128)S(1)} %broadcast_add_fusion.2.refs_0_, s32[4]{0:T(128)S(1)} %copy-done.79, bf16[1536,256]{1,0:T(8,128)(2,1)S(1)} %get-tuple-element.100.refs_2_.refs_3_.refs_6_, bf16[1536,256]{1,0:T(8,128)(2,1)S(1)} %copy-done.3, ...), custom_call_target="tpu_custom_call" | custom-call | tf_op jit(solution)/shard_map/attend_back/pallas_call | solution.py:101
  220.0 2.4 mix.3
  222.5 3.4 mix.2
  226.9 4.1 %fusion.51 = bf16[768,1024]{1,0:T(8,128)(2,1)S(1)} fusion(bf16[384,1024]{1,0:T(8,128)(2,1)S(1)} %copy-done.45, bf16[384,1024]{1,0:T(8,128)(2,1)} %collective-permute-done.refs_1_, bf16[384,1024]{1,0:T(8,128)(2,1)S(1)} %copy-done.54, bf16[384,1024]{1,0:T(8,128)(2,1)} %norm_one.1.refs_1_, bf16[768,768]{1,0:T(8,128)(2,1)S(1)} %get-tuple-element.152, ...), kind=kOutput, calls=%fused_computation.46 | convolution fusion | flops 2434007040 | bytes 7077888 | tf_op jit(solution)/shard_map/dot_general | solution.py:30
  231.1 3.5 collective-permute-start.27
  234.6 1.7 collective-permute-start.25
  237.9 2.4 fusion.56
  241.1 3.2 collective-permute-done.27
  249.2 3.8 %collective-permute-start.36 = (bf16[96,1024]{1,0:T(8,128)(2,1)S(1)}, bf16[96,1024]{1,0:T(8,128)(2,1)}, u32[]{:S(2)}, u32[]{:S(2)}) collective-permute-start(bf16[96,1024]{1,0:T(8,128)(2,1)S(1)} %broadcast_select_fusion.11.refs_5_), channel_id=1, source_target_pairs={{0,16},{4,20},{8,24},{12,28},{16,0},{20,4},{24,8},{28,12},{1,17},{... | collective-permute-start | bytes 589832 | tf_op jit(solution)/shard_map/ppermute | solution.py:557
  253.1 1.5 collective-permute-start.30
  254.6 2.5 finish.1
  263.8 1.9 collective-permute-start.37
  267.0 5.1 %collective-permute-start.32 = (bf16[48,1024]{1,0:T(8,128)(2,1)S(1)}, bf16[48,1024]{1,0:T(8,128)(2,1)S(1)}, u32[]{:S(2)}, u32[]{:S(2)}) collective-permute-start(bf16[48,1024]{1,0:T(8,128)(2,1)S(1)} %broadcast_select_fusion.23), channel_id=1, source_target_pairs={{0,16},{4,20},{8,24},{12,28},{16,0},{20,4},{24,8},{28,12},{1,17},{... | collective-permute-start | bytes 294920 | tf_op jit(solution)/shard_map/ppermute | solution.py:557
  272.1 2.2 collective-permute-start.38
  274.3 12.8 %collective-permute-done.32 = bf16[48,1024]{1,0:T(8,128)(2,1)S(1)} collective-permute-done((bf16[48,1024]{1,0:T(8,128)(2,1)S(1)}, bf16[48,1024]{1,0:T(8,128)(2,1)S(1)}, u32[]{:S(2)}, u32[]{:S(2)}) %collective-permute-start.32) | collective-permute-done | bytes 98336 | tf_op jit(solution)/shard_map/ppermute | solution.py:557
  287.3 1.7 collective-permute-start.42
  289.1 3.0 collective-permute-start.39
  292.1 5.2 %collective-permute-done.33 = bf16[48,1024]{1,0:T(8,128)(2,1)S(1)} collective-permute-done((bf16[48,1024]{1,0:T(8,128)(2,1)S(1)}, bf16[48,1024]{1,0:T(8,128)(2,1)S(1)}, u32[]{:S(2)}, u32[]{:S(2)}) %collective-permute-start.33) | collective-permute-done | bytes 98336 | tf_op jit(solution)/shard_map/ppermute | solution.py:557
  297.3 4.0 %collective-permute-start.43 = (bf16[32,1024]{1,0:T(8,128)(2,1)S(1)}, bf16[32,1024]{1,0:T(8,128)(2,1)S(1)}, u32[]{:S(2)}, u32[]{:S(2)}) collective-permute-start(bf16[32,1024]{1,0:T(8,128)(2,1)S(1)} %add_convert_fusion.12), channel_id=1, source_target_pairs={{0,4},{4,0},{8,12},{12,8},{16,20},{20,16},{24,28},{28,24},{1,5},{5... | collective-permute-start | bytes 196616 | tf_op jit(solution)/shard_map/ppermute | solution.py:557
  301.5 2.8 collective-permute-done.43
  304.5 3.7 norm_one_back.1
  310.1 12.9 %collective-permute-done.34 = bf16[96,1024]{1,0:T(8,128)(2,1)S(1)} collective-permute-done((bf16[96,1024]{1,0:T(8,128)(2,1)S(1)}, bf16[96,1024]{1,0:T(8,128)(2,1)S(1)}, u32[]{:S(2)}, u32[]{:S(2)}) %collective-permute-start.34) | collective-permute-done | bytes 196640 | tf_op jit(solution)/shard_map/ppermute | solution.py:557
  323.6 2.1 collective-permute-start.35
  325.7 2.3 collective-permute-done.48
  328.0 19.8 %collective-permute-done.49 = f32[4224]{0:T(1024)S(1)} collective-permute-done((f32[4224]{0:T(1024)S(1)}, f32[4224]{0:T(1024)S(1)}, u32[]{:S(2)}, u32[]{:S(2)}) %collective-permute-start.49) | collective-permute-done | bytes 16928 | tf_op jit(solution)/shard_map/ppermute | solution.py:557
  348.2 3.2 collective-permute-start.45
  351.4 1.7 collective-permute-done.50
  354.5 3.4 collective-permute-done.45
  359.7 2.1 copy.47
  361.7 6.7 %slice_convert_fusion = (f32[1024,1024]{1,0:T(8,128)}, f32[1024,1024]{1,0:T(8,128)}) fusion(bf16[2048,1024]{1,0:T(8,128)(2,1)} %all-gather.2.cloned.1.call-done), kind=kLoop, calls=%fused_computation.42 | loop fusion | flops 2097152 | bytes 12582912 | tf_op jit(solution)/shard_map/convert_element_type | solution.py:787
  (356 shorter events, 82.0 us)
Async XLA Ops:
  7.2 241.0 %reduce-scatter.2.cloned.1.call-start = ((), (), s32[]{:S(2)}) async-start(), calls=%async_computation.1 | async-start | bytes 4718592 | tf_op jit(solution)/shard_map/reduce_scatter | solution.py:759
  11.3 20.8 %collective-permute-start = (bf16[384,1024]{1,0:T(8,128)(2,1)}, bf16[384,1024]{1,0:T(8,128)(2,1)}, u32[]{:S(2)}, u32[]{:S(2)}) collective-permute-start(bf16[384,1024]{1,0:T(8,128)(2,1)} %norm_one.1.refs_1_), channel_id=1, source_target_pairs={{0,2},{1,3},{2,0},{3,1},{4,6},{5,7},{6,4},{7,5},{8,10},{9,11},{10,... | collective-permute-start | bytes 2359304 | tf_op jit(solution)/shard_map/ppermute | solution.py:557
  14.3 7.7 %collective-permute-start.1 = (bf16[384,1024]{1,0:T(8,128)(2,1)}, bf16[384,1024]{1,0:T(8,128)(2,1)S(1)}, u32[]{:S(2)}, u32[]{:S(2)}) collective-permute-start(bf16[384,1024]{1,0:T(8,128)(2,1)} %norm_one.1.refs_1_), channel_id=1, source_target_pairs={{0,1},{1,0},{2,3},{3,2},{4,5},{5,4},{6,7},{7,6},{8,9},{9,8},{10,11... | collective-permute-start | bytes 2359304 | tf_op jit(solution)/shard_map/ppermute | solution.py:557
  20.0 27.6 %copy-start.88 = (s32[1536]{0:T(1024)}, s32[1536]{0:T(1024)S(1)}, u32[]{:S(2)}) copy-start(s32[1536]{0:T(1024)S(1)} %get-tuple-element.209) | copy-start | bytes 18436
  32.1 2.5 collective-permute-start.2
  32.1 27.4 %collective-permute-start.5 = (bf16[384,1024]{1,0:T(8,128)(2,1)}, bf16[384,1024]{1,0:T(8,128)(2,1)}, u32[]{:S(2)}, u32[]{:S(2)}) collective-permute-start(bf16[384,1024]{1,0:T(8,128)(2,1)} %refs_0_.6), channel_id=1, source_target_pairs={{0,2},{1,3},{2,0},{3,1},{4,6},{5,7},{6,4},{7,5},{8,10},{9,11},{10,... | collective-permute-start | bytes 2359304 | tf_op jit(solution)/shard_map/ppermute | solution.py:557
  40.5 19.0 %collective-permute-start.4 = (bf16[80,256]{1,0:T(8,128)(2,1)S(1)}, bf16[80,256]{1,0:T(8,128)(2,1)S(1)}, u32[]{:S(2)}, u32[]{:S(2)}) collective-permute-start(bf16[80,256]{1,0:T(8,128)(2,1)S(1)} %convert_element_type.185), channel_id=1, source_target_pairs={{0,8},{4,12},{8,16},{12,20},{16,24},{20,28},{1,9},{5,13},{9,17},{1... | collective-permute-start | bytes 122888 | tf_op jit(solution)/shard_map/ppermute | solution.py:650
  44.2 15.3 %collective-permute-start.3 = (bf16[80,256]{1,0:T(8,128)(2,1)S(1)}, bf16[80,256]{1,0:T(8,128)(2,1)S(1)}, u32[]{:S(2)}, u32[]{:S(2)}) collective-permute-start(bf16[80,256]{1,0:T(8,128)(2,1)S(1)} %convert_element_type.185), channel_id=1, source_target_pairs={{0,4},{4,8},{8,12},{12,16},{16,20},{20,24},{24,28},{1,5},{5,9},{9,... | collective-permute-start | bytes 122888 | tf_op jit(solution)/shard_map/ppermute | solution.py:650
  61.9 22.8 %copy-start.19 = (bf16[384,1024]{1,0:T(8,128)(2,1)S(1)}, bf16[384,1024]{1,0:T(8,128)(2,1)}, u32[]{:S(2)}) copy-start(bf16[384,1024]{1,0:T(8,128)(2,1)} %refs_0_.7) | copy-start | bytes 2359300
  61.9 22.8 %copy-start.69 = (f32[1024]{0:T(1024)S(1)}, f32[1024]{0:T(1024)}, u32[]{:S(2)}) copy-start(f32[1024]{0:T(1024)} %param.20) | copy-start | bytes 12292
  61.9 22.8 %copy-start.73 = (f32[1024]{0:T(1024)S(1)}, f32[1024]{0:T(1024)}, u32[]{:S(2)}) copy-start(f32[1024]{0:T(1024)} %param.21) | copy-start | bytes 12292
  61.9 2.9 collective-permute-start.7
  64.3 25.1 %copy-start.9 = (bf16[1024,1024]{1,0:T(8,128)(2,1)S(1)}, bf16[1024,1024]{1,0:T(8,128)(2,1)}, u32[]{:S(2)}) copy-start(bf16[1024,1024]{1,0:T(8,128)(2,1)} %refs_4_.3) | copy-start | bytes 6291460
  64.3 25.1 %copy-start.10 = (bf16[1024,1024]{1,0:T(8,128)(2,1)S(1)}, bf16[1024,1024]{1,0:T(8,128)(2,1)}, u32[]{:S(2)}) copy-start(bf16[1024,1024]{1,0:T(8,128)(2,1)} %refs_5_.3) | copy-start | bytes 6291460
  64.3 2.4 collective-permute-start.6
  65.1 19.5 %collective-permute-start.8 = (bf16[384,1024]{1,0:T(8,128)(2,1)S(1)}, bf16[384,1024]{1,0:T(8,128)(2,1)S(1)}, u32[]{:S(2)}, u32[]{:S(2)}) collective-permute-start(bf16[384,1024]{1,0:T(8,128)(2,1)S(1)} %add_convert_fusion.3), channel_id=1, source_target_pairs={{0,2},{1,3},{2,0},{3,1},{4,6},{5,7},{6,4},{7,5},{8,10},{9,11},{10,... | collective-permute-start | bytes 2359304 | tf_op jit(solution)/shard_map/ppermute | solution.py:557
  66.7 22.2 %collective-permute-start.10 = (bf16[384,1024]{1,0:T(8,128)(2,1)S(1)}, bf16[384,1024]{1,0:T(8,128)(2,1)S(1)}, u32[]{:S(2)}, u32[]{:S(2)}) collective-permute-start(bf16[384,1024]{1,0:T(8,128)(2,1)S(1)} %copy-done.25), channel_id=1, source_target_pairs={{0,1},{1,0},{2,3},{3,2},{4,5},{5,4},{6,7},{7,6},{8,9},{9,8},{10,11... | collective-permute-start | bytes 2359304 | tf_op jit(solution)/shard_map/ppermute | solution.py:557
  87.2 2.3 collective-permute-start.9
  87.2 20.0 %collective-permute-start.12 = (bf16[384,1024]{1,0:T(8,128)(2,1)S(1)}, bf16[384,1024]{1,0:T(8,128)(2,1)S(1)}, u32[]{:S(2)}, u32[]{:S(2)}) collective-permute-start(bf16[384,1024]{1,0:T(8,128)(2,1)S(1)} %get-tuple-element.129.refs_0_), channel_id=1, source_target_pairs={{0,2},{1,3},{2,0},{3,1},{4,6},{5,7},{6,4},{7,5},{8,10},{9,11},{10,... | collective-permute-start | bytes 2359304 | tf_op jit(solution)/shard_map/ppermute | solution.py:557
  88.7 18.4 %collective-permute-start.14 = (bf16[384,1024]{1,0:T(8,128)(2,1)}, bf16[384,1024]{1,0:T(8,128)(2,1)S(1)}, u32[]{:S(2)}, u32[]{:S(2)}) collective-permute-start(bf16[384,1024]{1,0:T(8,128)(2,1)} %collective-permute-done.5.refs_7_.refs_2_), channel_id=1, source_target_pairs={{0,1},{1,0},{2,3},{3,2},{4,5},{5,4},{6,7},{7,6},{8,9},{9,8},{10,11... | collective-permute-start | bytes 2359304 | tf_op jit(solution)/shard_map/ppermute | solution.py:557
  107.1 2.3 collective-permute-start.13
  118.5 2.4 collective-permute-start.17
  122.1 19.9 %collective-permute-start.18 = (bf16[384,1024]{1,0:T(8,128)(2,1)}, bf16[384,1024]{1,0:T(8,128)(2,1)}, u32[]{:S(2)}, u32[]{:S(2)}) collective-permute-start(bf16[384,1024]{1,0:T(8,128)(2,1)} %add_convert_fusion.1), channel_id=1, source_target_pairs={{0,2},{1,3},{2,0},{3,1},{4,6},{5,7},{6,4},{7,5},{8,10},{9,11},{10,... | collective-permute-start | bytes 2359304 | tf_op jit(solution)/shard_map/ppermute | solution.py:557
  142.0 219.7 %all-gather.2.cloned.1.call-start = ((), (), s32[]{:S(2)}) async-start(), calls=%async_computation.2 | async-start | bytes 4718592 | tf_op jit(solution)/shard_map/all_gather | solution.py:786
  142.1 2.6 collective-permute-start.15
  142.1 3.9 %collective-permute-start.11 = (bf16[384,1024]{1,0:T(8,128)(2,1)}, bf16[384,1024]{1,0:T(8,128)(2,1)S(1)}, u32[]{:S(2)}, u32[]{:S(2)}) collective-permute-start(bf16[384,1024]{1,0:T(8,128)(2,1)} %copy-done.81), channel_id=1, source_target_pairs={{0,1},{1,0},{2,3},{3,2},{4,5},{5,4},{6,7},{7,6},{8,9},{9,8},{10,11... | collective-permute-start | bytes 2359304 | tf_op jit(solution)/shard_map/ppermute | solution.py:557
  142.6 4.2 %collective-permute-start.16 = (bf16[384,1024]{1,0:T(8,128)(2,1)}, bf16[384,1024]{1,0:T(8,128)(2,1)S(1)}, u32[]{:S(2)}, u32[]{:S(2)}) collective-permute-start(bf16[384,1024]{1,0:T(8,128)(2,1)} %copy-done.80), channel_id=1, source_target_pairs={{0,1},{1,0},{2,3},{3,2},{4,5},{5,4},{6,7},{7,6},{8,9},{9,8},{10,11... | collective-permute-start | bytes 2359304 | tf_op jit(solution)/shard_map/ppermute | solution.py:557
  154.6 20.2 %copy-start.74 = (f32[1,1024]{1,0:T(1,128)}, f32[1,1024]{1,0:T(1,128)S(1)}, u32[]{:S(2)}) copy-start(f32[1,1024]{1,0:T(1,128)S(1)} %get-tuple-element.175) | copy-start | bytes 12292
  154.6 24.7 %copy-start.90 = (s32[384]{0:T(512)S(1)}, s32[384]{0:T(512)}, u32[]{:S(2)}) copy-start(s32[384]{0:T(512)} %copy-done.89) | copy-start | bytes 4612
  154.7 2.4 collective-permute-start.20
  154.9 19.9 %collective-permute-start.19 = (bf16[384,1024]{1,0:T(8,128)(2,1)S(1)}, bf16[384,1024]{1,0:T(8,128)(2,1)}, u32[]{:S(2)}, u32[]{:S(2)}) collective-permute-start(bf16[384,1024]{1,0:T(8,128)(2,1)S(1)} %get-tuple-element.135.refs_1_), channel_id=1, source_target_pairs={{0,2},{1,3},{2,0},{3,1},{4,6},{5,7},{6,4},{7,5},{8,10},{9,11},{10,... | collective-permute-start | bytes 2359304 | tf_op jit(solution)/shard_map/ppermute | solution.py:557
  174.8 5.8 %collective-permute-start.22 = (bf16[384,1024]{1,0:T(8,128)(2,1)}, bf16[384,1024]{1,0:T(8,128)(2,1)}, u32[]{:S(2)}, u32[]{:S(2)}) collective-permute-start(bf16[384,1024]{1,0:T(8,128)(2,1)} %collective-permute-done.19.refs_1_), channel_id=1, source_target_pairs={{0,1},{1,0},{2,3},{3,2},{4,5},{5,4},{6,7},{7,6},{8,9},{9,8},{10,11... | collective-permute-start | bytes 2359304 | tf_op jit(solution)/shard_map/ppermute | solution.py:557
  192.9 26.2 %collective-permute-start.24 = (bf16[80,256]{1,0:T(8,128)(2,1)}, bf16[80,256]{1,0:T(8,128)(2,1)}, u32[]{:S(2)}, u32[]{:S(2)}) collective-permute-start(bf16[80,256]{1,0:T(8,128)(2,1)} %convert_element_type.199), channel_id=1, source_target_pairs={{8,0},{12,4},{16,8},{20,12},{24,16},{28,20},{9,1},{13,5},{17,9},{2... | collective-permute-start | bytes 122888 | tf_op jit(solution)/shard_map/ppermute | solution.py:650
  194.2 24.9 %collective-permute-start.23 = (bf16[80,256]{1,0:T(8,128)(2,1)}, bf16[80,256]{1,0:T(8,128)(2,1)}, u32[]{:S(2)}, u32[]{:S(2)}) collective-permute-start(bf16[80,256]{1,0:T(8,128)(2,1)} %convert_element_type.199), channel_id=1, source_target_pairs={{4,0},{8,4},{12,8},{16,12},{20,16},{24,20},{28,24},{5,1},{9,5},{13... | collective-permute-start | bytes 122888 | tf_op jit(solution)/shard_map/ppermute | solution.py:650
  198.1 55.0 %collective-permute-start.21 = (bf16[384,1024]{1,0:T(8,128)(2,1)}, bf16[384,1024]{1,0:T(8,128)(2,1)}, u32[]{:S(2)}, u32[]{:S(2)}) collective-permute-start(bf16[384,1024]{1,0:T(8,128)(2,1)} %copy-done.34), channel_id=1, source_target_pairs={{0,2},{1,3},{2,0},{3,1},{4,6},{5,7},{6,4},{7,5},{8,10},{9,11},{10,... | collective-permute-start | bytes 2359304 | tf_op jit(solution)/shard_map/ppermute | solution.py:557
  226.7 9.6 %collective-permute-start.26 = (bf16[384,1024]{1,0:T(8,128)(2,1)S(1)}, bf16[384,1024]{1,0:T(8,128)(2,1)S(1)}, u32[]{:S(2)}, u32[]{:S(2)}) collective-permute-start(bf16[384,1024]{1,0:T(8,128)(2,1)S(1)} %get-tuple-element.154), channel_id=1, source_target_pairs={{0,1},{1,0},{2,3},{3,2},{4,5},{5,4},{6,7},{7,6},{8,9},{9,8},{10,11... | collective-permute-start | bytes 2359304 | tf_op jit(solution)/shard_map/ppermute | solution.py:557
  231.1 13.2 %collective-permute-start.27 = (bf16[192,1024]{1,0:T(8,128)(2,1)S(1)}, bf16[192,1024]{1,0:T(8,128)(2,1)S(1)}, u32[]{:S(2)}, u32[]{:S(2)}) collective-permute-start(bf16[192,1024]{1,0:T(8,128)(2,1)S(1)} %get-tuple-element.185), channel_id=1, source_target_pairs={{0,8},{4,12},{8,0},{12,4},{16,24},{20,28},{24,16},{28,20},{1,9},{5... | collective-permute-start | bytes 1179656 | tf_op jit(solution)/shard_map/ppermute | solution.py:557
  234.6 11.2 %collective-permute-start.25 = (bf16[192,1024]{1,0:T(8,128)(2,1)S(1)}, bf16[192,1024]{1,0:T(8,128)(2,1)S(1)}, u32[]{:S(2)}, u32[]{:S(2)}) collective-permute-start(bf16[192,1024]{1,0:T(8,128)(2,1)S(1)} %get-tuple-element.186), channel_id=1, source_target_pairs={{0,4},{4,0},{8,12},{12,8},{16,20},{20,16},{24,28},{28,24},{1,5},{5... | collective-permute-start | bytes 1179656 | tf_op jit(solution)/shard_map/ppermute | solution.py:557
  236.3 68.2 %collective-permute-start.28 = (bf16[384,1024]{1,0:T(8,128)(2,1)}, bf16[384,1024]{1,0:T(8,128)(2,1)}, u32[]{:S(2)}, u32[]{:S(2)}) collective-permute-start(bf16[384,1024]{1,0:T(8,128)(2,1)} %get-tuple-element.159), channel_id=1, source_target_pairs={{0,1},{1,0},{2,3},{3,2},{4,5},{5,4},{6,7},{7,6},{8,9},{9,8},{10,11... | collective-permute-start | bytes 2359304 | tf_op jit(solution)/shard_map/ppermute | solution.py:557
  237.5 67.0 %collective-permute-start.29 = (bf16[384,1024]{1,0:T(8,128)(2,1)}, bf16[384,1024]{1,0:T(8,128)(2,1)}, u32[]{:S(2)}, u32[]{:S(2)}) collective-permute-start(bf16[384,1024]{1,0:T(8,128)(2,1)} %add_convert_fusion), channel_id=1, source_target_pairs={{0,2},{1,3},{2,0},{3,1},{4,6},{5,7},{6,4},{7,5},{8,10},{9,11},{10,... | collective-permute-start | bytes 2359304 | tf_op jit(solution)/shard_map/ppermute | solution.py:557
  245.8 15.2 %collective-permute-start.31 = (bf16[128,1024]{1,0:T(8,128)(2,1)}, bf16[128,1024]{1,0:T(8,128)(2,1)}, u32[]{:S(2)}, u32[]{:S(2)}) collective-permute-start(bf16[128,1024]{1,0:T(8,128)(2,1)} %broadcast_select_fusion.8), channel_id=1, source_target_pairs={{0,8},{4,12},{8,0},{12,4},{16,24},{20,28},{24,16},{28,20},{1,9},{5... | collective-permute-start | bytes 786440 | tf_op jit(solution)/shard_map/ppermute | solution.py:557
  249.2 13.3 %collective-permute-start.36 = (bf16[96,1024]{1,0:T(8,128)(2,1)S(1)}, bf16[96,1024]{1,0:T(8,128)(2,1)}, u32[]{:S(2)}, u32[]{:S(2)}) collective-permute-start(bf16[96,1024]{1,0:T(8,128)(2,1)S(1)} %broadcast_select_fusion.11.refs_5_), channel_id=1, source_target_pairs={{0,16},{4,20},{8,24},{12,28},{16,0},{20,4},{24,8},{28,12},{1,17},{... | collective-permute-start | bytes 589832 | tf_op jit(solution)/shard_map/ppermute | solution.py:557
  253.1 12.9 %collective-permute-start.30 = (bf16[96,1024]{1,0:T(8,128)(2,1)S(1)}, bf16[96,1024]{1,0:T(8,128)(2,1)}, u32[]{:S(2)}, u32[]{:S(2)}) collective-permute-start(bf16[96,1024]{1,0:T(8,128)(2,1)S(1)} %broadcast_select_fusion.14.refs_4_), channel_id=1, source_target_pairs={{0,8},{4,12},{8,0},{12,4},{16,24},{20,28},{24,16},{28,20},{1,9},{5... | collective-permute-start | bytes 589832 | tf_op jit(solution)/shard_map/ppermute | solution.py:557
  262.3 24.9 %collective-permute-start.41 = (bf16[64,1024]{1,0:T(8,128)(2,1)S(1)}, bf16[64,1024]{1,0:T(8,128)(2,1)S(1)}, u32[]{:S(2)}, u32[]{:S(2)}) collective-permute-start(bf16[64,1024]{1,0:T(8,128)(2,1)S(1)} %broadcast_select_fusion.17), channel_id=1, source_target_pairs={{0,16},{4,20},{8,24},{12,28},{16,0},{20,4},{24,8},{28,12},{1,17},{... | collective-permute-start | bytes 393224 | tf_op jit(solution)/shard_map/ppermute | solution.py:557
  263.7 40.8 %copy-start.20 = (bf16[384,1024]{1,0:T(8,128)(2,1)S(1)}, bf16[384,1024]{1,0:T(8,128)(2,1)}, u32[]{:S(2)}) copy-start(bf16[384,1024]{1,0:T(8,128)(2,1)} %refs_0_.7) | copy-start | bytes 2359300
  263.7 40.8 %copy-start.56 = (bf16[384,1024]{1,0:T(8,128)(2,1)S(1)}, bf16[384,1024]{1,0:T(8,128)(2,1)}, u32[]{:S(2)}) copy-start(bf16[384,1024]{1,0:T(8,128)(2,1)} %copy-done.55) | copy-start | bytes 2359300
  263.7 40.8 %copy-start.71 = (f32[1024]{0:T(1024)S(1)}, f32[1024]{0:T(1024)}, u32[]{:S(2)}) copy-start(f32[1024]{0:T(1024)} %param.18) | copy-start | bytes 12292
  263.8 8.3 %collective-permute-start.37 = (bf16[48,1024]{1,0:T(8,128)(2,1)S(1)}, bf16[48,1024]{1,0:T(8,128)(2,1)S(1)}, u32[]{:S(2)}, u32[]{:S(2)}) collective-permute-start(bf16[48,1024]{1,0:T(8,128)(2,1)S(1)} %broadcast_select_fusion.20), channel_id=1, source_target_pairs={{0,4},{4,0},{8,12},{12,8},{16,20},{20,16},{24,28},{28,24},{1,5},{5... | collective-permute-start | bytes 294920 | tf_op jit(solution)/shard_map/ppermute | solution.py:557
  267.0 20.2 %collective-permute-start.32 = (bf16[48,1024]{1,0:T(8,128)(2,1)S(1)}, bf16[48,1024]{1,0:T(8,128)(2,1)S(1)}, u32[]{:S(2)}, u32[]{:S(2)}) collective-permute-start(bf16[48,1024]{1,0:T(8,128)(2,1)S(1)} %broadcast_select_fusion.23), channel_id=1, source_target_pairs={{0,16},{4,20},{8,24},{12,28},{16,0},{20,4},{24,8},{28,12},{1,17},{... | collective-permute-start | bytes 294920 | tf_op jit(solution)/shard_map/ppermute | solution.py:557
  272.1 16.9 %collective-permute-start.38 = (bf16[48,1024]{1,0:T(8,128)(2,1)S(1)}, bf16[48,1024]{1,0:T(8,128)(2,1)S(1)}, u32[]{:S(2)}, u32[]{:S(2)}) collective-permute-start(bf16[48,1024]{1,0:T(8,128)(2,1)S(1)} %add_convert_fusion.10), channel_id=1, source_target_pairs={{0,4},{4,0},{8,12},{12,8},{16,20},{20,16},{24,28},{28,24},{1,5},{5... | collective-permute-start | bytes 294920 | tf_op jit(solution)/shard_map/ppermute | solution.py:557
  287.2 10.1 %collective-permute-start.33 = (bf16[48,1024]{1,0:T(8,128)(2,1)S(1)}, bf16[48,1024]{1,0:T(8,128)(2,1)S(1)}, u32[]{:S(2)}, u32[]{:S(2)}) collective-permute-start(bf16[48,1024]{1,0:T(8,128)(2,1)S(1)} %add_convert_fusion.11), channel_id=1, source_target_pairs={{0,16},{4,20},{8,24},{12,28},{16,0},{20,4},{24,8},{28,12},{1,17},{... | collective-permute-start | bytes 294920 | tf_op jit(solution)/shard_map/ppermute | solution.py:557
  287.3 10.0 %collective-permute-start.42 = (bf16[32,1024]{1,0:T(8,128)(2,1)S(1)}, bf16[32,1024]{1,0:T(8,128)(2,1)S(1)}, u32[]{:S(2)}, u32[]{:S(2)}) collective-permute-start(bf16[32,1024]{1,0:T(8,128)(2,1)S(1)} %broadcast_select_fusion.26), channel_id=1, source_target_pairs={{0,4},{4,0},{8,12},{12,8},{16,20},{20,16},{24,28},{28,24},{1,5},{5... | collective-permute-start | bytes 196616 | tf_op jit(solution)/shard_map/ppermute | solution.py:557
  289.1 15.3 %collective-permute-start.39 = (bf16[96,1024]{1,0:T(8,128)(2,1)S(1)}, bf16[96,1024]{1,0:T(8,128)(2,1)S(1)}, u32[]{:S(2)}, u32[]{:S(2)}) collective-permute-start(bf16[96,1024]{1,0:T(8,128)(2,1)S(1)} %pad_maximum_fusion.7), channel_id=1, source_target_pairs={{0,16},{4,20},{8,24},{12,28},{16,0},{20,4},{24,8},{28,12},{1,17},{... | collective-permute-start | bytes 589832 | tf_op jit(solution)/shard_map/ppermute | solution.py:557
  297.3 6.9 %collective-permute-start.43 = (bf16[32,1024]{1,0:T(8,128)(2,1)S(1)}, bf16[32,1024]{1,0:T(8,128)(2,1)S(1)}, u32[]{:S(2)}, u32[]{:S(2)}) collective-permute-start(bf16[32,1024]{1,0:T(8,128)(2,1)S(1)} %add_convert_fusion.12), channel_id=1, source_target_pairs={{0,4},{4,0},{8,12},{12,8},{16,20},{20,16},{24,28},{28,24},{1,5},{5... | collective-permute-start | bytes 196616 | tf_op jit(solution)/shard_map/ppermute | solution.py:557
  301.4 21.7 %collective-permute-start.34 = (bf16[96,1024]{1,0:T(8,128)(2,1)S(1)}, bf16[96,1024]{1,0:T(8,128)(2,1)S(1)}, u32[]{:S(2)}, u32[]{:S(2)}) collective-permute-start(bf16[96,1024]{1,0:T(8,128)(2,1)S(1)} %pad_maximum_fusion.6), channel_id=1, source_target_pairs={{0,8},{4,12},{8,0},{12,4},{16,24},{20,28},{24,16},{28,20},{1,9},{5... | collective-permute-start | bytes 589832 | tf_op jit(solution)/shard_map/ppermute | solution.py:557
  304.3 21.4 %collective-permute-start.44 = (bf16[64,1024]{1,0:T(8,128)(2,1)S(1)}, bf16[64,1024]{1,0:T(8,128)(2,1)S(1)}, u32[]{:S(2)}, u32[]{:S(2)}) collective-permute-start(bf16[64,1024]{1,0:T(8,128)(2,1)S(1)} %pad_maximum_fusion.8), channel_id=1, source_target_pairs={{0,16},{4,20},{8,24},{12,28},{16,0},{20,4},{24,8},{28,12},{1,17},{... | collective-permute-start | bytes 393224 | tf_op jit(solution)/shard_map/ppermute | solution.py:557
  308.3 1.6 collective-permute-start.46
  308.4 50.7 %collective-permute-start.40 = (bf16[192,1024]{1,0:T(8,128)(2,1)S(1)}, bf16[192,1024]{1,0:T(8,128)(2,1)S(1)}, u32[]{:S(2)}, u32[]{:S(2)}) collective-permute-start(bf16[192,1024]{1,0:T(8,128)(2,1)S(1)} %pad_maximum_fusion.4), channel_id=1, source_target_pairs={{0,8},{4,12},{8,0},{12,4},{16,24},{20,28},{24,16},{28,20},{1,9},{5... | collective-permute-start | bytes 1179656 | tf_op jit(solution)/shard_map/ppermute | solution.py:557
  309.9 13.3 %collective-permute-start.47 = (f32[4224]{0:T(1024)S(1)}, f32[4224]{0:T(1024)S(1)}, u32[]{:S(2)}, u32[]{:S(2)}) collective-permute-start(f32[4224]{0:T(1024)S(1)} %add.232), channel_id=1, source_target_pairs={{0,2},{1,3},{2,0},{3,1},{4,6},{5,7},{6,4},{7,5},{8,10},{9,11},{10,... | collective-permute-start | bytes 50696 | tf_op jit(solution)/shard_map/ppermute | solution.py:557
  323.2 4.8 %collective-permute-start.48 = (f32[4224]{0:T(1024)S(1)}, f32[4224]{0:T(1024)S(1)}, u32[]{:S(2)}, u32[]{:S(2)}) collective-permute-start(f32[4224]{0:T(1024)S(1)} %add.233), channel_id=1, source_target_pairs={{0,4},{4,0},{8,12},{12,8},{16,20},{20,16},{24,28},{28,24},{1,5},{5... | collective-permute-start | bytes 50696 | tf_op jit(solution)/shard_map/ppermute | solution.py:557
  323.6 35.7 %collective-permute-start.35 = (bf16[192,1024]{1,0:T(8,128)(2,1)S(1)}, bf16[192,1024]{1,0:T(8,128)(2,1)S(1)}, u32[]{:S(2)}, u32[]{:S(2)}) collective-permute-start(bf16[192,1024]{1,0:T(8,128)(2,1)S(1)} %pad_maximum_fusion.3), channel_id=1, source_target_pairs={{0,4},{4,0},{8,12},{12,8},{16,20},{20,16},{24,28},{28,24},{1,5},{5... | collective-permute-start | bytes 1179656 | tf_op jit(solution)/shard_map/ppermute | solution.py:557
  327.9 19.8 %collective-permute-start.49 = (f32[4224]{0:T(1024)S(1)}, f32[4224]{0:T(1024)S(1)}, u32[]{:S(2)}, u32[]{:S(2)}) collective-permute-start(f32[4224]{0:T(1024)S(1)} %add.234), channel_id=1, source_target_pairs={{0,8},{4,12},{8,0},{12,4},{16,24},{20,28},{24,16},{28,20},{1,9},{5... | collective-permute-start | bytes 50696 | tf_op jit(solution)/shard_map/ppermute | solution.py:557
  347.8 5.3 %collective-permute-start.50 = (f32[4224]{0:T(1024)S(1)}, f32[4224]{0:T(1024)S(1)}, u32[]{:S(2)}, u32[]{:S(2)}) collective-permute-start(f32[4224]{0:T(1024)S(1)} %add.235), channel_id=1, source_target_pairs={{0,16},{4,20},{8,24},{12,28},{16,0},{20,4},{24,8},{28,12},{1,17},{... | collective-permute-start | bytes 50696 | tf_op jit(solution)/shard_map/ppermute | solution.py:557
  348.2 9.7 %collective-permute-start.45 = (bf16[128,1024]{1,0:T(8,128)(2,1)S(1)}, bf16[128,1024]{1,0:T(8,128)(2,1)S(1)}, u32[]{:S(2)}, u32[]{:S(2)}) collective-permute-start(bf16[128,1024]{1,0:T(8,128)(2,1)S(1)} %pad_maximum_fusion.5), channel_id=1, source_target_pairs={{0,8},{4,12},{8,0},{12,4},{16,24},{20,28},{24,16},{28,20},{1,9},{5... | collective-permute-start | bytes 786440 | tf_op jit(solution)/shard_map/ppermute | solution.py:557
  (88 other events, 480.1 us)
Sparse Core Ops, SparseCore 0:
  142.1 87.1 reduce-scatter.1
  248.3 106.8 all-gather.1

commit v2 on v1

--- a/solution.py
+++ b/solution.py
@@ -9,7 +9,6 @@
 
 D = 1024
 HEAD = 64
-CHUNK = 384
 CROP_MAX = 3072
 PACK = HEAD + 16
 
@@ -81,24 +80,56 @@
     return [slice(i, i + ROW_TILE) for i in range(0, rows, ROW_TILE)]
 
 
-def kernel(body, name, out_shape, in_specs, megabytes, scratch=(), aliases=None, tokens=()):
+class Incoming:
+    def __init__(self, buffer, copy):
+        self.buffer, self.copy, self.shape = buffer, copy, buffer.shape
+        copy.start()
+
+    def here(self):
+        if self.copy is not None:
+            self.copy.wait()
+            self.copy = None
+        return self.buffer
+
+    def __getitem__(self, index):
+        return self.here()[index]
+
+
+def kernel(body, name, out_shape, in_specs, megabytes, scratch=(), aliases=None, tokens=(), far=()):
     outs = vmem() if not isinstance(out_shape, tuple) else (vmem(),) * len(out_shape)
+    made = 1 if not isinstance(out_shape, tuple) else len(out_shape)
     count = len(in_specs)
-
-    def run(*refs):
-        body(*refs[:count], *refs[count + len(tokens) :])
-
-    call = pl.pallas_call(
-        run,
-        out_shape=out_shape,
-        in_specs=in_specs + [pl.BlockSpec(memory_space=pl.ANY)] * len(tokens),
-        out_specs=outs,
-        scratch_shapes=list(scratch),
-        input_output_aliases=aliases or {},
-        compiler_params=pltpu.CompilerParams(vmem_limit_bytes=megabytes << 20),
-        name=name,
-    )
-    return lambda *args: call(*args, *tokens)
+    specs = [pl.BlockSpec(memory_space=pl.ANY) if i in far else spec for i, spec in enumerate(in_specs)]
+    skip = pl.BlockSpec(memory_space=pl.ANY)
+
+    def call(*args):
+        buffers = [pltpu.VMEM(args[i].shape, args[i].dtype) for i in far]
+
+        def run(*refs):
+            given = list(refs[:count])
+            rest = refs[count + len(tokens) :]
+            results, own, copied = rest[:made], rest[made : made + len(scratch)], rest[made + len(scratch) :]
+            arriving = []
+            for n, i in enumerate(far):
+                given[i] = Incoming(copied[n], pltpu.make_async_copy(given[i], copied[n], copied[-1].at[n]))
+                arriving.append(given[i])
+            body(*given, *results, *own)
+            for value in arriving:
+                value.here()
+
+        sems = [pltpu.SemaphoreType.DMA((len(far),))] if far else []
+        return pl.pallas_call(
+            run,
+            out_shape=out_shape,
+            in_specs=specs + [skip] * len(tokens),
+            out_specs=outs,
+            scratch_shapes=list(scratch) + buffers + sems,
+            input_output_aliases=aliases or {},
+            compiler_params=pltpu.CompilerParams(vmem_limit_bytes=(60 if far else megabytes) << 20),
+            name=name,
+        )(*args, *tokens)
+
+    return call
 
 
 def normal(values):
@@ -183,7 +214,7 @@
     call = kernel(
         middle_back_body, "norm_two_back",
         (shape(rows, D, BF), shape(1, D, F32), shape(1, D, F32)),
-        [vmem()] * (3 + len(parts)), 9, tokens=tokens,
+        [vmem()] * (3 + len(parts)), 9, tokens=tokens, far=(0, 1) + tuple(range(3, 3 + len(parts))),
     )
     return call(grad, middle, gain, *parts)
 
@@ -233,7 +264,8 @@
     return call(middle, *parts)
 
 
-def decode(code):
+def decode(row):
+    code = jnp.broadcast_to(row, (128, row.shape[1])).T[:, 0:1]
     return code >> 1, (code & 1).astype(F32)
 
 
@@ -242,15 +274,22 @@
         yield i, slice(i * rows, (i + 1) * rows), slice((2 * pair + i) * rows, (2 * pair + i + 1) * rows)
 
 
+def keep_made(pair, rows, made, refs):
+    done = 2 * pair * rows
+    for old_ref, new_ref in zip(made, refs):
+        new_ref[0:done, :] = old_ref[0:done, :]
+
+
 def qkv_body(pair, tail_ref, xa_ref, xb_ref, w_ref, code_ref, was_ref, *rest):
     q_ref, k_ref, v_ref, pack_ref = rest[-4:]
+    keep_made(pair, xa_ref.shape[0], rest[:-4], rest[-4:-1])
     width = q_ref.shape[1]
     block = same_head(width)
     state, sums = was_ref[0:HEAD, :], was_ref[HEAD:PACK, :]
     for i, _, at in pair_slices(pair, xa_ref.shape[0]):
         x = (xa_ref, xb_ref)[i][...]
         q_ref[at, :] = feature(nn(x, w_ref[0])).astype(BF)
-        segment, valid = decode(code_ref[at, :])
+        segment, valid = decode(code_ref[2 * pair + i])
         k = (feature(nn(x, w_ref[1])) * valid).astype(BF)
         v = nn(x, w_ref[2]).astype(BF)
         k_ref[at, :] = k
@@ -262,13 +301,13 @@
     pack_ref[HEAD:PACK, :] = sums
 
 
-def project_qkv(pair, tail, xa, xb, w, code, was, made):
-    width, whole = w.shape[2], code.shape[0]
+def project_qkv(pair, tail, xa, xb, w, code, was, made, tokens=()):
+    width, whole = w.shape[2], code.shape[0] * code.shape[2]
     call = kernel(
         functools.partial(qkv_body, pair), "project_qkv",
         (shape(whole, width, BF),) * 3 + (shape(PACK, width, F32),),
         [smem()] + [vmem()] * (5 + len(made)), 8,
-        aliases={6 + i: i for i in range(len(made))},
+        aliases={6 + i: i for i in range(len(made))}, tokens=tokens,
     )
     return call(tail, xa, xb, w, code, was, *made)
 
@@ -280,10 +319,10 @@
 
 
 def forward_body(
-    last_ref, spot_ref, q_ref, k_ref, v_ref, code_ref, segr_ref, num_ref, den_ref, st_ref, ks_ref
+    last_ref, spot_ref, q_ref, k_ref, v_ref, code_ref, num_ref, den_ref, st_ref, ks_ref
 ):
     rows, width = q_ref.shape
-    size = CHUNK
+    size = code_ref.shape[2]
     block = same_head(width)
     ones_block = block.astype(BF)
     lanes = lane_head(size, width)
@@ -296,8 +335,8 @@
         spot = spot_ref[c]
         at = pl.ds(pl.multiple_of(spot * size, size), size)
         q, k, v = q_ref[at, :], k_ref[at, :], v_ref[at, :]
-        seg = decode(code_ref[at, :])[0]
-        keep = (lower & (seg == segr_ref[spot])).astype(BF)
+        seg = decode(code_ref[spot])[0]
+        keep = (lower & (seg == code_ref[spot] >> 1)).astype(BF)
         before, after = last_ref[c], last_ref[c + 1]
         carried = (seg == before).astype(F32)
         sums = [jnp.zeros((size, width), F32)] * 2
@@ -319,13 +358,13 @@
     lax.fori_loop(0, rows // size, step, 0)
 
 
-def attend(last, spot, q, k, v, code, segr):
+def attend(last, spot, q, k, v, code):
     rows, width = q.shape
     call = kernel(
-        forward_body, "attend", (shape(rows, width, F32),) * 2, [smem()] * 2 + [vmem()] * 5, 8,
+        forward_body, "attend", (shape(rows, width, F32),) * 2, [smem()] * 2 + [vmem()] * 4, 8,
         scratch=[pltpu.VMEM((width, width), F32), pltpu.VMEM((8, width), F32)],
     )
-    return call(last, spot, q, k, v, code, segr)
+    return call(last, spot, q, k, v, code)
 
 
 def project_body(
@@ -338,7 +377,7 @@
     sums = pack_ref[HEAD : HEAD + 1, :]
     for i, own, at in pair_slices(pair, a_ref.shape[0]):
         q = q_ref[at, :]
-        segment, valid = decode(code_ref[at, :])
+        segment, valid = decode(code_ref[2 * pair + i])
         opening = (segment == first_ref[0]).astype(F32)
         num = num_ref[at, :] + opening * nn(q, state)
         den = den_ref[at, :] + opening * nn((q.astype(F32) * sums).astype(BF), block.astype(BF))
@@ -393,6 +432,7 @@
     pair, first_ref, ga_ref, gb_ref, w_ref, heads_ref, rinv_ref, q_ref, code_ref, was_ref, *rest
 ):
     ng_ref, dg_ref, pack_ref = rest[-3:]
+    keep_made(pair, ga_ref.shape[0], rest[:-3], rest[-3:-1])
     width = q_ref.shape[1]
     block = same_head(width)
     ones_block = block.astype(BF)
@@ -407,7 +447,7 @@
         dg = -(nn(high, ones_block) + nn(low, ones_block)) * rinv
         ng_ref[at, :] = ng
         dg_ref[at, :] = dg
-        opened = pick(decode(code_ref[at, :])[0] == first_ref[0], q_ref[at, :])
+        opened = pick(decode(code_ref[2 * pair + i])[0] == first_ref[0], q_ref[at, :])
         state = state + fold_heads(pick(block, tn(opened, ng)), width)
         sums = sums + jnp.sum(opened.astype(F32) * dg, axis=0, keepdims=True)
     pack_ref[0:HEAD, :] = state
@@ -426,11 +466,11 @@
 
 
 def backward_body(
-    last_ref, spot_ref, q_ref, k_ref, v_ref, ng_ref, dg_ref, code_ref, segr_ref, pack_ref,
+    last_ref, spot_ref, q_ref, k_ref, v_ref, ng_ref, dg_ref, code_ref, pack_ref,
     dq_ref, dk_ref, dv_ref, all_ref, sums_ref, st_ref, ks_ref
 ):
     rows, width = q_ref.shape
-    size = CHUNK
+    size = code_ref.shape[2]
     count = rows // size
     block = same_head(width)
     lanes = lane_head(size, width)
@@ -438,19 +478,21 @@
     lower = causal(size)
     st_ref[...] = spread_heads(pack_ref[0:HEAD, :], width, block)
     ks_ref[...] = jnp.broadcast_to(pack_ref[HEAD : HEAD + 1, :], ks_ref.shape)
+    k_ref, v_ref = k_ref.here(), v_ref.here()
 
     def collect(c, carry):
         at = pl.ds(pl.multiple_of(spot_ref[c] * size, size), size)
         all_ref[c] = st_ref[...].astype(BF)
         sums_ref[c] = ks_ref[...]
         before, after = last_ref[c], last_ref[c + 1]
-        kept = pick(decode(code_ref[at, :])[0] == after, k_ref[at, :])
+        kept = pick(decode(code_ref[spot_ref[c]])[0] == after, k_ref[at, :])
         cont = (before == after).astype(F32)
         st_ref[...] = cont * st_ref[...] + pick(block, tn(kept, v_ref[at, :]))
         ks_ref[...] = cont * ks_ref[...] + jnp.sum(kept.astype(F32), axis=0, keepdims=True)
         return carry
 
     lax.fori_loop(0, count, collect, 0)
+    q_ref, ng_ref, dg_ref = q_ref.here(), ng_ref.here(), dg_ref.here()
     st_ref[...] = jnp.zeros_like(st_ref)
     ks_ref[...] = jnp.zeros_like(ks_ref)
 
@@ -459,8 +501,8 @@
         spot = spot_ref[c]
         at = pl.ds(pl.multiple_of(spot * size, size), size)
         q, k, v, ng, dg = q_ref[at, :], k_ref[at, :], v_ref[at, :], ng_ref[at, :], dg_ref[at, :]
-        seg = decode(code_ref[at, :])[0]
-        keep = (lower & (seg == segr_ref[spot])).astype(BF)
+        seg = decode(code_ref[spot])[0]
+        keep = (lower & (seg == code_ref[spot] >> 1)).astype(BF)
         before, after = last_ref[c], last_ref[c + 1]
         opened = seg == before
         carried = opened.astype(F32)
@@ -494,13 +536,13 @@
     lax.fori_loop(0, count, step, 0)
 
 
-def attend_back(last, spot, q, k, v, ng, dg, code, segr, pack, tokens):
+def attend_back(last, spot, q, k, v, ng, dg, code, pack, tokens):
     rows, width = q.shape
-    count = rows // CHUNK
+    count = code.shape[0]
     call = kernel(
         backward_body, "attend_back",
         (shape(rows, width, BF),) * 3,
-        [smem()] * 2 + [vmem()] * 8, 12,
+        [smem()] * 2 + [vmem()] * 7, 12, far=(3, 4, 2, 5, 6),
         scratch=[
             pltpu.VMEM((count, width, width), BF),
             pltpu.VMEM((count, 8, width), F32),
@@ -509,38 +551,35 @@
         ],
         tokens=tokens,
     )
-    return call(last, spot, q, k, v, ng, dg, code, segr, pack)
-
-
-def mix_body(
-    pair, tail_ref, dq_ref, dk_ref, dv_ref, k_ref, v_ref, code_ref, pack_ref, w_ref,
-    mixed_ref, a_ref, b_ref
-):
+    return call(last, spot, q, k, v, ng, dg, code, pack)
+
+
+def mix_body(tail_ref, dq_ref, dk_ref, dv_ref, k_ref, v_ref, code_ref, pack_ref, w_ref, mixed_ref, *part_refs):
     width = k_ref.shape[1]
+    rows = part_refs[0].shape[0]
     block = same_head(width)
     state = spread_heads(pack_ref[0:HEAD, :], width, block).astype(BF)
     sums = pack_ref[HEAD : HEAD + 1, :]
-    for i, own, at in pair_slices(pair, a_ref.shape[0]):
-        tail = (decode(code_ref[at, :])[0] == tail_ref[0]).astype(F32)
+    for i, part_ref in enumerate(part_refs):
+        at = slice(i * rows, (i + 1) * rows)
+        tail = (decode(code_ref[i])[0] == tail_ref[0]).astype(F32)
         k = k_ref[at, :]
         dk = dk_ref[at, :].astype(F32) + tail * (nt(v_ref[at, :], state) + sums)
         dv = dv_ref[at, :].astype(F32) + tail * nn(k, state)
         dq = dq_ref[at, :]
         dk = (dk * jnp.minimum(k.astype(F32), 1.0)).astype(BF)
         dv = dv.astype(BF)
-        mixed_ref[own, 0:width] = dq
-        mixed_ref[own, width : 2 * width] = dk
-        mixed_ref[own, 2 * width : 3 * width] = dv
-        out = nt(dq, w_ref[0]) + nt(dk, w_ref[1]) + nt(dv, w_ref[2])
-        (a_ref, b_ref)[i][...] = out.astype(BF)
-
-
-def mix(pair, rows, tail, dq, dk, dv, k, v, code, pack, w, tokens):
-    width = k.shape[1]
-    call = kernel(
-        functools.partial(mix_body, pair), "mix",
-        (shape(2 * rows, 3 * width, BF),) + (shape(rows, D, BF),) * 2,
-        [smem()] + [vmem()] * 8, 8, tokens=tokens,
+        mixed_ref[at, 0:width] = dq
+        mixed_ref[at, width : 2 * width] = dk
+        mixed_ref[at, 2 * width : 3 * width] = dv
+        part_ref[...] = (nt(dq, w_ref[0]) + nt(dk, w_ref[1]) + nt(dv, w_ref[2])).astype(BF)
+
+
+def mix(rows, tail, dq, dk, dv, k, v, code, pack, w):
+    whole, width = k.shape
+    call = kernel(
+        mix_body, "mix", (shape(whole, 3 * width, BF),) + (shape(rows, D, BF),) * (whole // rows),
+        [smem()] + [vmem()] * 8, 8, far=(4, 1, 2, 5, 3, 8),
     )
     return call(tail, dq, dk, dv, k, v, code, pack, w)
 
@@ -650,16 +689,23 @@
     return lax.ppermute(pack, "rows", pairs)
 
 
-def gather_carry(pack, crops_at, here, groups, reach, reverse):
-    total = jnp.zeros(pack.shape, F32)
+def reached(crops_at, here, groups, reach, reverse):
     mine = crops_at[here + 1] if reverse else crops_at[here]
+    flags = []
     for hop in range(1, reach + 1):
-        got = shifted(pack, hop, groups, reverse).astype(F32)
         other = here + hop if reverse else here - hop
         inside = (other < groups) if reverse else (other >= 0)
         at = jnp.clip(other, 0, groups - 1)
         theirs = crops_at[at] if reverse else crops_at[at + 1]
-        total = total + jnp.where(inside & (theirs == mine), got, 0.0)
+        flags.append((inside & (theirs == mine)).astype(F32))
+    return jnp.stack(flags)
+
+
+def gather_carry(pack, flags, groups, reverse):
+    total = jnp.zeros(pack.shape, F32)
+    for i in range(flags.shape[0]):
+        got = shifted(pack, i + 1, groups, reverse).astype(F32)
+        total = total + jnp.where(flags[i] > 0, got, 0.0)
     return total
 
 
@@ -705,32 +751,30 @@
     pixel_valid = (mask * inside).astype(F32)
     edges = jnp.arange(groups + 1, dtype=jnp.int32) * group_rows - 1
     crops_at = jnp.sum((crop_offsets[None, :] <= edges[:, None]).astype(jnp.int32), axis=1) - 1
-    chunks = group_rows // CHUNK
-    per = local_rows // CHUNK
-    chunk_edges = group_start - 1 + jnp.arange(chunks + 1, dtype=jnp.int32) * CHUNK
+    chunk_edges = group_start - 1 + jnp.arange(members + 1, dtype=jnp.int32) * local_rows
     last = jnp.sum((crop_offsets[None, :] <= chunk_edges[:, None]).astype(jnp.int32), axis=1) - 1
     tail = last[-1:]
-    order = jnp.arange(chunks, dtype=jnp.int32)
-    spot = ((order // per) ^ member) * per + order % per
-    code = (segment * 2 + mask * inside)[:, None]
-    segr = segment.reshape(chunks, 1, CHUNK)
+    spot = slot_ids
+    code = (segment * 2 + mask * inside).reshape(members, 1, local_rows)
     validc = pixel_valid[:, None]
     gain1, bias1, gain2, bias2 = (
         a[None, :] for a in (norm1_gain, norm1_bias, norm2_gain, norm2_bias)
     )
     no_pack = jnp.zeros((PACK, width), F32)
+    before = reached(crops_at, here, groups, reach, False)
+    behind = reached(crops_at, here, groups, reach, True)
 
     normed_slots = gather_begin(norm_one(pixels, gain1, bias1))
     grad_slots = gather_begin(after(out_grad, normed_slots[members // 2]))
-    *made, pack = project_qkv(0, tail, normed_slots[0], normed_slots[1], qkv_weight, code, no_pack, ())
+    *made, pack = project_qkv(0, tail, normed_slots[0], normed_slots[1], qkv_weight, code, no_pack, (), [before, behind, spot])
     normed_slots = gather_end(normed_slots, pack)
     for p in range(1, pairs):
         *made, pack = project_qkv(
             p, tail, normed_slots[2 * p], normed_slots[2 * p + 1], qkv_weight, code, pack, made
         )
     q, k, v = made
-    carry = gather_carry(pack.astype(BF), crops_at, here, groups, reach, False)
-    num, den = attend(last, spot, q, k, v, code, segr)
+    carry = gather_carry(pack.astype(BF), before, groups, False)
+    num, den = attend(last, spot, q, k, v, code)
     grad_slots = gather_end(grad_slots, num)
     sent = {
         p: project(
@@ -751,6 +795,7 @@
     acts, hids, twos = after(
         ([h[0] for h in hidden], [h[1] for h in hidden], two_slots), two_sums[members - 2]
     )
+    hids = after(hids, two_sums[0][1], branch_sums[0][1], branch_sums[members - 2])
     down_grad = tn(jnp.concatenate(acts, axis=0), jnp.concatenate(grad_slots, axis=0)).astype(BF)
     up_grad = tn(jnp.concatenate(twos, axis=0), jnp.concatenate(hids, axis=0)).astype(BF)
     bits = bits_of(groups)
@@ -773,26 +818,24 @@
             sent[p][0], sent[p][1], q, code, grad_pack, made
         )
     ng, dg = made
-    grad_carry = gather_carry(grad_pack.astype(BF), crops_at, here, groups, reach, True)
-    dq, dk, dv = attend_back(last, spot, q, k, v, ng, dg, code, segr, carry, [])
-    mixes = {
-        p: mix(p, local_rows, tail, dq, dk, dv, k, v, code, grad_carry, qkv_weight, [])
-        for p in reversed(range(pairs))
-    }
-    normed_sums = scatter_begin([mixes[s // 2][1 + s % 2] for s in range(members)])
+    grad_carry = gather_carry(grad_pack.astype(BF), behind, groups, True)
+    heads_all = jnp.concatenate([sent[p][0] for p in range(pairs)], axis=0)
+    out_weight_grad = tn(heads_all, jnp.concatenate(middle_slots, axis=0))
+    out_sum = RowSum(out_weight_grad.astype(BF), turned)
+    dq, dk, dv = attend_back(last, spot, q, k, v, ng, dg, code, carry, [out_sum.sent])
+    out_sum.next(dq)
+    mixed_grad, *mixed_parts = mix(local_rows, tail, dq, dk, dv, k, v, code, grad_carry, qkv_weight)
+    normed_sums = scatter_begin(mixed_parts)
     normed_parts = scatter_end(normed_sums)
-    mixed_grad = jnp.concatenate([mixes[p][0] for p in range(pairs)], axis=0)
     qkv_grad = tn(mixed_grad, jnp.concatenate(normed_slots, axis=0)).astype(BF)
     both = lax.all_gather(after(both, dq), "rows", axis=0, tiled=True)
     down_grad = both[: down_grad.shape[0]].astype(F32)
     up_grad = both[down_grad.shape[0] :].reshape(up_grad.shape).astype(F32)
+    out_sum.next(mixed_grad)
     cut = 3 * width // 2
     low_sum = RowSum(qkv_grad[:cut], bits)
     high_sum = RowSum(qkv_grad[cut:], turned)
     normed_sent = normed_sums[members - 2]
-    heads_all = jnp.concatenate([sent[p][0] for p in range(pairs)], axis=0)
-    out_weight_grad = tn(after(heads_all, low_sum.sent, normed_sent), jnp.concatenate(middle_slots, axis=0))
-    out_sum = RowSum(out_weight_grad.astype(BF), turned)
     tokens = [low_sum.next(normed_sent), high_sum.next(normed_sent)]
     output, result_square, branch_square = finish(middle, branch_parts, tokens)
     pixels_grad, gain1_grad, bias1_grad = norm_one_back(pixels, middle_low, gain1, normed_parts)

time: 383 us -> 369 us (0.963)
  local copies, waits for them, and re-layouts: 53.3 us -> 35.8 us
  starting transfers between devices: 61.7 us -> 47.7 us
  waiting for transfers between devices: 123 us -> 136 us
  Pallas kernels: 70.6 us -> 80.9 us
  other arithmetic: 31 us -> 24.4 us
    ppermute x47, starting transfers between devices: 52 us -> 38 us  [swap(): lax.ppermute(value, axis, [(i, i ^ bit) for i in range(lax.axis_size(axis...]
    ppermute x47, waiting for transfers between devices: 123 us -> 136 us  [swap(): lax.ppermute(value, axis, [(i, i ^ bit) for i in range(lax.axis_size(axis...]
    unnamed x202 -> x136, local copies, waits for them, and re-layouts: 41.4 us -> 29.9 us
    pallas_call x17 -> x16, Pallas kernels: 70.6 us -> 80.9 us  [call(): pl.pallas_call(run, out_shape=out_shape, in_specs=specs + [skip] * len(to...]
  transfers between devices with their start and end apart: 53 -> 53, of which waited for: 23 -> 23; matrix products, arithmetic and copies ran while one was open for 13% -> 11% of each run, Pallas kernels for 16% -> 19%
where the time goes in v2:
time: 369 us; the launch traced here: 363 us
  waiting for transfers between devices  136 us (37%)
  Pallas kernels  80.9 us (22%)
  starting transfers between devices  47.7 us (13%)
  local copies, waits for them, and re-layouts  35.8 us (10%)
  other arithmetic  24.4 us (7%)
  between operations  20.6 us (6%)
  matrix products  17.2 us (5%)
    ppermute x47, waiting for transfers between devices, swap(): lax.ppermute(value, axis, [(i, i ^ bit) for i in range(lax.axis_size(axis...  136 us
    pallas_call x16, Pallas kernels, call(): pl.pallas_call(run, out_shape=out_shape, in_specs=specs + [skip] * len(to...  80.9 us
    ppermute x47, starting transfers between devices, swap(): lax.ppermute(value, axis, [(i, i ^ bit) for i in range(lax.axis_size(axis...  38 us
    unnamed x136, local copies, waits for them, and re-layouts  29.9 us
    dot_general x4, matrix products, tn(): lax.dot_general(a, b, (((0,), (0,)), ((), ())), preferred_element_type=F32)  16.3 us
    ppermute x4, starting transfers between devices, shifted(): return lax.ppermute(pack, 'rows', pairs)  9.68 us
  transfers between devices with their start and end apart: 53, of which 23 were waited for; matrix products, arithmetic and copies ran while one was open for 11% of the time, Pallas kernels for 19%

profile of v2, /device:TPU:0, one launch (start us, length us, event | category | flops | bytes accessed | tf_op | source)
XLA Modules:
  0.0 362.5 jit_solution(10337821618163938665)
XLA Ops:
  9.9 1.4 norm_one.1.refs_1_
  11.7 2.5 collective-permute-start
  26.0 1.4 copy-done.1
  28.5 4.1 %project_qkv.2 = (bf16[1536,256]{1,0:T(8,128)(2,1)S(1)}, bf16[1536,256]{1,0:T(8,128)(2,1)S(1)}, bf16[1536,256]{1,0:T(8,128)(2,1)S(1)}, f32[80,256]{1,0:T(8,128)S(1)}) custom-call(s32[1]{0:T(128)} %slice.108.refs_0_, bf16[384,1024]{1,0:T(8,128)(2,1)} %norm_one.1.refs_1_, bf16[384,1024]{1,0:T(8,128)(2,1)S(1)} %copy-done.34, ...), custom_call_target="tpu_custom_call" | custom-call | tf_op jit(solution)/shard_map/project_qkv/pallas_call | solution.py:121
  32.9 1.7 collective-permute-start.5
  35.3 4.2 %project_qkv.3 = (bf16[1536,256]{1,0:T(8,128)(2,1)S(1)}, bf16[1536,256]{1,0:T(8,128)(2,1)S(1)}, bf16[1536,256]{1,0:T(8,128)(2,1)S(1)}, f32[80,256]{1,0:T(8,128)S(1)}) custom-call(s32[1]{0:T(128)} %slice.108.refs_0_, bf16[384,1024]{1,0:T(8,128)(2,1)} %collective-permute-done.refs_1_, ...), custom_call_target="tpu_custom_call", output_to_operand_aliasing={{0}: (6, {}), {1}: (7, {}), {2}: (8, {})} | custom-call | tf_op jit(solution)/shard_map/project_qkv/pallas_call | solution.py:121
  40.4 3.7 %collective-permute-start.4 = (bf16[80,256]{1,0:T(8,128)(2,1)S(1)}, bf16[80,256]{1,0:T(8,128)(2,1)S(1)}, u32[]{:S(2)}, u32[]{:S(2)}) collective-permute-start(bf16[80,256]{1,0:T(8,128)(2,1)S(1)} %convert_element_type.201), channel_id=1, source_target_pairs={{0,8},{4,12},{8,16},{12,20},{16,24},{20,28},{1,9},{5,13},{9,17},{1... | collective-permute-start | bytes 122888 | tf_op jit(solution)/shard_map/ppermute | solution.py:689
  44.1 3.4 collective-permute-start.3
  48.6 6.2 %attend.1 = (f32[1536,256]{1,0:T(8,128)S(1)}, f32[1536,256]{1,0:T(8,128)S(1)}) custom-call(s32[5]{0:T(128)S(1)} %broadcast_add_fusion.2.refs_0_, s32[4]{0:T(128)S(1)} %iota_xor_fusion.refs_8_.refs_1_, bf16[1536,256]{1,0:T(8,128)(2,1)S(1)} %get-tuple-element.100.refs_2_.refs_3_.refs_6_, bf16[1536,256]{1,0:T(8,128)(2,1)S(1)} %get-tuple-element.101.refs_3_.refs_4_, ...), custom_call_target="tpu_custom_call" | custom-call | tf_op jit(solution)/shard_map/attend/pallas_call | solution.py:121
  56.0 1.6 project.3
  58.5 1.6 project.2
  62.5 1.6 collective-permute-start.8
  64.0 17.9 %collective-permute-done.8.refs_5_ = bf16[384,1024]{1,0:T(8,128)(2,1)S(1)} collective-permute-done((bf16[384,1024]{1,0:T(8,128)(2,1)S(1)}, bf16[384,1024]{1,0:T(8,128)(2,1)S(1)}, u32[]{:S(2)}, u32[]{:S(2)}) %collective-permute-start.8) | collective-permute-done | bytes 786464 | tf_op jit(solution)/shard_map/ppermute | solution.py:596
  83.8 1.5 collective-permute-start.12
  86.1 8.9 %mlp.2 = (bf16[768,1024]{1,0:T(8,128)(2,1)S(1)}, bf16[768,1024]{1,0:T(8,128)(2,1)S(1)}, bf16[384,1024]{1,0:T(8,128)(2,1)S(1)}, bf16[384,1024]{1,0:T(8,128)(2,1)S...) custom-call(bf16[384,1024]{1,0:T(8,128)(2,1)S(1)} %get-tuple-element.129.refs_0_, ...), custom_call_target="tpu_custom_call" | custom-call | tf_op jit(solution)/shard_map/mlp/pallas_call | solution.py:121
  96.8 7.0 %collective-permute-done.12.refs_0_ = bf16[384,1024]{1,0:T(8,128)(2,1)S(1)} collective-permute-done((bf16[384,1024]{1,0:T(8,128)(2,1)S(1)}, bf16[384,1024]{1,0:T(8,128)(2,1)S(1)}, u32[]{:S(2)}, u32[]{:S(2)}) %collective-permute-start.12) | collective-permute-done | bytes 786464 | tf_op jit(solution)/shard_map/ppermute | solution.py:596
  103.8 2.3 collective-permute-done.13.refs_1_
  106.1 9.1 %mlp.3 = (bf16[768,1024]{1,0:T(8,128)(2,1)S(1)}, bf16[768,1024]{1,0:T(8,128)(2,1)S(1)}, bf16[384,1024]{1,0:T(8,128)(2,1)S(1)}, bf16[384,1024]{1,0:T(8,128)(2,1)S...) custom-call(bf16[384,1024]{1,0:T(8,128)(2,1)S(1)} %collective-permute-done.12.refs_0_, ...), custom_call_target="tpu_custom_call" | custom-call | tf_op jit(solution)/shard_map/mlp/pallas_call | solution.py:121
  116.2 1.3 collective-permute-done.17
  118.7 1.5 collective-permute-start.18
  120.2 1.3 add_convert_fusion.2.refs_9_
  121.5 5.3 %fusion.43.refs_6_ = bf16[1024,1024]{1,0:T(8,128)(2,1)S(1)} fusion(bf16[384,1024]{1,0:T(8,128)(2,1)S(1)} %collective-permute-done.14.refs_3_, bf16[384,1024]{1,0:T(8,128)(2,1)} %collective-permute-done.5.refs_7_.refs_2_, bf16[384,1024]{1,0:T(8,128)(2,1)S(1)} %collective-permute-done.10.refs_3_, bf16[384,1024]{1,0:T(8,128)(2,1)} %refs_0_.6, ...), kind=kOutput, calls=%fused_computation.42 | convolution fusion | flops 3241148416 | bytes 8388608 | tf_op jit(solution)/shard_map/dot_general | solution.py:29
  126.8 4.0 %fusion.38.refs_7_ = bf16[1024,1024]{1,0:T(8,128)(2,1)S(1)} fusion(bf16[768,1024]{1,0:T(8,128)(2,1)S(1)} %get-tuple-element.136, bf16[768,1024]{1,0:T(8,128)(2,1)S(1)} %get-tuple-element.135, bf16[384,1024]{1,0:T(8,128)(2,1)S(1)} %collective-permute-done.13.refs_1_, bf16[384,1024]{1,0:T(8,128)(2,1)S(1)} %collective-permute-done.12.refs_0_, ...), kind=kOutput, calls=%fused_computation.41 | convolution fusion | flops 3241148416 | bytes 8388608 | tf_op jit(solution)/shard_map/dot_general | solution.py:29
  130.9 1.3 copy-done.57
  132.2 2.5 pad_maximum_fusion
  134.6 4.0 %collective-permute-done.18.refs_5_ = bf16[384,1024]{1,0:T(8,128)(2,1)} collective-permute-done((bf16[384,1024]{1,0:T(8,128)(2,1)}, bf16[384,1024]{1,0:T(8,128)(2,1)}, u32[]{:S(2)}, u32[]{:S(2)}) %collective-permute-start.18) | collective-permute-done | bytes 786464 | tf_op jit(solution)/shard_map/ppermute | solution.py:596
  138.7 5.3 %norm_two_back.1 = (bf16[384,1024]{1,0:T(8,128)(2,1)}, f32[1,1024]{1,0:T(1,128)}, f32[1,1024]{1,0:T(1,128)}) custom-call(bf16[384,1024]{1,0:T(8,128)(2,1)} %refs_0_.6, bf16[384,1024]{1,0:T(8,128)(2,1)} %copy-done.15, f32[1,1024]{1,0:T(1,128)} %bitcast.21, bf16[384,1024]{1,0:T(8,128)(2,1)} %copy-done.29, bf16[384,1024]{1,0:T(8,128)(2,1)} %collective-permute-done.16.refs_4_, ...), custom_call_target="tpu_custom_call" | custom-call | tf_op jit(solution)/shard_map/norm_two_back/pallas_call | solution.py:121
  144.0 1.6 collective-permute-start.19
  146.5 1.4 copy-done.19
  148.9 2.3 heads_back.2
  153.3 10.9 %collective-permute-done.19.refs_1_ = bf16[384,1024]{1,0:T(8,128)(2,1)S(1)} collective-permute-done((bf16[384,1024]{1,0:T(8,128)(2,1)}, bf16[384,1024]{1,0:T(8,128)(2,1)S(1)}, u32[]{:S(2)}, u32[]{:S(2)}) %collective-permute-start.19) | collective-permute-done | bytes 786464 | tf_op jit(solution)/shard_map/ppermute | solution.py:596
  165.8 1.6 collective-permute-start.21
  167.4 1.4 copy-done.13
  173.0 3.2 heads_back.3
  178.9 1.3 collective-permute-start.24
  180.2 1.3 collective-permute-start.23
  181.5 2.2 fusion.51
  184.5 3.7 %collective-permute-start.31 = (bf16[128,1024]{1,0:T(8,128)(2,1)S(1)}, bf16[128,1024]{1,0:T(8,128)(2,1)S(1)}, u32[]{:S(2)}, u32[]{:S(2)}) collective-permute-start(bf16[128,1024]{1,0:T(8,128)(2,1)S(1)} %broadcast_select_fusion.8.refs_9_), channel_id=1, source_target_pairs={{0,8},{4,12},{8,0},{12,4},{16,24},{20,28},{24,16},{28,20},{1,9},{5... | collective-permute-start | bytes 786440 | tf_op jit(solution)/shard_map/ppermute | solution.py:596
  188.2 17.2 %attend_back.1 = (bf16[1536,256]{1,0:T(8,128)(2,1)}, bf16[1536,256]{1,0:T(8,128)(2,1)}, bf16[1536,256]{1,0:T(8,128)(2,1)}) custom-call(s32[5]{0:T(128)} %copy-done.49, s32[4]{0:T(128)} %copy-done.53, bf16[1536,256]{1,0:T(8,128)(2,1)} %copy-done, bf16[1536,256]{1,0:T(8,128)(2,1)} %copy-done.3, bf16[1536,256]{1,0:T(8,128)(2,1)} %copy-done.4, ...), custom_call_target="tpu_custom_call" | custom-call | tf_op jit(solution)/shard_map/attend_back/pallas_call | solution.py:121
  206.1 8.8 %mix.1 = (bf16[1536,768]{1,0:T(8,128)(2,1)}, bf16[384,1024]{1,0:T(8,128)(2,1)}, bf16[384,1024]{1,0:T(8,128)(2,1)}, bf16[384,1024]{1,0:T(8,128)(2,1)}, bf16[384,1024]{1,0:T(8,128)(2,1)}) custom-call(s32[1]{0:T(128)} %slice.108.refs_0_, bf16[1536,256]{1,0:T(8,128)(2,1)} %get-tuple-element.149.refs_1_, bf16[1536,256]{1,0:T(8,128)(2,1)} %get-tuple-element.150.refs_2_, ...), custom_call_target="tpu_custom_call" | custom-call | tf_op jit(solution)/shard_map/mix/pallas_call | solution.py:121
  215.0 4.8 %fusion.48 = bf16[768,1024]{1,0:T(8,128)(2,1)S(1)} fusion(bf16[1536,768]{1,0:T(8,128)(2,1)} %get-tuple-element.153, bf16[384,1024]{1,0:T(8,128)(2,1)S(1)} %copy-done.26, bf16[384,1024]{1,0:T(8,128)(2,1)} %collective-permute-done.refs_1_, bf16[384,1024]{1,0:T(8,128)(2,1)S(1)} %copy-done.35, bf16[384,1024]{1,0:T(8,128)(2,1)} %norm_one.1.refs_1_), kind=kOutput, calls=%fused_computation.43 | convolution fusion | flops 2429288448 | bytes 7077888 | tf_op jit(solution)/shard_map/dot_general | solution.py:29
  220.0 3.6 %collective-permute-start.32 = (bf16[64,1024]{1,0:T(8,128)(2,1)S(1)}, bf16[64,1024]{1,0:T(8,128)(2,1)S(1)}, u32[]{:S(2)}, u32[]{:S(2)}) collective-permute-start(bf16[64,1024]{1,0:T(8,128)(2,1)S(1)} %broadcast_select_fusion.17), channel_id=1, source_target_pairs={{0,16},{4,20},{8,24},{12,28},{16,0},{20,4},{24,8},{28,12},{1,17},{... | collective-permute-start | bytes 393224 | tf_op jit(solution)/shard_map/ppermute | solution.py:596
  225.1 6.8 %collective-permute-done.32 = bf16[64,1024]{1,0:T(8,128)(2,1)S(1)} collective-permute-done((bf16[64,1024]{1,0:T(8,128)(2,1)S(1)}, bf16[64,1024]{1,0:T(8,128)(2,1)S(1)}, u32[]{:S(2)}, u32[]{:S(2)}) %collective-permute-start.32) | collective-permute-done | bytes 131104 | tf_op jit(solution)/shard_map/ppermute | solution.py:596
  232.1 1.5 collective-permute-start.33
  233.6 2.5 add_convert_fusion
  236.0 1.7 collective-permute-done.27
  238.9 1.6 add_convert_fusion.4
  240.7 2.0 collective-permute-start.38
  242.7 2.6 finish.1
  246.5 1.5 collective-permute-start.43
  248.0 11.2 %collective-permute-done.30 = bf16[96,1024]{1,0:T(8,128)(2,1)} collective-permute-done((bf16[96,1024]{1,0:T(8,128)(2,1)S(1)}, bf16[96,1024]{1,0:T(8,128)(2,1)}, u32[]{:S(2)}, u32[]{:S(2)}) %collective-permute-start.30) | collective-permute-done | bytes 196640 | tf_op jit(solution)/shard_map/ppermute | solution.py:596
  261.2 1.6 collective-permute-start.39
  264.1 9.6 %collective-permute-done.34 = bf16[48,1024]{1,0:T(8,128)(2,1)S(1)} collective-permute-done((bf16[48,1024]{1,0:T(8,128)(2,1)S(1)}, bf16[48,1024]{1,0:T(8,128)(2,1)S(1)}, u32[]{:S(2)}, u32[]{:S(2)}) %collective-permute-start.34) | collective-permute-done | bytes 98336 | tf_op jit(solution)/shard_map/ppermute | solution.py:596
  275.0 6.1 %collective-permute-done.44 = bf16[64,1024]{1,0:T(8,128)(2,1)S(1)} collective-permute-done((bf16[64,1024]{1,0:T(8,128)(2,1)S(1)}, bf16[64,1024]{1,0:T(8,128)(2,1)S(1)}, u32[]{:S(2)}, u32[]{:S(2)}) %collective-permute-start.44) | collective-permute-done | bytes 131104 | tf_op jit(solution)/shard_map/ppermute | solution.py:596
  281.3 1.6 collective-permute-done.35
  283.5 2.0 collective-permute-start.41
  285.5 32.2 %collective-permute-done.36 = bf16[96,1024]{1,0:T(8,128)(2,1)S(1)} collective-permute-done((bf16[96,1024]{1,0:T(8,128)(2,1)S(1)}, bf16[96,1024]{1,0:T(8,128)(2,1)S(1)}, u32[]{:S(2)}, u32[]{:S(2)}) %collective-permute-start.36) | collective-permute-done | bytes 196640 | tf_op jit(solution)/shard_map/ppermute | solution.py:596
  317.8 3.7 %norm_one_back.1 = (bf16[384,1024]{1,0:T(8,128)(2,1)}, f32[1,1024]{1,0:T(1,128)S(1)}, f32[1,1024]{1,0:T(1,128)S(1)}) custom-call(bf16[384,1024]{1,0:T(8,128)(2,1)S(1)} %copy-done.11, bf16[384,1024]{1,0:T(8,128)(2,1)S(1)} %copy-done.20, f32[1,1024]{1,0:T(1,128)S(1)} %bitcast.24, bf16[384,1024]{1,0:T(8,128)(2,1)S(1)} %copy-done.36, ...), custom_call_target="tpu_custom_call" | custom-call | tf_op jit(solution)/shard_map/norm_one_back/pallas_call | solution.py:121
  322.9 3.7 %collective-permute-done.47 = f32[4224]{0:T(1024)S(1)} collective-permute-done((f32[4224]{0:T(1024)S(1)}, f32[4224]{0:T(1024)S(1)}, u32[]{:S(2)}, u32[]{:S(2)}) %collective-permute-start.47) | collective-permute-done | bytes 16928 | tf_op jit(solution)/shard_map/ppermute | solution.py:596
  327.7 5.9 %collective-permute-done.48 = f32[4224]{0:T(1024)S(1)} collective-permute-done((f32[4224]{0:T(1024)S(1)}, f32[4224]{0:T(1024)S(1)}, u32[]{:S(2)}, u32[]{:S(2)}) %collective-permute-start.48) | collective-permute-done | bytes 16928 | tf_op jit(solution)/shard_map/ppermute | solution.py:596
  333.8 6.2 %collective-permute-done.49 = f32[4224]{0:T(1024)S(1)} collective-permute-done((f32[4224]{0:T(1024)S(1)}, f32[4224]{0:T(1024)S(1)}, u32[]{:S(2)}, u32[]{:S(2)}) %collective-permute-start.49) | collective-permute-done | bytes 16928 | tf_op jit(solution)/shard_map/ppermute | solution.py:596
  341.7 3.1 collective-permute-done.50
  346.8 2.1 copy.34
  348.8 6.7 %slice_convert_fusion = (f32[1024,1024]{1,0:T(8,128)}, f32[1024,1024]{1,0:T(8,128)}) fusion(bf16[2048,1024]{1,0:T(8,128)(2,1)} %all-gather.2.cloned.1.call-done), kind=kLoop, calls=%fused_computation.39 | loop fusion | flops 2097152 | bytes 12582912 | tf_op jit(solution)/shard_map/convert_element_type | solution.py:832
  (288 shorter events, 54.6 us)
Async XLA Ops:
  7.2 28.1 %copy-start.2 = (bf16[3,1024,256]{2,1,0:T(8,128)(2,1)S(1)}, bf16[3,1024,256]{2,1,0:T(8,128)(2,1)}, u32[]{:S(2)}) copy-start(bf16[3,1024,256]{2,1,0:T(8,128)(2,1)} %refs_8_.1) | copy-start | bytes 4718596
  7.2 224.8 %reduce-scatter.2.cloned.1.call-start = ((), (), s32[]{:S(2)}) async-start(), calls=%async_computation.1 | async-start | bytes 4718592 | tf_op jit(solution)/shard_map/reduce_scatter | solution.py:804
  11.3 13.8 %collective-permute-start.1 = (bf16[384,1024]{1,0:T(8,128)(2,1)}, bf16[384,1024]{1,0:T(8,128)(2,1)S(1)}, u32[]{:S(2)}, u32[]{:S(2)}) collective-permute-start(bf16[384,1024]{1,0:T(8,128)(2,1)} %norm_one.1.refs_1_), channel_id=1, source_target_pairs={{0,1},{1,0},{2,3},{3,2},{4,5},{5,4},{6,7},{7,6},{8,9},{9,8},{10,11... | collective-permute-start | bytes 2359304 | tf_op jit(solution)/shard_map/ppermute | solution.py:596
  11.7 21.0 %collective-permute-start = (bf16[384,1024]{1,0:T(8,128)(2,1)}, bf16[384,1024]{1,0:T(8,128)(2,1)}, u32[]{:S(2)}, u32[]{:S(2)}) collective-permute-start(bf16[384,1024]{1,0:T(8,128)(2,1)} %norm_one.1.refs_1_), channel_id=1, source_target_pairs={{0,2},{1,3},{2,0},{3,1},{4,6},{5,7},{6,4},{7,5},{8,10},{9,11},{10,... | collective-permute-start | bytes 2359304 | tf_op jit(solution)/shard_map/ppermute | solution.py:596
  15.1 152.2 %copy-start.49 = (s32[5]{0:T(128)}, s32[5]{0:T(128)S(1)}, u32[]{:S(2)}) copy-start(s32[5]{0:T(128)S(1)} %broadcast_add_fusion.2.refs_0_) | copy-start | bytes 64
  32.8 2.5 collective-permute-start.2
  32.9 22.0 %collective-permute-start.5 = (bf16[384,1024]{1,0:T(8,128)(2,1)}, bf16[384,1024]{1,0:T(8,128)(2,1)}, u32[]{:S(2)}, u32[]{:S(2)}) collective-permute-start(bf16[384,1024]{1,0:T(8,128)(2,1)} %refs_0_.6), channel_id=1, source_target_pairs={{0,2},{1,3},{2,0},{3,1},{4,6},{5,7},{6,4},{7,5},{8,10},{9,11},{10,... | collective-permute-start | bytes 2359304 | tf_op jit(solution)/shard_map/ppermute | solution.py:596
  40.3 127.0 %copy-start = (bf16[1536,256]{1,0:T(8,128)(2,1)}, bf16[1536,256]{1,0:T(8,128)(2,1)S(1)}, u32[]{:S(2)}) copy-start(bf16[1536,256]{1,0:T(8,128)(2,1)S(1)} %get-tuple-element.100.refs_2_.refs_3_.refs_6_) | copy-start | bytes 2359300
  40.4 14.5 %collective-permute-start.4 = (bf16[80,256]{1,0:T(8,128)(2,1)S(1)}, bf16[80,256]{1,0:T(8,128)(2,1)S(1)}, u32[]{:S(2)}, u32[]{:S(2)}) collective-permute-start(bf16[80,256]{1,0:T(8,128)(2,1)S(1)} %convert_element_type.201), channel_id=1, source_target_pairs={{0,8},{4,12},{8,16},{12,20},{16,24},{20,28},{1,9},{5,13},{9,17},{1... | collective-permute-start | bytes 122888 | tf_op jit(solution)/shard_map/ppermute | solution.py:689
  44.1 10.8 %collective-permute-start.3 = (bf16[80,256]{1,0:T(8,128)(2,1)S(1)}, bf16[80,256]{1,0:T(8,128)(2,1)S(1)}, u32[]{:S(2)}, u32[]{:S(2)}) collective-permute-start(bf16[80,256]{1,0:T(8,128)(2,1)S(1)} %convert_element_type.201), channel_id=1, source_target_pairs={{0,4},{4,8},{8,12},{12,16},{16,20},{20,24},{24,28},{1,5},{5,9},{9,... | collective-permute-start | bytes 122888 | tf_op jit(solution)/shard_map/ppermute | solution.py:689
  58.4 23.6 %copy-start.50 = (f32[1024]{0:T(1024)S(1)}, f32[1024]{0:T(1024)}, u32[]{:S(2)}) copy-start(f32[1024]{0:T(1024)} %param.20) | copy-start | bytes 12292
  58.4 23.6 %copy-start.55 = (f32[1024]{0:T(1024)S(1)}, f32[1024]{0:T(1024)}, u32[]{:S(2)}) copy-start(f32[1024]{0:T(1024)} %param.21) | copy-start | bytes 12292
  58.4 3.8 %collective-permute-start.7 = (bf16[384,1024]{1,0:T(8,128)(2,1)S(1)}, bf16[384,1024]{1,0:T(8,128)(2,1)S(1)}, u32[]{:S(2)}, u32[]{:S(2)}) collective-permute-start(bf16[384,1024]{1,0:T(8,128)(2,1)S(1)} %get-tuple-element.110), channel_id=1, source_target_pairs={{0,1},{1,0},{2,3},{3,2},{4,5},{5,4},{6,7},{7,6},{8,9},{9,8},{10,11... | collective-permute-start | bytes 2359304 | tf_op jit(solution)/shard_map/ppermute | solution.py:596
  61.6 24.5 %copy-start.6 = (bf16[1024,1024]{1,0:T(8,128)(2,1)S(1)}, bf16[1024,1024]{1,0:T(8,128)(2,1)}, u32[]{:S(2)}) copy-start(bf16[1024,1024]{1,0:T(8,128)(2,1)} %refs_4_.3) | copy-start | bytes 6291460
  61.6 24.5 %copy-start.7 = (bf16[1024,1024]{1,0:T(8,128)(2,1)S(1)}, bf16[1024,1024]{1,0:T(8,128)(2,1)}, u32[]{:S(2)}) copy-start(bf16[1024,1024]{1,0:T(8,128)(2,1)} %refs_5_.3) | copy-start | bytes 6291460
  61.6 2.4 collective-permute-start.6
  62.5 19.5 %collective-permute-start.8 = (bf16[384,1024]{1,0:T(8,128)(2,1)S(1)}, bf16[384,1024]{1,0:T(8,128)(2,1)S(1)}, u32[]{:S(2)}, u32[]{:S(2)}) collective-permute-start(bf16[384,1024]{1,0:T(8,128)(2,1)S(1)} %add_convert_fusion.3), channel_id=1, source_target_pairs={{0,2},{1,3},{2,0},{3,1},{4,6},{5,7},{6,4},{7,5},{8,10},{9,11},{10,... | collective-permute-start | bytes 2359304 | tf_op jit(solution)/shard_map/ppermute | solution.py:596
  64.0 21.5 %collective-permute-start.10 = (bf16[384,1024]{1,0:T(8,128)(2,1)}, bf16[384,1024]{1,0:T(8,128)(2,1)S(1)}, u32[]{:S(2)}, u32[]{:S(2)}) collective-permute-start(bf16[384,1024]{1,0:T(8,128)(2,1)} %refs_0_.6), channel_id=1, source_target_pairs={{0,1},{1,0},{2,3},{3,2},{4,5},{5,4},{6,7},{7,6},{8,9},{9,8},{10,11... | collective-permute-start | bytes 2359304 | tf_op jit(solution)/shard_map/ppermute | solution.py:596
  83.8 2.3 collective-permute-start.9
  83.8 20.0 %collective-permute-start.12 = (bf16[384,1024]{1,0:T(8,128)(2,1)S(1)}, bf16[384,1024]{1,0:T(8,128)(2,1)S(1)}, u32[]{:S(2)}, u32[]{:S(2)}) collective-permute-start(bf16[384,1024]{1,0:T(8,128)(2,1)S(1)} %get-tuple-element.129.refs_0_), channel_id=1, source_target_pairs={{0,2},{1,3},{2,0},{3,1},{4,6},{5,7},{6,4},{7,5},{8,10},{9,11},{10,... | collective-permute-start | bytes 2359304 | tf_op jit(solution)/shard_map/ppermute | solution.py:596
  85.3 18.4 %collective-permute-start.14 = (bf16[384,1024]{1,0:T(8,128)(2,1)}, bf16[384,1024]{1,0:T(8,128)(2,1)S(1)}, u32[]{:S(2)}, u32[]{:S(2)}) collective-permute-start(bf16[384,1024]{1,0:T(8,128)(2,1)} %collective-permute-done.5.refs_7_.refs_2_), channel_id=1, source_target_pairs={{0,1},{1,0},{2,3},{3,2},{4,5},{5,4},{6,7},{7,6},{8,9},{9,8},{10,11... | collective-permute-start | bytes 2359304 | tf_op jit(solution)/shard_map/ppermute | solution.py:596
  103.8 2.3 collective-permute-start.13
  115.1 2.4 collective-permute-start.17
  115.3 4.9 %collective-permute-start.15 = (bf16[384,1024]{1,0:T(8,128)(2,1)S(1)}, bf16[384,1024]{1,0:T(8,128)(2,1)S(1)}, u32[]{:S(2)}, u32[]{:S(2)}) collective-permute-start(bf16[384,1024]{1,0:T(8,128)(2,1)S(1)} %get-tuple-element.119), channel_id=1, source_target_pairs={{0,1},{1,0},{2,3},{3,2},{4,5},{5,4},{6,7},{7,6},{8,9},{9,8},{10,11... | collective-permute-start | bytes 2359304 | tf_op jit(solution)/shard_map/ppermute | solution.py:596
  115.7 5.8 %collective-permute-start.11 = (bf16[384,1024]{1,0:T(8,128)(2,1)S(1)}, bf16[384,1024]{1,0:T(8,128)(2,1)S(1)}, u32[]{:S(2)}, u32[]{:S(2)}) collective-permute-start(bf16[384,1024]{1,0:T(8,128)(2,1)S(1)} %get-tuple-element.114), channel_id=1, source_target_pairs={{0,1},{1,0},{2,3},{3,2},{4,5},{5,4},{6,7},{7,6},{8,9},{9,8},{10,11... | collective-permute-start | bytes 2359304 | tf_op jit(solution)/shard_map/ppermute | solution.py:596
  115.8 5.7 %collective-permute-start.16 = (bf16[384,1024]{1,0:T(8,128)(2,1)S(1)}, bf16[384,1024]{1,0:T(8,128)(2,1)}, u32[]{:S(2)}, u32[]{:S(2)}) collective-permute-start(bf16[384,1024]{1,0:T(8,128)(2,1)S(1)} %get-tuple-element.121), channel_id=1, source_target_pairs={{0,1},{1,0},{2,3},{3,2},{4,5},{5,4},{6,7},{7,6},{8,9},{9,8},{10,11... | collective-permute-start | bytes 2359304 | tf_op jit(solution)/shard_map/ppermute | solution.py:596
  118.7 19.9 %collective-permute-start.18 = (bf16[384,1024]{1,0:T(8,128)(2,1)}, bf16[384,1024]{1,0:T(8,128)(2,1)}, u32[]{:S(2)}, u32[]{:S(2)}) collective-permute-start(bf16[384,1024]{1,0:T(8,128)(2,1)} %add_convert_fusion.1), channel_id=1, source_target_pairs={{0,2},{1,3},{2,0},{3,1},{4,6},{5,7},{6,4},{7,5},{8,10},{9,11},{10,... | collective-permute-start | bytes 2359304 | tf_op jit(solution)/shard_map/ppermute | solution.py:596
  138.6 210.2 %all-gather.2.cloned.1.call-start = ((), (), s32[]{:S(2)}) async-start(), calls=%async_computation.2 | async-start | bytes 4718592 | tf_op jit(solution)/shard_map/all_gather | solution.py:831
  144.0 2.6 collective-permute-start.20
  144.0 20.2 %collective-permute-start.19 = (bf16[384,1024]{1,0:T(8,128)(2,1)}, bf16[384,1024]{1,0:T(8,128)(2,1)S(1)}, u32[]{:S(2)}, u32[]{:S(2)}) collective-permute-start(bf16[384,1024]{1,0:T(8,128)(2,1)} %get-tuple-element.137.refs_1_), channel_id=1, source_target_pairs={{0,2},{1,3},{2,0},{3,1},{4,6},{5,7},{6,4},{7,5},{8,10},{9,11},{10,... | collective-permute-start | bytes 2359304 | tf_op jit(solution)/shard_map/ppermute | solution.py:596
  164.2 3.1 collective-permute-start.22
  165.8 76.9 %collective-permute-start.21 = (bf16[384,1024]{1,0:T(8,128)(2,1)}, bf16[384,1024]{1,0:T(8,128)(2,1)}, u32[]{:S(2)}, u32[]{:S(2)}) collective-permute-start(bf16[384,1024]{1,0:T(8,128)(2,1)} %add_convert_fusion.2.refs_9_), channel_id=1, source_target_pairs={{0,2},{1,3},{2,0},{3,1},{4,6},{5,7},{6,4},{7,5},{8,10},{9,11},{10,... | collective-permute-start | bytes 2359304 | tf_op jit(solution)/shard_map/ppermute | solution.py:596
  178.9 26.6 %collective-permute-start.24 = (bf16[80,256]{1,0:T(8,128)(2,1)S(1)}, bf16[80,256]{1,0:T(8,128)(2,1)S(1)}, u32[]{:S(2)}, u32[]{:S(2)}) collective-permute-start(bf16[80,256]{1,0:T(8,128)(2,1)S(1)} %convert_element_type.216), channel_id=1, source_target_pairs={{8,0},{12,4},{16,8},{20,12},{24,16},{28,20},{9,1},{13,5},{17,9},{2... | collective-permute-start | bytes 122888 | tf_op jit(solution)/shard_map/ppermute | solution.py:689
  180.2 25.3 %collective-permute-start.23 = (bf16[80,256]{1,0:T(8,128)(2,1)S(1)}, bf16[80,256]{1,0:T(8,128)(2,1)S(1)}, u32[]{:S(2)}, u32[]{:S(2)}) collective-permute-start(bf16[80,256]{1,0:T(8,128)(2,1)S(1)} %convert_element_type.216), channel_id=1, source_target_pairs={{4,0},{8,4},{12,8},{16,12},{20,16},{24,20},{28,24},{5,1},{9,5},{13... | collective-permute-start | bytes 122888 | tf_op jit(solution)/shard_map/ppermute | solution.py:689
  184.5 35.3 %collective-permute-start.31 = (bf16[128,1024]{1,0:T(8,128)(2,1)S(1)}, bf16[128,1024]{1,0:T(8,128)(2,1)S(1)}, u32[]{:S(2)}, u32[]{:S(2)}) collective-permute-start(bf16[128,1024]{1,0:T(8,128)(2,1)S(1)} %broadcast_select_fusion.8.refs_9_), channel_id=1, source_target_pairs={{0,8},{4,12},{8,0},{12,4},{16,24},{20,28},{24,16},{28,20},{1,9},{5... | collective-permute-start | bytes 786440 | tf_op jit(solution)/shard_map/ppermute | solution.py:596
  214.9 17.1 %collective-permute-start.26 = (bf16[384,1024]{1,0:T(8,128)(2,1)}, bf16[384,1024]{1,0:T(8,128)(2,1)}, u32[]{:S(2)}, u32[]{:S(2)}) collective-permute-start(bf16[384,1024]{1,0:T(8,128)(2,1)} %get-tuple-element.155), channel_id=1, source_target_pairs={{0,1},{1,0},{2,3},{3,2},{4,5},{5,4},{6,7},{7,6},{8,9},{9,8},{10,11... | collective-permute-start | bytes 2359304 | tf_op jit(solution)/shard_map/ppermute | solution.py:596
  220.0 11.8 %collective-permute-start.32 = (bf16[64,1024]{1,0:T(8,128)(2,1)S(1)}, bf16[64,1024]{1,0:T(8,128)(2,1)S(1)}, u32[]{:S(2)}, u32[]{:S(2)}) collective-permute-start(bf16[64,1024]{1,0:T(8,128)(2,1)S(1)} %broadcast_select_fusion.17), channel_id=1, source_target_pairs={{0,16},{4,20},{8,24},{12,28},{16,0},{20,4},{24,8},{28,12},{1,17},{... | collective-permute-start | bytes 393224 | tf_op jit(solution)/shard_map/ppermute | solution.py:596
  223.8 14.0 %collective-permute-start.27 = (bf16[192,1024]{1,0:T(8,128)(2,1)S(1)}, bf16[192,1024]{1,0:T(8,128)(2,1)}, u32[]{:S(2)}, u32[]{:S(2)}) collective-permute-start(bf16[192,1024]{1,0:T(8,128)(2,1)S(1)} %get-tuple-element.185), channel_id=1, source_target_pairs={{0,8},{4,12},{8,0},{12,4},{16,24},{20,28},{24,16},{28,20},{1,9},{5... | collective-permute-start | bytes 1179656 | tf_op jit(solution)/shard_map/ppermute | solution.py:596
  224.6 14.4 %collective-permute-start.25 = (bf16[192,1024]{1,0:T(8,128)(2,1)S(1)}, bf16[192,1024]{1,0:T(8,128)(2,1)}, u32[]{:S(2)}, u32[]{:S(2)}) collective-permute-start(bf16[192,1024]{1,0:T(8,128)(2,1)S(1)} %get-tuple-element.186), channel_id=1, source_target_pairs={{0,4},{4,0},{8,12},{12,8},{16,20},{20,16},{24,28},{28,24},{1,5},{5... | collective-permute-start | bytes 1179656 | tf_op jit(solution)/shard_map/ppermute | solution.py:596
  231.9 85.9 %collective-permute-start.28 = (bf16[384,1024]{1,0:T(8,128)(2,1)}, bf16[384,1024]{1,0:T(8,128)(2,1)}, u32[]{:S(2)}, u32[]{:S(2)}) collective-permute-start(bf16[384,1024]{1,0:T(8,128)(2,1)} %get-tuple-element.160), channel_id=1, source_target_pairs={{0,1},{1,0},{2,3},{3,2},{4,5},{5,4},{6,7},{7,6},{8,9},{9,8},{10,11... | collective-permute-start | bytes 2359304 | tf_op jit(solution)/shard_map/ppermute | solution.py:596
  232.1 8.6 %collective-permute-start.33 = (bf16[32,1024]{1,0:T(8,128)(2,1)S(1)}, bf16[32,1024]{1,0:T(8,128)(2,1)S(1)}, u32[]{:S(2)}, u32[]{:S(2)}) collective-permute-start(bf16[32,1024]{1,0:T(8,128)(2,1)S(1)} %broadcast_select_fusion.26), channel_id=1, source_target_pairs={{0,4},{4,0},{8,12},{12,8},{16,20},{20,16},{24,28},{28,24},{1,5},{5... | collective-permute-start | bytes 196616 | tf_op jit(solution)/shard_map/ppermute | solution.py:596
  237.8 80.0 %collective-permute-start.29 = (bf16[384,1024]{1,0:T(8,128)(2,1)}, bf16[384,1024]{1,0:T(8,128)(2,1)}, u32[]{:S(2)}, u32[]{:S(2)}) collective-permute-start(bf16[384,1024]{1,0:T(8,128)(2,1)} %add_convert_fusion), channel_id=1, source_target_pairs={{0,2},{1,3},{2,0},{3,1},{4,6},{5,7},{6,4},{7,5},{8,10},{9,11},{10,... | collective-permute-start | bytes 2359304 | tf_op jit(solution)/shard_map/ppermute | solution.py:596
  240.6 18.6 %collective-permute-start.30 = (bf16[96,1024]{1,0:T(8,128)(2,1)S(1)}, bf16[96,1024]{1,0:T(8,128)(2,1)}, u32[]{:S(2)}, u32[]{:S(2)}) collective-permute-start(bf16[96,1024]{1,0:T(8,128)(2,1)S(1)} %broadcast_select_fusion.14.refs_4_), channel_id=1, source_target_pairs={{0,8},{4,12},{8,0},{12,4},{16,24},{20,28},{24,16},{28,20},{1,9},{5... | collective-permute-start | bytes 589832 | tf_op jit(solution)/shard_map/ppermute | solution.py:596
  240.7 20.4 %collective-permute-start.38 = (bf16[96,1024]{1,0:T(8,128)(2,1)S(1)}, bf16[96,1024]{1,0:T(8,128)(2,1)S(1)}, u32[]{:S(2)}, u32[]{:S(2)}) collective-permute-start(bf16[96,1024]{1,0:T(8,128)(2,1)S(1)} %broadcast_select_fusion.11.refs_5_), channel_id=1, source_target_pairs={{0,16},{4,20},{8,24},{12,28},{16,0},{20,4},{24,8},{28,12},{1,17},{... | collective-permute-start | bytes 589832 | tf_op jit(solution)/shard_map/ppermute | solution.py:596
  246.5 16.3 %collective-permute-start.43 = (bf16[32,1024]{1,0:T(8,128)(2,1)S(1)}, bf16[32,1024]{1,0:T(8,128)(2,1)S(1)}, u32[]{:S(2)}, u32[]{:S(2)}) collective-permute-start(bf16[32,1024]{1,0:T(8,128)(2,1)S(1)} %add_convert_fusion.12), channel_id=1, source_target_pairs={{0,4},{4,0},{8,12},{12,8},{16,20},{20,16},{24,28},{28,24},{1,5},{5... | collective-permute-start | bytes 196616 | tf_op jit(solution)/shard_map/ppermute | solution.py:596
  260.2 57.5 %copy-start.36 = (bf16[384,1024]{1,0:T(8,128)(2,1)S(1)}, bf16[384,1024]{1,0:T(8,128)(2,1)}, u32[]{:S(2)}) copy-start(bf16[384,1024]{1,0:T(8,128)(2,1)} %get-tuple-element.159.refs_3_) | copy-start | bytes 2359300
  260.2 57.5 %copy-start.52 = (f32[1024]{0:T(1024)S(1)}, f32[1024]{0:T(1024)}, u32[]{:S(2)}) copy-start(f32[1024]{0:T(1024)} %param.18) | copy-start | bytes 12292
  260.3 13.4 %collective-permute-start.34 = (bf16[48,1024]{1,0:T(8,128)(2,1)S(1)}, bf16[48,1024]{1,0:T(8,128)(2,1)S(1)}, u32[]{:S(2)}, u32[]{:S(2)}) collective-permute-start(bf16[48,1024]{1,0:T(8,128)(2,1)S(1)} %broadcast_select_fusion.23), channel_id=1, source_target_pairs={{0,16},{4,20},{8,24},{12,28},{16,0},{20,4},{24,8},{28,12},{1,17},{... | collective-permute-start | bytes 294920 | tf_op jit(solution)/shard_map/ppermute | solution.py:596
  261.2 12.6 %collective-permute-start.39 = (bf16[48,1024]{1,0:T(8,128)(2,1)S(1)}, bf16[48,1024]{1,0:T(8,128)(2,1)S(1)}, u32[]{:S(2)}, u32[]{:S(2)}) collective-permute-start(bf16[48,1024]{1,0:T(8,128)(2,1)S(1)} %broadcast_select_fusion.20), channel_id=1, source_target_pairs={{0,4},{4,0},{8,12},{12,8},{16,20},{20,16},{24,28},{28,24},{1,5},{5... | collective-permute-start | bytes 294920 | tf_op jit(solution)/shard_map/ppermute | solution.py:596
  262.8 18.3 %collective-permute-start.44 = (bf16[64,1024]{1,0:T(8,128)(2,1)S(1)}, bf16[64,1024]{1,0:T(8,128)(2,1)S(1)}, u32[]{:S(2)}, u32[]{:S(2)}) collective-permute-start(bf16[64,1024]{1,0:T(8,128)(2,1)S(1)} %pad_maximum_fusion.7), channel_id=1, source_target_pairs={{0,16},{4,20},{8,24},{12,28},{16,0},{20,4},{24,8},{28,12},{1,17},{... | collective-permute-start | bytes 393224 | tf_op jit(solution)/shard_map/ppermute | solution.py:596
  273.7 9.2 %collective-permute-start.35 = (bf16[48,1024]{1,0:T(8,128)(2,1)S(1)}, bf16[48,1024]{1,0:T(8,128)(2,1)S(1)}, u32[]{:S(2)}, u32[]{:S(2)}) collective-permute-start(bf16[48,1024]{1,0:T(8,128)(2,1)S(1)} %add_convert_fusion.11), channel_id=1, source_target_pairs={{0,16},{4,20},{8,24},{12,28},{16,0},{20,4},{24,8},{28,12},{1,17},{... | collective-permute-start | bytes 294920 | tf_op jit(solution)/shard_map/ppermute | solution.py:596
  273.8 9.6 %collective-permute-start.40 = (bf16[48,1024]{1,0:T(8,128)(2,1)S(1)}, bf16[48,1024]{1,0:T(8,128)(2,1)S(1)}, u32[]{:S(2)}, u32[]{:S(2)}) collective-permute-start(bf16[48,1024]{1,0:T(8,128)(2,1)S(1)} %add_convert_fusion.10), channel_id=1, source_target_pairs={{0,4},{4,0},{8,12},{12,8},{16,20},{20,16},{24,28},{28,24},{1,5},{5... | collective-permute-start | bytes 294920 | tf_op jit(solution)/shard_map/ppermute | solution.py:596
  281.2 40.3 %copy-start.65 = (f32[1,1024]{1,0:T(1,128)S(1)}, f32[1,1024]{1,0:T(1,128)}, u32[]{:S(2)}) copy-start(f32[1,1024]{1,0:T(1,128)} %get-tuple-element.174) | copy-start | bytes 12292
  281.2 40.3 %copy-start.64 = (f32[1,1024]{1,0:T(1,128)S(1)}, f32[1,1024]{1,0:T(1,128)}, u32[]{:S(2)}) copy-start(f32[1,1024]{1,0:T(1,128)} %get-tuple-element.175) | copy-start | bytes 12292
  281.2 46.5 %collective-permute-start.45 = (bf16[128,1024]{1,0:T(8,128)(2,1)S(1)}, bf16[128,1024]{1,0:T(8,128)(2,1)S(1)}, u32[]{:S(2)}, u32[]{:S(2)}) collective-permute-start(bf16[128,1024]{1,0:T(8,128)(2,1)S(1)} %pad_maximum_fusion.4), channel_id=1, source_target_pairs={{0,8},{4,12},{8,0},{12,4},{16,24},{20,28},{24,16},{28,20},{1,9},{5... | collective-permute-start | bytes 786440 | tf_op jit(solution)/shard_map/ppermute | solution.py:596
  283.0 34.7 %collective-permute-start.36 = (bf16[96,1024]{1,0:T(8,128)(2,1)S(1)}, bf16[96,1024]{1,0:T(8,128)(2,1)S(1)}, u32[]{:S(2)}, u32[]{:S(2)}) collective-permute-start(bf16[96,1024]{1,0:T(8,128)(2,1)S(1)} %pad_maximum_fusion.5), channel_id=1, source_target_pairs={{0,8},{4,12},{8,0},{12,4},{16,24},{20,28},{24,16},{28,20},{1,9},{5... | collective-permute-start | bytes 589832 | tf_op jit(solution)/shard_map/ppermute | solution.py:596
  283.5 39.3 %collective-permute-start.41 = (bf16[96,1024]{1,0:T(8,128)(2,1)S(1)}, bf16[96,1024]{1,0:T(8,128)(2,1)S(1)}, u32[]{:S(2)}, u32[]{:S(2)}) collective-permute-start(bf16[96,1024]{1,0:T(8,128)(2,1)S(1)} %pad_maximum_fusion.6), channel_id=1, source_target_pairs={{0,16},{4,20},{8,24},{12,28},{16,0},{20,4},{24,8},{28,12},{1,17},{... | collective-permute-start | bytes 589832 | tf_op jit(solution)/shard_map/ppermute | solution.py:596
  321.5 1.3 collective-permute-start.46
  321.6 24.6 %collective-permute-start.37 = (bf16[192,1024]{1,0:T(8,128)(2,1)S(1)}, bf16[192,1024]{1,0:T(8,128)(2,1)S(1)}, u32[]{:S(2)}, u32[]{:S(2)}) collective-permute-start(bf16[192,1024]{1,0:T(8,128)(2,1)S(1)} %pad_maximum_fusion.2), channel_id=1, source_target_pairs={{0,4},{4,0},{8,12},{12,8},{16,20},{20,16},{24,28},{28,24},{1,5},{5... | collective-permute-start | bytes 1179656 | tf_op jit(solution)/shard_map/ppermute | solution.py:596
  322.8 3.8 %collective-permute-start.47 = (f32[4224]{0:T(1024)S(1)}, f32[4224]{0:T(1024)S(1)}, u32[]{:S(2)}, u32[]{:S(2)}) collective-permute-start(f32[4224]{0:T(1024)S(1)} %add.218), channel_id=1, source_target_pairs={{0,2},{1,3},{2,0},{3,1},{4,6},{5,7},{6,4},{7,5},{8,10},{9,11},{10,... | collective-permute-start | bytes 50696 | tf_op jit(solution)/shard_map/ppermute | solution.py:596
  326.6 7.1 %collective-permute-start.48 = (f32[4224]{0:T(1024)S(1)}, f32[4224]{0:T(1024)S(1)}, u32[]{:S(2)}, u32[]{:S(2)}) collective-permute-start(f32[4224]{0:T(1024)S(1)} %add.219), channel_id=1, source_target_pairs={{0,4},{4,0},{8,12},{12,8},{16,20},{20,16},{24,28},{28,24},{1,5},{5... | collective-permute-start | bytes 50696 | tf_op jit(solution)/shard_map/ppermute | solution.py:596
  327.6 18.8 %collective-permute-start.42 = (bf16[192,1024]{1,0:T(8,128)(2,1)S(1)}, bf16[192,1024]{1,0:T(8,128)(2,1)S(1)}, u32[]{:S(2)}, u32[]{:S(2)}) collective-permute-start(bf16[192,1024]{1,0:T(8,128)(2,1)S(1)} %pad_maximum_fusion.3), channel_id=1, source_target_pairs={{0,8},{4,12},{8,0},{12,4},{16,24},{20,28},{24,16},{28,20},{1,9},{5... | collective-permute-start | bytes 1179656 | tf_op jit(solution)/shard_map/ppermute | solution.py:596
  333.7 6.3 %collective-permute-start.49 = (f32[4224]{0:T(1024)S(1)}, f32[4224]{0:T(1024)S(1)}, u32[]{:S(2)}, u32[]{:S(2)}) collective-permute-start(f32[4224]{0:T(1024)S(1)} %add.220), channel_id=1, source_target_pairs={{0,8},{4,12},{8,0},{12,4},{16,24},{20,28},{24,16},{28,20},{1,9},{5... | collective-permute-start | bytes 50696 | tf_op jit(solution)/shard_map/ppermute | solution.py:596
  340.0 4.8 %collective-permute-start.50 = (f32[4224]{0:T(1024)S(1)}, f32[4224]{0:T(1024)S(1)}, u32[]{:S(2)}, u32[]{:S(2)}) collective-permute-start(f32[4224]{0:T(1024)S(1)} %add.221), channel_id=1, source_target_pairs={{0,16},{4,20},{8,24},{12,28},{16,0},{20,4},{24,8},{28,12},{1,17},{... | collective-permute-start | bytes 50696 | tf_op jit(solution)/shard_map/ppermute | solution.py:596
  (55 other events, 261.9 us)
Sparse Core Ops, SparseCore 0:
  138.7 89.8 reduce-scatter.1
  232.1 100.5 all-gather.1
